TPU v7x, 32 devices: a whole 2x2x4 slice. The times are simulated.
32 devices in a mesh: rows: 2 (over y), seq: 16 (over z, x, core).
Axes of the slice: x: 2, y: 2, z: 4, core: 2. Of those that a mesh axis runs over, the one named last changes fastest.
Arguments:
- frames: bfloat16 [2, 2048, 768], P('rows', 'seq'), may hold values from -6 to 6
- segment_ids: int32 [2, 2048], P('rows', 'seq'), may hold values from 0 to 7, never falling along the last dimension, each value on 1 to 1024 neighbouring positions
- qkv_weight: bfloat16 [768, 2304], replicated, may hold values from -0.21875 to 0.21875
- query_bias: float32 [768], replicated, may hold values from -3 to 3
- value_bias: float32 [768], replicated, may hold values from -0.3125 to 0.3125
- out_weight: bfloat16 [768, 768], replicated, may hold values from -3.5 to 3.5
- out_bias: float32 [768], replicated, may hold values from -3 to 3
- norm1_gain: float32 [768], replicated, may hold values from 0.5 to 1.5
- norm1_shift: float32 [768], replicated, may hold values from -3 to 3
- up_weight: bfloat16 [768, 3072], replicated, may hold values from -0.21875 to 0.21875
- up_bias: float32 [3072], replicated, may hold values from -3 to 3
- down_weight: bfloat16 [3072, 768], replicated, may hold values from -0.109375 to 0.109375
- down_bias: float32 [768], replicated, may hold values from -3 to 3
- norm2_gain: float32 [768], replicated, may hold values from 0.5 to 1.5
- norm2_shift: float32 [768], replicated, may hold values from -3 to 3
- cotangent: bfloat16 [2, 2048, 768], P('rows', 'seq'), may hold values from -6 to 6
Outputs:
- layer_out: bfloat16 [2, 2048, 768], P('rows', 'seq')
- input_grad: float32 [2, 2048, 768], P('rows', 'seq')
- qkv_gradient: float32 [768, 2304], P(('rows', 'seq'))
- querybias_gradient: float32 [768], P(('rows', 'seq'))
- valuebias_gradient: float32 [768], P(('rows', 'seq'))
- out_gradient: float32 [768, 768], P(('rows', 'seq'))
- outbias_gradient: float32 [768], P(('rows', 'seq'))
- gain1_gradient: float32 [768], P(('rows', 'seq'))
- shift1_gradient: float32 [768], P(('rows', 'seq'))
- up_gradient: float32 [768, 3072], P(('rows', 'seq'))
- upbias_gradient: float32 [3072], P(('rows', 'seq'))
- down_gradient: float32 [3072, 768], P(('rows', 'seq'))
- downbias_gradient: float32 [768], P(('rows', 'seq'))
- gain2_gradient: float32 [768], P(('rows', 'seq'))
- shift2_gradient: float32 [768], P(('rows', 'seq'))
Inputs may be any that keep to these rules, and one draw needn't show every extreme that they name: `segment_ids`: along each row the ids never fall; each clip has 1 to 1024 frames and one has exactly 1024.
All inputs are finite; a program needn't handle non-finite values.
Results may differ from a plain program's by a relative error of at most 0.02.
Values may be sent and summed in bfloat16 or wider, within the bound.
A program may use at most 192 MiB of HBM per device.

v0:
```python
import math

import jax
import jax.numpy as jnp
from jax import lax
from jax.sharding import PartitionSpec as P

HEADS = 12
HEAD_DIM = 64


norm_eps = 1e-05
mask_fill = -1e30


def shortened(shard):

    def short(part):
        return part.astype(jnp.bfloat16) if part.dtype == jnp.float32 else part

    return jax.tree.map(short, shard)


def passed_along(value, axis, steps):
    count = lax.axis_size(axis)
    pairs = [(source, (source + steps) % count) for source in range(count)]
    return lax.ppermute(value, axis, pairs)


def layer_norm(resid, gain, shift):
    centred = resid - jnp.mean(resid, axis=-1, keepdims=True)
    inv_std = lax.rsqrt(jnp.mean(centred * centred, axis=-1, keepdims=True) + norm_eps)
    normed = centred * inv_std
    return (normed * gain + shift, normed, inv_std)


def norm_back(upstream, normed, inv_std, gain):
    scaled = upstream * gain
    first_mean = jnp.mean(scaled, axis=-1, keepdims=True)
    second_mean = jnp.mean(scaled * normed, axis=-1, keepdims=True)
    grad_in = inv_std * (scaled - first_mean - normed * second_mean)
    return (grad_in, jnp.sum(upstream * normed, axis=0), jnp.sum(upstream, axis=0))


def gelu_slope(pre_act):
    normal_cdf = 0.5 * (1.0 + lax.erf(pre_act * 0.5**0.5))
    normal_pdf = jnp.exp(-0.5 * pre_act * pre_act) * (2.0 * math.pi) ** (-0.5)
    return normal_cdf + pre_act * normal_pdf


def head_groups(head_count):
    return [(0, head_count, 1)]


def pass_keys(blocks):
    return jax.tree.map(
        lambda part, own: part.astype(own.dtype), passed_along(shortened(blocks), "seq", 1), blocks
    )


def pass_again(blocks):
    return jax.tree.map(
        lambda part, own: part.astype(own.dtype), passed_along(shortened(blocks), "seq", 1), blocks
    )


def pass_grads(blocks):
    return (
        passed_along(blocks[0].astype(jnp.bfloat16), "seq", 1).astype(jnp.float32),
        passed_along(blocks[1].astype(jnp.bfloat16), "seq", 1).astype(jnp.float32),
    )


def block_scores(query_part, key_part, query_ids, key_ids):
    scores = jnp.einsum(
        "qhe,khe->hqk", query_part, key_part, preferred_element_type=jnp.float32
    ) * HEAD_DIM ** (-0.5)
    return jnp.where((query_ids[:, None] == key_ids[None, :])[None], scores, mask_fill)


def attend_block(carried, query_part, key_part, value_part, query_ids, key_ids):
    run_max, run_total, run_acc = carried
    scores = block_scores(query_part, key_part, query_ids, key_ids)
    new_max = jnp.maximum(run_max, jnp.max(scores, axis=-1))
    weights = jnp.exp(scores - new_max[:, :, None])
    factor = jnp.exp(run_max - new_max)
    new_total = run_total * factor + jnp.sum(weights, axis=-1)
    update = jnp.einsum(
        "hqk,khe->qhe", weights.astype(jnp.bfloat16), value_part, preferred_element_type=jnp.float32
    )
    return (new_max, new_total, run_acc * factor.T[:, :, None] + update)


def grad_block(
    carried,
    query_part,
    key_part,
    value_part,
    query_ids,
    key_ids,
    context_part,
    log_part,
    delta_part,
):
    query_acc, key_acc, value_acc = carried
    scores = block_scores(query_part, key_part, query_ids, key_ids)
    probs = jnp.exp(scores - log_part[:, :, None])
    prob_grad = jnp.einsum(
        "qhe,khe->hqk", context_part, value_part, preferred_element_type=jnp.float32
    )
    score_grad = (probs * (prob_grad - delta_part[:, :, None])).astype(jnp.bfloat16)
    scale = HEAD_DIM ** (-0.5)
    query_acc = query_acc + scale * jnp.einsum(
        "hqk,khe->qhe", score_grad, key_part, preferred_element_type=jnp.float32
    )
    key_acc = key_acc + scale * jnp.einsum(
        "hqk,qhe->khe", score_grad, query_part, preferred_element_type=jnp.float32
    )
    value_acc = value_acc + jnp.einsum(
        "hqk,qhe->khe", probs.astype(jnp.bfloat16), context_part, preferred_element_type=jnp.float32
    )
    return (query_acc, key_acc, value_acc)


def forward_cycle(
    query_heads, key_heads, value_heads, local_ids, every_id, cycle_place, cycle_size
):
    frame_count, head_count, head_width = query_heads.shape
    grouping = head_groups(head_count)
    states = []
    blocks = []
    for head_first, head_last, direction in grouping:
        head_span = head_last - head_first
        initial = (
            jnp.full((head_span, frame_count), mask_fill, jnp.float32),
            jnp.zeros((head_span, frame_count), jnp.float32),
            jnp.zeros((frame_count, head_span, head_width), jnp.float32),
        )
        states.append(
            attend_block(initial, query_heads, key_heads, value_heads, local_ids, local_ids)
        )
        blocks.append((key_heads, value_heads))

    def forward_cycle_turn(turn_index, cycle_carry):
        old_states, old_blocks = cycle_carry
        new_states = []
        new_blocks = []
        for group_info, part_state, part_block in zip(grouping, old_states, old_blocks):
            head_first, head_last, direction = group_info
            part_block = pass_keys(part_block)
            source_index = (cycle_place - direction * turn_index) % cycle_size
            key_ids = lax.dynamic_slice_in_dim(every_id, source_index * frame_count, frame_count)
            new_states.append(
                attend_block(
                    part_state, query_heads, part_block[0], part_block[1], local_ids, key_ids
                )
            )
            new_blocks.append(part_block)
        return (new_states, new_blocks)

    states, blocks = lax.fori_loop(1, cycle_size, forward_cycle_turn, (states, blocks))
    maxima = jnp.concatenate([part_state[0] for part_state in states], axis=0)
    totals = jnp.concatenate([part_state[1] for part_state in states], axis=0)
    sums_all = jnp.concatenate([part_state[2] for part_state in states], axis=1)
    attended = sums_all / totals.T[:, :, None]
    return (attended, maxima + jnp.log(totals))


def backward_cycle(
    query_heads,
    key_heads,
    value_heads,
    local_ids,
    every_id,
    context_heads,
    log_total,
    row_delta,
    cycle_place,
    cycle_size,
):
    frame_count, head_count, head_width = query_heads.shape
    grouping = head_groups(head_count)
    initial = []
    for head_first, head_last, direction in grouping:
        zero_part = jnp.zeros((frame_count, head_last - head_first, head_width), jnp.float32)
        initial.append((zero_part, (key_heads, value_heads), (zero_part, zero_part)))

    def backward_cycle_turn(turn_index, cycle_carry):
        new_carry = []
        for group_info, part_carry in zip(grouping, cycle_carry):
            head_first, head_last, direction = group_info
            query_acc, part_block, part_grads = part_carry
            source_index = (cycle_place - direction * turn_index) % cycle_size
            key_ids = lax.dynamic_slice_in_dim(every_id, source_index * frame_count, frame_count)
            query_acc, key_acc, value_acc = grad_block(
                (query_acc, part_grads[0], part_grads[1]),
                query_heads,
                part_block[0],
                part_block[1],
                local_ids,
                key_ids,
                context_heads,
                log_total,
                row_delta,
            )
            part_grads = pass_grads((key_acc, value_acc))
            part_block = pass_again(part_block)
            new_carry.append((query_acc, part_block, part_grads))
        return new_carry

    final = lax.fori_loop(0, cycle_size, backward_cycle_turn, initial)
    query_grad = jnp.concatenate([part_carry[0] for part_carry in final], axis=1)
    key_grad = jnp.concatenate([part_carry[2][0] for part_carry in final], axis=1)
    value_grad = jnp.concatenate([part_carry[2][1] for part_carry in final], axis=1)
    return (query_grad, key_grad, value_grad)


def shards(
    frames,
    segment_ids,
    qkv_weight,
    query_bias,
    value_bias,
    out_weight,
    out_bias,
    norm1_gain,
    norm1_shift,
    up_weight,
    up_bias,
    down_weight,
    down_bias,
    norm2_gain,
    norm2_shift,
    cotangent,
):
    inputs = frames[0]
    local_ids = segment_ids[0]
    frame_count, model_width = inputs.shape
    cycle_size = lax.axis_size("seq")
    cycle_place = lax.axis_index("seq")
    every_id = lax.all_gather(segment_ids, "seq", axis=1, tiled=True)[0]
    head_shape = (frame_count, HEADS, HEAD_DIM)
    projected = jnp.dot(inputs, qkv_weight, preferred_element_type=jnp.float32)
    query_heads = (projected[:, :model_width] + query_bias).astype(jnp.bfloat16).reshape(head_shape)
    key_heads = projected[:, model_width : 2 * model_width].astype(jnp.bfloat16).reshape(head_shape)
    value_heads = (
        (projected[:, 2 * model_width :] + value_bias).astype(jnp.bfloat16).reshape(head_shape)
    )
    attended, log_total = forward_cycle(
        query_heads, key_heads, value_heads, local_ids, every_id, cycle_place, cycle_size
    )
    context = attended.astype(jnp.bfloat16).reshape(frame_count, model_width)
    resid_one = (
        inputs.astype(jnp.float32)
        + jnp.dot(context, out_weight, preferred_element_type=jnp.float32)
        + out_bias
    )
    hidden, normed_one, inverse_one = layer_norm(resid_one, norm1_gain, norm1_shift)
    hidden_low = hidden.astype(jnp.bfloat16)
    pre_act = jnp.dot(hidden_low, up_weight, preferred_element_type=jnp.float32) + up_bias
    act_low = jax.nn.gelu(pre_act, approximate=False).astype(jnp.bfloat16)
    resid_two = (
        hidden + jnp.dot(act_low, down_weight, preferred_element_type=jnp.float32) + down_bias
    )
    output, normed_two, inverse_two = layer_norm(resid_two, norm2_gain, norm2_shift)
    upstream = cotangent[0].astype(jnp.float32)
    second_grad, gain_two_grad, shift_two_grad = norm_back(
        upstream, normed_two, inverse_two, norm2_gain
    )
    second_low = second_grad.astype(jnp.bfloat16)
    down_grad = jnp.einsum("tf,td->fd", act_low, second_low, preferred_element_type=jnp.float32)
    pre_grad = jnp.einsum(
        "td,fd->tf", second_low, down_weight, preferred_element_type=jnp.float32
    ) * gelu_slope(pre_act)
    pre_low = pre_grad.astype(jnp.bfloat16)
    up_grad = jnp.einsum("td,tf->df", hidden_low, pre_low, preferred_element_type=jnp.float32)
    hidden_grad = second_grad + jnp.einsum(
        "tf,df->td", pre_low, up_weight, preferred_element_type=jnp.float32
    )
    first_grad, gain_one_grad, shift_one_grad = norm_back(
        hidden_grad, normed_one, inverse_one, norm1_gain
    )
    first_low = first_grad.astype(jnp.bfloat16)
    out_grad = jnp.einsum("td,te->de", context, first_low, preferred_element_type=jnp.float32)
    context_grad = (
        jnp.einsum("te,de->td", first_low, out_weight, preferred_element_type=jnp.float32)
        .astype(jnp.bfloat16)
        .reshape(head_shape)
    )
    row_delta = jnp.einsum("qhe,qhe->hq", context_grad.astype(jnp.float32), attended)
    query_grad, key_grad, value_grad = backward_cycle(
        query_heads,
        key_heads,
        value_heads,
        local_ids,
        every_id,
        context_grad,
        log_total,
        row_delta,
        cycle_place,
        cycle_size,
    )
    query_low = query_grad.astype(jnp.bfloat16).reshape(frame_count, model_width)
    key_low = key_grad.astype(jnp.bfloat16).reshape(frame_count, model_width)
    value_low = value_grad.astype(jnp.bfloat16).reshape(frame_count, model_width)
    proj_grad = jnp.concatenate([query_low, key_low, value_low], axis=1)
    qkv_grad = jnp.einsum("td,te->de", inputs, proj_grad, preferred_element_type=jnp.float32)
    input_grad = (
        jnp.einsum("te,de->td", proj_grad, qkv_weight, preferred_element_type=jnp.float32)
        + first_grad
    )
    summed = (
        lax.psum_scatter(qkv_grad, ("rows", "seq"), scatter_dimension=0, tiled=True),
        lax.psum_scatter(
            jnp.sum(query_low.astype(jnp.float32), axis=0),
            ("rows", "seq"),
            scatter_dimension=0,
            tiled=True,
        ),
        lax.psum_scatter(
            jnp.sum(value_low.astype(jnp.float32), axis=0),
            ("rows", "seq"),
            scatter_dimension=0,
            tiled=True,
        ),
        lax.psum_scatter(out_grad, ("rows", "seq"), scatter_dimension=0, tiled=True),
        lax.psum_scatter(
            jnp.sum(first_grad, axis=0), ("rows", "seq"), scatter_dimension=0, tiled=True
        ),
        lax.psum_scatter(gain_one_grad, ("rows", "seq"), scatter_dimension=0, tiled=True),
        lax.psum_scatter(shift_one_grad, ("rows", "seq"), scatter_dimension=0, tiled=True),
        lax.psum_scatter(up_grad, ("rows", "seq"), scatter_dimension=0, tiled=True),
        lax.psum_scatter(
            jnp.sum(pre_grad, axis=0), ("rows", "seq"), scatter_dimension=0, tiled=True
        ),
        lax.psum_scatter(down_grad, ("rows", "seq"), scatter_dimension=0, tiled=True),
        lax.psum_scatter(
            jnp.sum(second_grad, axis=0), ("rows", "seq"), scatter_dimension=0, tiled=True
        ),
        lax.psum_scatter(gain_two_grad, ("rows", "seq"), scatter_dimension=0, tiled=True),
        lax.psum_scatter(shift_two_grad, ("rows", "seq"), scatter_dimension=0, tiled=True),
    )
    return (
        output.astype(jnp.bfloat16)[None],
        input_grad[None],
        summed[0],
        summed[1],
        summed[2],
        summed[3],
        summed[4],
        summed[5],
        summed[6],
        summed[7],
        summed[8],
        summed[9],
        summed[10],
        summed[11],
        summed[12],
    )


def solution(mesh):
    in_specs = (
        P("rows", "seq", None),
        P("rows", "seq"),
        P(),
        P(),
        P(),
        P(),
        P(),
        P(),
        P(),
        P(),
        P(),
        P(),
        P(),
        P(),
        P(),
        P("rows", "seq", None),
    )
    out_specs = (
        P("rows", "seq", None),
        P("rows", "seq", None),
        P(("rows", "seq"), None),
        P(("rows", "seq")),
        P(("rows", "seq")),
        P(("rows", "seq"), None),
        P(("rows", "seq")),
        P(("rows", "seq")),
        P(("rows", "seq")),
        P(("rows", "seq"), None),
        P(("rows", "seq")),
        P(("rows", "seq"), None),
        P(("rows", "seq")),
        P(("rows", "seq")),
        P(("rows", "seq")),
    )
    return jax.shard_map(shards, mesh=mesh, in_specs=in_specs, out_specs=out_specs, check_vma=False)
```

profile of v0, /device:TPU:0, one launch (start us, length us, event | category | flops | bytes accessed | tf_op | source)
XLA Modules:
  0.0 1068.5 jit_solution(424066450494285101)
XLA Ops:
  15.8 23.7 %all_gather.3 = s32[1,2048]{1,0:T(1,128)} all-gather(s32[1,128]{1,0:T(1,128)S(1)} %copy-done.24), channel_id=1, replica_groups=mesh['rows'=2,'seq'=16] {'seq'}, dimensions={1}, use_global_device_ids=true | all-gather | bytes 8704 | tf_op jit(solution)/shard_map/all_gather | solution.py:241
  47.6 2.2 fusion.35
  49.8 222.5 %while.47 = (s32[]{:T(128)}, f32[12,128]{1,0:T(8,128)S(1)}, f32[12,128]{1,0:T(8,128)S(1)}, f32[128,12,64]{0,2,1:T(8,128)}, bf16[128,12,64]{0,2,1:T(8,128)(2,1)},...) while((s32[]{:T(128)}, f32[12,128]{1,0:T(8,128)S(1)}, ...), condition=%wide.region_5.6_spmd, body=%wide.region_2.5_spmd.sunk | while | flops 51925520 | bytes 9374152 | solution.py:161
  51.6 6.3 collective-permute-done
  66.1 6.6 collective-permute-done
  81.0 6.6 collective-permute-done
  95.8 6.6 collective-permute-done
  110.6 6.6 collective-permute-done
  125.5 6.6 collective-permute-done
  140.3 6.6 collective-permute-done
  155.1 6.6 collective-permute-done
  170.0 6.5 collective-permute-done
  184.8 6.5 collective-permute-done
  199.7 6.5 collective-permute-done
  214.5 6.5 collective-permute-done
  229.3 6.5 collective-permute-done
  244.2 6.5 collective-permute-done
  259.0 6.5 collective-permute-done
  275.6 5.9 fusion.22
  284.9 2.3 fusion.83
  287.3 2.3 multiply_reduce_fusion
  293.3 2.6 convolution_convert_fusion
  300.1 342.9 %while.48 = (s32[]{:T(128)}, f32[128,12,64]{0,2,1:T(8,128)}, bf16[128,12,64]{0,2,1:T(8,128)(2,1)}, bf16[128,12,64]{0,2,1:T(8,128)(2,1)}, f32[128,12,64]{0,2,1:T(...) while((s32[]{:T(128)}, f32[128,12,64]{0,2,1:T(8,128)}, ...), condition=%wide.region_15.16_spmd.clone, body=%wide.region_14.15_spmd.clone.sunk | while | flops 128401424 | bytes 18356908 | solution.py:211
  310.5 2.2 fusion.156
  312.7 5.0 collective-permute-done.4
  332.0 2.3 fusion.156
  334.3 4.9 collective-permute-done.4
  353.4 2.3 fusion.156
  355.7 4.9 collective-permute-done.4
  374.8 2.3 fusion.156
  377.1 4.9 collective-permute-done.4
  396.5 2.3 fusion.156
  398.8 4.9 collective-permute-done.4
  417.9 2.3 fusion.156
  420.2 4.9 collective-permute-done.4
  439.3 2.3 fusion.156
  441.6 4.9 collective-permute-done.4
  460.7 2.3 fusion.156
  463.0 4.9 collective-permute-done.4
  482.1 2.3 fusion.156
  484.4 4.9 collective-permute-done.4
  503.5 2.3 fusion.156
  505.8 4.9 collective-permute-done.4
  524.9 2.3 fusion.156
  527.2 4.9 collective-permute-done.4
  546.3 2.3 fusion.156
  548.6 4.9 collective-permute-done.4
  567.7 2.3 fusion.156
  570.0 4.9 collective-permute-done.4
  589.1 2.3 fusion.156
  591.5 4.9 collective-permute-done.4
  610.5 2.3 fusion.156
  612.9 4.9 collective-permute-done.4
  632.0 2.3 fusion.156
  634.3 4.9 collective-permute-done.4
  647.8 4.0 convolution_bitcast_fusion.2
  651.8 8.0 copy.68
  660.5 6.4 fusion.54
  667.0 6.4 fusion.67
  675.1 39.4 %all-reduce.9 = (f32[768]{0:T(1024)}, f32[768]{0:T(1024)}, f32[768]{0:T(1024)}, f32[768]{0:T(1024)}, f32[768]{0:T(1024)}, /*index=5*/f32[3072]{0:T(1024)}, f32[768]{0:T(1024)}, f32[768]{0:T(1024)S(1)}, f32[768]{0:T(1024)S(1)}) all-reduce(f32[768]{0:T(1024)} %reduce_sum.192, ...), channel_id=3, replica_groups=mesh['rows'=2,'seq'=16] {'rows','seq'}, use_global_device_ids=true, to_apply=%region_18.19.clone | all-reduce | flops 9216 | bytes 73728
  724.5 3.3 fusion.37
  727.8 51.0 %reduce-scatter.13.cloned.1.call-done = f32[24,2304]{1,0:T(8,128)} async-done(((f32[768,2304]{1,0:T(8,128)}), f32[24,2304]{1,0:T(8,128)}) %reduce-scatter.13.cloned.1.call-update) | async-done | bytes 221200
  778.8 141.1 %reduce-scatter.9.cloned.1.call-done = f32[24,3072]{1,0:T(8,128)} async-done(((f32[768,3072]{1,0:T(8,128)}), f32[24,3072]{1,0:T(8,128)}) %reduce-scatter.9.cloned.1.call-update) | async-done | bytes 294928 | tf_op jit(solution)/shard_map/reduce_scatter | solution.py:332
  919.9 142.1 %reduce-scatter.11.cloned.1.call-done = f32[96,768]{1,0:T(8,128)} async-done(((f32[3072,768]{1,0:T(8,128)}), f32[96,768]{1,0:T(8,128)}) %reduce-scatter.11.cloned.1.call-update) | async-done | bytes 294928 | tf_op jit(solution)/shard_map/reduce_scatter | solution.py:336
  (840 shorter events, 398.8 us)
Async XLA Ops:
  7.2 720.6 %reduce-scatter.7.cloned.1.call-start = ((), (), s32[]{:S(2)}) async-start(), calls=%async_computation.4 | async-start | bytes 2433024 | tf_op jit(solution)/shard_map/reduce_scatter | solution.py:326
  50.0 11.0 %collective-permute-start.1 = (bf16[128,12,64]{0,2,1:T(8,128)(2,1)}, bf16[128,12,64]{0,2,1:T(8,128)(2,1)}, u32[]{:S(2)}, u32[]{:S(2)}) collective-permute-start(bf16[128,12,64]{0,2,1:T(8,128)(2,1)} %get-tuple-element.950), channel_id=1, source_target_pairs={{0,1},{1,2},{2,3},{3,4},{4,5},{5,6},{6,7},{7,8},{8,9},{9,10},{10,1... | collective-permute-start | bytes 589832 | tf_op jit(solution)/shard_map/while/body/eval_jaxpr/ppermute | solution.py:27
  64.6 11.3 %collective-permute-start.1 = (bf16[128,12,64]{0,2,1:T(8,128)(2,1)}, bf16[128,12,64]{0,2,1:T(8,128)(2,1)}, u32[]{:S(2)}, u32[]{:S(2)}) collective-permute-start(bf16[128,12,64]{0,2,1:T(8,128)(2,1)} %get-tuple-element.950), channel_id=1, source_target_pairs={{0,1},{1,2},{2,3},{3,4},{4,5},{5,6},{6,7},{7,8},{8,9},{9,10},{10,1... | collective-permute-start | bytes 589832 | tf_op jit(solution)/shard_map/while/body/eval_jaxpr/ppermute | solution.py:27
  79.4 11.3 %collective-permute-start.1 = (bf16[128,12,64]{0,2,1:T(8,128)(2,1)}, bf16[128,12,64]{0,2,1:T(8,128)(2,1)}, u32[]{:S(2)}, u32[]{:S(2)}) collective-permute-start(bf16[128,12,64]{0,2,1:T(8,128)(2,1)} %get-tuple-element.950), channel_id=1, source_target_pairs={{0,1},{1,2},{2,3},{3,4},{4,5},{5,6},{6,7},{7,8},{8,9},{9,10},{10,1... | collective-permute-start | bytes 589832 | tf_op jit(solution)/shard_map/while/body/eval_jaxpr/ppermute | solution.py:27
  94.3 11.3 %collective-permute-start.1 = (bf16[128,12,64]{0,2,1:T(8,128)(2,1)}, bf16[128,12,64]{0,2,1:T(8,128)(2,1)}, u32[]{:S(2)}, u32[]{:S(2)}) collective-permute-start(bf16[128,12,64]{0,2,1:T(8,128)(2,1)} %get-tuple-element.950), channel_id=1, source_target_pairs={{0,1},{1,2},{2,3},{3,4},{4,5},{5,6},{6,7},{7,8},{8,9},{9,10},{10,1... | collective-permute-start | bytes 589832 | tf_op jit(solution)/shard_map/while/body/eval_jaxpr/ppermute | solution.py:27
  109.1 11.3 %collective-permute-start.1 = (bf16[128,12,64]{0,2,1:T(8,128)(2,1)}, bf16[128,12,64]{0,2,1:T(8,128)(2,1)}, u32[]{:S(2)}, u32[]{:S(2)}) collective-permute-start(bf16[128,12,64]{0,2,1:T(8,128)(2,1)} %get-tuple-element.950), channel_id=1, source_target_pairs={{0,1},{1,2},{2,3},{3,4},{4,5},{5,6},{6,7},{7,8},{8,9},{9,10},{10,1... | collective-permute-start | bytes 589832 | tf_op jit(solution)/shard_map/while/body/eval_jaxpr/ppermute | solution.py:27
  123.9 11.3 %collective-permute-start.1 = (bf16[128,12,64]{0,2,1:T(8,128)(2,1)}, bf16[128,12,64]{0,2,1:T(8,128)(2,1)}, u32[]{:S(2)}, u32[]{:S(2)}) collective-permute-start(bf16[128,12,64]{0,2,1:T(8,128)(2,1)} %get-tuple-element.950), channel_id=1, source_target_pairs={{0,1},{1,2},{2,3},{3,4},{4,5},{5,6},{6,7},{7,8},{8,9},{9,10},{10,1... | collective-permute-start | bytes 589832 | tf_op jit(solution)/shard_map/while/body/eval_jaxpr/ppermute | solution.py:27
  138.8 11.3 %collective-permute-start.1 = (bf16[128,12,64]{0,2,1:T(8,128)(2,1)}, bf16[128,12,64]{0,2,1:T(8,128)(2,1)}, u32[]{:S(2)}, u32[]{:S(2)}) collective-permute-start(bf16[128,12,64]{0,2,1:T(8,128)(2,1)} %get-tuple-element.950), channel_id=1, source_target_pairs={{0,1},{1,2},{2,3},{3,4},{4,5},{5,6},{6,7},{7,8},{8,9},{9,10},{10,1... | collective-permute-start | bytes 589832 | tf_op jit(solution)/shard_map/while/body/eval_jaxpr/ppermute | solution.py:27
  153.6 11.3 %collective-permute-start.1 = (bf16[128,12,64]{0,2,1:T(8,128)(2,1)}, bf16[128,12,64]{0,2,1:T(8,128)(2,1)}, u32[]{:S(2)}, u32[]{:S(2)}) collective-permute-start(bf16[128,12,64]{0,2,1:T(8,128)(2,1)} %get-tuple-element.950), channel_id=1, source_target_pairs={{0,1},{1,2},{2,3},{3,4},{4,5},{5,6},{6,7},{7,8},{8,9},{9,10},{10,1... | collective-permute-start | bytes 589832 | tf_op jit(solution)/shard_map/while/body/eval_jaxpr/ppermute | solution.py:27
  168.4 11.3 %collective-permute-start.1 = (bf16[128,12,64]{0,2,1:T(8,128)(2,1)}, bf16[128,12,64]{0,2,1:T(8,128)(2,1)}, u32[]{:S(2)}, u32[]{:S(2)}) collective-permute-start(bf16[128,12,64]{0,2,1:T(8,128)(2,1)} %get-tuple-element.950), channel_id=1, source_target_pairs={{0,1},{1,2},{2,3},{3,4},{4,5},{5,6},{6,7},{7,8},{8,9},{9,10},{10,1... | collective-permute-start | bytes 589832 | tf_op jit(solution)/shard_map/while/body/eval_jaxpr/ppermute | solution.py:27
  183.3 11.3 %collective-permute-start.1 = (bf16[128,12,64]{0,2,1:T(8,128)(2,1)}, bf16[128,12,64]{0,2,1:T(8,128)(2,1)}, u32[]{:S(2)}, u32[]{:S(2)}) collective-permute-start(bf16[128,12,64]{0,2,1:T(8,128)(2,1)} %get-tuple-element.950), channel_id=1, source_target_pairs={{0,1},{1,2},{2,3},{3,4},{4,5},{5,6},{6,7},{7,8},{8,9},{9,10},{10,1... | collective-permute-start | bytes 589832 | tf_op jit(solution)/shard_map/while/body/eval_jaxpr/ppermute | solution.py:27
  198.1 11.3 %collective-permute-start.1 = (bf16[128,12,64]{0,2,1:T(8,128)(2,1)}, bf16[128,12,64]{0,2,1:T(8,128)(2,1)}, u32[]{:S(2)}, u32[]{:S(2)}) collective-permute-start(bf16[128,12,64]{0,2,1:T(8,128)(2,1)} %get-tuple-element.950), channel_id=1, source_target_pairs={{0,1},{1,2},{2,3},{3,4},{4,5},{5,6},{6,7},{7,8},{8,9},{9,10},{10,1... | collective-permute-start | bytes 589832 | tf_op jit(solution)/shard_map/while/body/eval_jaxpr/ppermute | solution.py:27
  212.9 11.3 %collective-permute-start.1 = (bf16[128,12,64]{0,2,1:T(8,128)(2,1)}, bf16[128,12,64]{0,2,1:T(8,128)(2,1)}, u32[]{:S(2)}, u32[]{:S(2)}) collective-permute-start(bf16[128,12,64]{0,2,1:T(8,128)(2,1)} %get-tuple-element.950), channel_id=1, source_target_pairs={{0,1},{1,2},{2,3},{3,4},{4,5},{5,6},{6,7},{7,8},{8,9},{9,10},{10,1... | collective-permute-start | bytes 589832 | tf_op jit(solution)/shard_map/while/body/eval_jaxpr/ppermute | solution.py:27
  227.8 11.3 %collective-permute-start.1 = (bf16[128,12,64]{0,2,1:T(8,128)(2,1)}, bf16[128,12,64]{0,2,1:T(8,128)(2,1)}, u32[]{:S(2)}, u32[]{:S(2)}) collective-permute-start(bf16[128,12,64]{0,2,1:T(8,128)(2,1)} %get-tuple-element.950), channel_id=1, source_target_pairs={{0,1},{1,2},{2,3},{3,4},{4,5},{5,6},{6,7},{7,8},{8,9},{9,10},{10,1... | collective-permute-start | bytes 589832 | tf_op jit(solution)/shard_map/while/body/eval_jaxpr/ppermute | solution.py:27
  242.6 11.3 %collective-permute-start.1 = (bf16[128,12,64]{0,2,1:T(8,128)(2,1)}, bf16[128,12,64]{0,2,1:T(8,128)(2,1)}, u32[]{:S(2)}, u32[]{:S(2)}) collective-permute-start(bf16[128,12,64]{0,2,1:T(8,128)(2,1)} %get-tuple-element.950), channel_id=1, source_target_pairs={{0,1},{1,2},{2,3},{3,4},{4,5},{5,6},{6,7},{7,8},{8,9},{9,10},{10,1... | collective-permute-start | bytes 589832 | tf_op jit(solution)/shard_map/while/body/eval_jaxpr/ppermute | solution.py:27
  257.4 11.3 %collective-permute-start.1 = (bf16[128,12,64]{0,2,1:T(8,128)(2,1)}, bf16[128,12,64]{0,2,1:T(8,128)(2,1)}, u32[]{:S(2)}, u32[]{:S(2)}) collective-permute-start(bf16[128,12,64]{0,2,1:T(8,128)(2,1)} %get-tuple-element.950), channel_id=1, source_target_pairs={{0,1},{1,2},{2,3},{3,4},{4,5},{5,6},{6,7},{7,8},{8,9},{9,10},{10,1... | collective-permute-start | bytes 589832 | tf_op jit(solution)/shard_map/while/body/eval_jaxpr/ppermute | solution.py:27
  293.1 485.7 %reduce-scatter.13.cloned.1.call-start = ((), (), s32[]{:S(2)}) async-start(), calls=%async_computation.7 | async-start | bytes 7299072
  301.7 19.8 %collective-permute-start.2 = (bf16[128,12,64]{0,2,1:T(8,128)(2,1)}, bf16[128,12,64]{0,2,1:T(8,128)(2,1)}, u32[]{:S(2)}, u32[]{:S(2)}) collective-permute-start(bf16[128,12,64]{0,2,1:T(8,128)(2,1)} %copy.97), channel_id=1, source_target_pairs={{0,1},{1,2},{2,3},{3,4},{4,5},{5,6},{6,7},{7,8},{8,9},{9,10},{10,1... | collective-permute-start | bytes 589832 | tf_op jit(solution)/shard_map/while/body/eval_jaxpr/ppermute | solution.py:27
  303.3 18.2 %collective-permute-start.3 = (bf16[128,12,64]{0,2,1:T(8,128)(2,1)}, bf16[128,12,64]{0,2,1:T(8,128)(2,1)}, u32[]{:S(2)}, u32[]{:S(2)}) collective-permute-start(bf16[128,12,64]{0,2,1:T(8,128)(2,1)} %copy.98), channel_id=1, source_target_pairs={{0,1},{1,2},{2,3},{3,4},{4,5},{5,6},{6,7},{7,8},{8,9},{9,10},{10,1... | collective-permute-start | bytes 589832 | tf_op jit(solution)/shard_map/while/body/eval_jaxpr/ppermute | solution.py:27
  323.2 19.8 %collective-permute-start.2 = (bf16[128,12,64]{0,2,1:T(8,128)(2,1)}, bf16[128,12,64]{0,2,1:T(8,128)(2,1)}, u32[]{:S(2)}, u32[]{:S(2)}) collective-permute-start(bf16[128,12,64]{0,2,1:T(8,128)(2,1)} %copy.97), channel_id=1, source_target_pairs={{0,1},{1,2},{2,3},{3,4},{4,5},{5,6},{6,7},{7,8},{8,9},{9,10},{10,1... | collective-permute-start | bytes 589832 | tf_op jit(solution)/shard_map/while/body/eval_jaxpr/ppermute | solution.py:27
  324.8 18.2 %collective-permute-start.3 = (bf16[128,12,64]{0,2,1:T(8,128)(2,1)}, bf16[128,12,64]{0,2,1:T(8,128)(2,1)}, u32[]{:S(2)}, u32[]{:S(2)}) collective-permute-start(bf16[128,12,64]{0,2,1:T(8,128)(2,1)} %copy.98), channel_id=1, source_target_pairs={{0,1},{1,2},{2,3},{3,4},{4,5},{5,6},{6,7},{7,8},{8,9},{9,10},{10,1... | collective-permute-start | bytes 589832 | tf_op jit(solution)/shard_map/while/body/eval_jaxpr/ppermute | solution.py:27
  332.0 9.3 collective-permute-start.5
  344.6 19.8 %collective-permute-start.2 = (bf16[128,12,64]{0,2,1:T(8,128)(2,1)}, bf16[128,12,64]{0,2,1:T(8,128)(2,1)}, u32[]{:S(2)}, u32[]{:S(2)}) collective-permute-start(bf16[128,12,64]{0,2,1:T(8,128)(2,1)} %copy.97), channel_id=1, source_target_pairs={{0,1},{1,2},{2,3},{3,4},{4,5},{5,6},{6,7},{7,8},{8,9},{9,10},{10,1... | collective-permute-start | bytes 589832 | tf_op jit(solution)/shard_map/while/body/eval_jaxpr/ppermute | solution.py:27
  346.2 18.2 %collective-permute-start.3 = (bf16[128,12,64]{0,2,1:T(8,128)(2,1)}, bf16[128,12,64]{0,2,1:T(8,128)(2,1)}, u32[]{:S(2)}, u32[]{:S(2)}) collective-permute-start(bf16[128,12,64]{0,2,1:T(8,128)(2,1)} %copy.98), channel_id=1, source_target_pairs={{0,1},{1,2},{2,3},{3,4},{4,5},{5,6},{6,7},{7,8},{8,9},{9,10},{10,1... | collective-permute-start | bytes 589832 | tf_op jit(solution)/shard_map/while/body/eval_jaxpr/ppermute | solution.py:27
  353.4 9.3 collective-permute-start.5
  366.0 20.0 %collective-permute-start.2 = (bf16[128,12,64]{0,2,1:T(8,128)(2,1)}, bf16[128,12,64]{0,2,1:T(8,128)(2,1)}, u32[]{:S(2)}, u32[]{:S(2)}) collective-permute-start(bf16[128,12,64]{0,2,1:T(8,128)(2,1)} %copy.97), channel_id=1, source_target_pairs={{0,1},{1,2},{2,3},{3,4},{4,5},{5,6},{6,7},{7,8},{8,9},{9,10},{10,1... | collective-permute-start | bytes 589832 | tf_op jit(solution)/shard_map/while/body/eval_jaxpr/ppermute | solution.py:27
  367.7 18.4 %collective-permute-start.3 = (bf16[128,12,64]{0,2,1:T(8,128)(2,1)}, bf16[128,12,64]{0,2,1:T(8,128)(2,1)}, u32[]{:S(2)}, u32[]{:S(2)}) collective-permute-start(bf16[128,12,64]{0,2,1:T(8,128)(2,1)} %copy.98), channel_id=1, source_target_pairs={{0,1},{1,2},{2,3},{3,4},{4,5},{5,6},{6,7},{7,8},{8,9},{9,10},{10,1... | collective-permute-start | bytes 589832 | tf_op jit(solution)/shard_map/while/body/eval_jaxpr/ppermute | solution.py:27
  374.8 9.6 collective-permute-start.5
  387.7 19.8 %collective-permute-start.2 = (bf16[128,12,64]{0,2,1:T(8,128)(2,1)}, bf16[128,12,64]{0,2,1:T(8,128)(2,1)}, u32[]{:S(2)}, u32[]{:S(2)}) collective-permute-start(bf16[128,12,64]{0,2,1:T(8,128)(2,1)} %copy.97), channel_id=1, source_target_pairs={{0,1},{1,2},{2,3},{3,4},{4,5},{5,6},{6,7},{7,8},{8,9},{9,10},{10,1... | collective-permute-start | bytes 589832 | tf_op jit(solution)/shard_map/while/body/eval_jaxpr/ppermute | solution.py:27
  389.3 18.2 %collective-permute-start.3 = (bf16[128,12,64]{0,2,1:T(8,128)(2,1)}, bf16[128,12,64]{0,2,1:T(8,128)(2,1)}, u32[]{:S(2)}, u32[]{:S(2)}) collective-permute-start(bf16[128,12,64]{0,2,1:T(8,128)(2,1)} %copy.98), channel_id=1, source_target_pairs={{0,1},{1,2},{2,3},{3,4},{4,5},{5,6},{6,7},{7,8},{8,9},{9,10},{10,1... | collective-permute-start | bytes 589832 | tf_op jit(solution)/shard_map/while/body/eval_jaxpr/ppermute | solution.py:27
  409.1 19.8 %collective-permute-start.2 = (bf16[128,12,64]{0,2,1:T(8,128)(2,1)}, bf16[128,12,64]{0,2,1:T(8,128)(2,1)}, u32[]{:S(2)}, u32[]{:S(2)}) collective-permute-start(bf16[128,12,64]{0,2,1:T(8,128)(2,1)} %copy.97), channel_id=1, source_target_pairs={{0,1},{1,2},{2,3},{3,4},{4,5},{5,6},{6,7},{7,8},{8,9},{9,10},{10,1... | collective-permute-start | bytes 589832 | tf_op jit(solution)/shard_map/while/body/eval_jaxpr/ppermute | solution.py:27
  410.7 18.2 %collective-permute-start.3 = (bf16[128,12,64]{0,2,1:T(8,128)(2,1)}, bf16[128,12,64]{0,2,1:T(8,128)(2,1)}, u32[]{:S(2)}, u32[]{:S(2)}) collective-permute-start(bf16[128,12,64]{0,2,1:T(8,128)(2,1)} %copy.98), channel_id=1, source_target_pairs={{0,1},{1,2},{2,3},{3,4},{4,5},{5,6},{6,7},{7,8},{8,9},{9,10},{10,1... | collective-permute-start | bytes 589832 | tf_op jit(solution)/shard_map/while/body/eval_jaxpr/ppermute | solution.py:27
  430.5 19.8 %collective-permute-start.2 = (bf16[128,12,64]{0,2,1:T(8,128)(2,1)}, bf16[128,12,64]{0,2,1:T(8,128)(2,1)}, u32[]{:S(2)}, u32[]{:S(2)}) collective-permute-start(bf16[128,12,64]{0,2,1:T(8,128)(2,1)} %copy.97), channel_id=1, source_target_pairs={{0,1},{1,2},{2,3},{3,4},{4,5},{5,6},{6,7},{7,8},{8,9},{9,10},{10,1... | collective-permute-start | bytes 589832 | tf_op jit(solution)/shard_map/while/body/eval_jaxpr/ppermute | solution.py:27
  432.1 18.2 %collective-permute-start.3 = (bf16[128,12,64]{0,2,1:T(8,128)(2,1)}, bf16[128,12,64]{0,2,1:T(8,128)(2,1)}, u32[]{:S(2)}, u32[]{:S(2)}) collective-permute-start(bf16[128,12,64]{0,2,1:T(8,128)(2,1)} %copy.98), channel_id=1, source_target_pairs={{0,1},{1,2},{2,3},{3,4},{4,5},{5,6},{6,7},{7,8},{8,9},{9,10},{10,1... | collective-permute-start | bytes 589832 | tf_op jit(solution)/shard_map/while/body/eval_jaxpr/ppermute | solution.py:27
  439.3 9.3 collective-permute-start.5
  451.9 19.8 %collective-permute-start.2 = (bf16[128,12,64]{0,2,1:T(8,128)(2,1)}, bf16[128,12,64]{0,2,1:T(8,128)(2,1)}, u32[]{:S(2)}, u32[]{:S(2)}) collective-permute-start(bf16[128,12,64]{0,2,1:T(8,128)(2,1)} %copy.97), channel_id=1, source_target_pairs={{0,1},{1,2},{2,3},{3,4},{4,5},{5,6},{6,7},{7,8},{8,9},{9,10},{10,1... | collective-permute-start | bytes 589832 | tf_op jit(solution)/shard_map/while/body/eval_jaxpr/ppermute | solution.py:27
  453.5 18.2 %collective-permute-start.3 = (bf16[128,12,64]{0,2,1:T(8,128)(2,1)}, bf16[128,12,64]{0,2,1:T(8,128)(2,1)}, u32[]{:S(2)}, u32[]{:S(2)}) collective-permute-start(bf16[128,12,64]{0,2,1:T(8,128)(2,1)} %copy.98), channel_id=1, source_target_pairs={{0,1},{1,2},{2,3},{3,4},{4,5},{5,6},{6,7},{7,8},{8,9},{9,10},{10,1... | collective-permute-start | bytes 589832 | tf_op jit(solution)/shard_map/while/body/eval_jaxpr/ppermute | solution.py:27
  460.7 9.3 collective-permute-start.5
  473.3 19.8 %collective-permute-start.2 = (bf16[128,12,64]{0,2,1:T(8,128)(2,1)}, bf16[128,12,64]{0,2,1:T(8,128)(2,1)}, u32[]{:S(2)}, u32[]{:S(2)}) collective-permute-start(bf16[128,12,64]{0,2,1:T(8,128)(2,1)} %copy.97), channel_id=1, source_target_pairs={{0,1},{1,2},{2,3},{3,4},{4,5},{5,6},{6,7},{7,8},{8,9},{9,10},{10,1... | collective-permute-start | bytes 589832 | tf_op jit(solution)/shard_map/while/body/eval_jaxpr/ppermute | solution.py:27
  474.9 18.2 %collective-permute-start.3 = (bf16[128,12,64]{0,2,1:T(8,128)(2,1)}, bf16[128,12,64]{0,2,1:T(8,128)(2,1)}, u32[]{:S(2)}, u32[]{:S(2)}) collective-permute-start(bf16[128,12,64]{0,2,1:T(8,128)(2,1)} %copy.98), channel_id=1, source_target_pairs={{0,1},{1,2},{2,3},{3,4},{4,5},{5,6},{6,7},{7,8},{8,9},{9,10},{10,1... | collective-permute-start | bytes 589832 | tf_op jit(solution)/shard_map/while/body/eval_jaxpr/ppermute | solution.py:27
  482.1 9.3 collective-permute-start.5
  494.7 19.8 %collective-permute-start.2 = (bf16[128,12,64]{0,2,1:T(8,128)(2,1)}, bf16[128,12,64]{0,2,1:T(8,128)(2,1)}, u32[]{:S(2)}, u32[]{:S(2)}) collective-permute-start(bf16[128,12,64]{0,2,1:T(8,128)(2,1)} %copy.97), channel_id=1, source_target_pairs={{0,1},{1,2},{2,3},{3,4},{4,5},{5,6},{6,7},{7,8},{8,9},{9,10},{10,1... | collective-permute-start | bytes 589832 | tf_op jit(solution)/shard_map/while/body/eval_jaxpr/ppermute | solution.py:27
  496.3 18.2 %collective-permute-start.3 = (bf16[128,12,64]{0,2,1:T(8,128)(2,1)}, bf16[128,12,64]{0,2,1:T(8,128)(2,1)}, u32[]{:S(2)}, u32[]{:S(2)}) collective-permute-start(bf16[128,12,64]{0,2,1:T(8,128)(2,1)} %copy.98), channel_id=1, source_target_pairs={{0,1},{1,2},{2,3},{3,4},{4,5},{5,6},{6,7},{7,8},{8,9},{9,10},{10,1... | collective-permute-start | bytes 589832 | tf_op jit(solution)/shard_map/while/body/eval_jaxpr/ppermute | solution.py:27
  503.5 9.3 collective-permute-start.5
  516.1 19.8 %collective-permute-start.2 = (bf16[128,12,64]{0,2,1:T(8,128)(2,1)}, bf16[128,12,64]{0,2,1:T(8,128)(2,1)}, u32[]{:S(2)}, u32[]{:S(2)}) collective-permute-start(bf16[128,12,64]{0,2,1:T(8,128)(2,1)} %copy.97), channel_id=1, source_target_pairs={{0,1},{1,2},{2,3},{3,4},{4,5},{5,6},{6,7},{7,8},{8,9},{9,10},{10,1... | collective-permute-start | bytes 589832 | tf_op jit(solution)/shard_map/while/body/eval_jaxpr/ppermute | solution.py:27
  517.8 18.2 %collective-permute-start.3 = (bf16[128,12,64]{0,2,1:T(8,128)(2,1)}, bf16[128,12,64]{0,2,1:T(8,128)(2,1)}, u32[]{:S(2)}, u32[]{:S(2)}) collective-permute-start(bf16[128,12,64]{0,2,1:T(8,128)(2,1)} %copy.98), channel_id=1, source_target_pairs={{0,1},{1,2},{2,3},{3,4},{4,5},{5,6},{6,7},{7,8},{8,9},{9,10},{10,1... | collective-permute-start | bytes 589832 | tf_op jit(solution)/shard_map/while/body/eval_jaxpr/ppermute | solution.py:27
  524.9 9.3 collective-permute-start.5
  537.5 19.8 %collective-permute-start.2 = (bf16[128,12,64]{0,2,1:T(8,128)(2,1)}, bf16[128,12,64]{0,2,1:T(8,128)(2,1)}, u32[]{:S(2)}, u32[]{:S(2)}) collective-permute-start(bf16[128,12,64]{0,2,1:T(8,128)(2,1)} %copy.97), channel_id=1, source_target_pairs={{0,1},{1,2},{2,3},{3,4},{4,5},{5,6},{6,7},{7,8},{8,9},{9,10},{10,1... | collective-permute-start | bytes 589832 | tf_op jit(solution)/shard_map/while/body/eval_jaxpr/ppermute | solution.py:27
  539.2 18.2 %collective-permute-start.3 = (bf16[128,12,64]{0,2,1:T(8,128)(2,1)}, bf16[128,12,64]{0,2,1:T(8,128)(2,1)}, u32[]{:S(2)}, u32[]{:S(2)}) collective-permute-start(bf16[128,12,64]{0,2,1:T(8,128)(2,1)} %copy.98), channel_id=1, source_target_pairs={{0,1},{1,2},{2,3},{3,4},{4,5},{5,6},{6,7},{7,8},{8,9},{9,10},{10,1... | collective-permute-start | bytes 589832 | tf_op jit(solution)/shard_map/while/body/eval_jaxpr/ppermute | solution.py:27
  546.3 9.3 collective-permute-start.5
  559.0 19.8 %collective-permute-start.2 = (bf16[128,12,64]{0,2,1:T(8,128)(2,1)}, bf16[128,12,64]{0,2,1:T(8,128)(2,1)}, u32[]{:S(2)}, u32[]{:S(2)}) collective-permute-start(bf16[128,12,64]{0,2,1:T(8,128)(2,1)} %copy.97), channel_id=1, source_target_pairs={{0,1},{1,2},{2,3},{3,4},{4,5},{5,6},{6,7},{7,8},{8,9},{9,10},{10,1... | collective-permute-start | bytes 589832 | tf_op jit(solution)/shard_map/while/body/eval_jaxpr/ppermute | solution.py:27
  560.6 18.2 %collective-permute-start.3 = (bf16[128,12,64]{0,2,1:T(8,128)(2,1)}, bf16[128,12,64]{0,2,1:T(8,128)(2,1)}, u32[]{:S(2)}, u32[]{:S(2)}) collective-permute-start(bf16[128,12,64]{0,2,1:T(8,128)(2,1)} %copy.98), channel_id=1, source_target_pairs={{0,1},{1,2},{2,3},{3,4},{4,5},{5,6},{6,7},{7,8},{8,9},{9,10},{10,1... | collective-permute-start | bytes 589832 | tf_op jit(solution)/shard_map/while/body/eval_jaxpr/ppermute | solution.py:27
  567.7 9.3 collective-permute-start.5
  580.4 19.8 %collective-permute-start.2 = (bf16[128,12,64]{0,2,1:T(8,128)(2,1)}, bf16[128,12,64]{0,2,1:T(8,128)(2,1)}, u32[]{:S(2)}, u32[]{:S(2)}) collective-permute-start(bf16[128,12,64]{0,2,1:T(8,128)(2,1)} %copy.97), channel_id=1, source_target_pairs={{0,1},{1,2},{2,3},{3,4},{4,5},{5,6},{6,7},{7,8},{8,9},{9,10},{10,1... | collective-permute-start | bytes 589832 | tf_op jit(solution)/shard_map/while/body/eval_jaxpr/ppermute | solution.py:27
  582.0 18.2 %collective-permute-start.3 = (bf16[128,12,64]{0,2,1:T(8,128)(2,1)}, bf16[128,12,64]{0,2,1:T(8,128)(2,1)}, u32[]{:S(2)}, u32[]{:S(2)}) collective-permute-start(bf16[128,12,64]{0,2,1:T(8,128)(2,1)} %copy.98), channel_id=1, source_target_pairs={{0,1},{1,2},{2,3},{3,4},{4,5},{5,6},{6,7},{7,8},{8,9},{9,10},{10,1... | collective-permute-start | bytes 589832 | tf_op jit(solution)/shard_map/while/body/eval_jaxpr/ppermute | solution.py:27
  589.1 9.3 collective-permute-start.5
  601.8 19.8 %collective-permute-start.2 = (bf16[128,12,64]{0,2,1:T(8,128)(2,1)}, bf16[128,12,64]{0,2,1:T(8,128)(2,1)}, u32[]{:S(2)}, u32[]{:S(2)}) collective-permute-start(bf16[128,12,64]{0,2,1:T(8,128)(2,1)} %copy.97), channel_id=1, source_target_pairs={{0,1},{1,2},{2,3},{3,4},{4,5},{5,6},{6,7},{7,8},{8,9},{9,10},{10,1... | collective-permute-start | bytes 589832 | tf_op jit(solution)/shard_map/while/body/eval_jaxpr/ppermute | solution.py:27
  603.4 18.2 %collective-permute-start.3 = (bf16[128,12,64]{0,2,1:T(8,128)(2,1)}, bf16[128,12,64]{0,2,1:T(8,128)(2,1)}, u32[]{:S(2)}, u32[]{:S(2)}) collective-permute-start(bf16[128,12,64]{0,2,1:T(8,128)(2,1)} %copy.98), channel_id=1, source_target_pairs={{0,1},{1,2},{2,3},{3,4},{4,5},{5,6},{6,7},{7,8},{8,9},{9,10},{10,1... | collective-permute-start | bytes 589832 | tf_op jit(solution)/shard_map/while/body/eval_jaxpr/ppermute | solution.py:27
  610.5 9.3 collective-permute-start.5
  623.2 19.8 %collective-permute-start.2 = (bf16[128,12,64]{0,2,1:T(8,128)(2,1)}, bf16[128,12,64]{0,2,1:T(8,128)(2,1)}, u32[]{:S(2)}, u32[]{:S(2)}) collective-permute-start(bf16[128,12,64]{0,2,1:T(8,128)(2,1)} %copy.97), channel_id=1, source_target_pairs={{0,1},{1,2},{2,3},{3,4},{4,5},{5,6},{6,7},{7,8},{8,9},{9,10},{10,1... | collective-permute-start | bytes 589832 | tf_op jit(solution)/shard_map/while/body/eval_jaxpr/ppermute | solution.py:27
  624.8 18.2 %collective-permute-start.3 = (bf16[128,12,64]{0,2,1:T(8,128)(2,1)}, bf16[128,12,64]{0,2,1:T(8,128)(2,1)}, u32[]{:S(2)}, u32[]{:S(2)}) collective-permute-start(bf16[128,12,64]{0,2,1:T(8,128)(2,1)} %copy.98), channel_id=1, source_target_pairs={{0,1},{1,2},{2,3},{3,4},{4,5},{5,6},{6,7},{7,8},{8,9},{9,10},{10,1... | collective-permute-start | bytes 589832 | tf_op jit(solution)/shard_map/while/body/eval_jaxpr/ppermute | solution.py:27
  631.9 9.3 collective-permute-start.5
  659.8 260.1 %reduce-scatter.9.cloned.1.call-start = ((), (), s32[]{:S(2)}) async-start(), calls=%async_computation.5 | async-start | bytes 9732096 | tf_op jit(solution)/shard_map/reduce_scatter | solution.py:332
  666.9 395.0 %reduce-scatter.11.cloned.1.call-start = ((), (), s32[]{:S(2)}) async-start(), calls=%async_computation.6 | async-start | bytes 9732096 | tf_op jit(solution)/shard_map/reduce_scatter | solution.py:336
  (190 other events, 983.5 us)
Sparse Core Ops, SparseCore 0:
  293.2 99.6 reduce-scatter.6
  659.9 118.7 reduce-scatter.12
  785.3 134.5 reduce-scatter.8
  927.2 134.7 reduce-scatter.10
where the time goes:
time: 1070 us
  waiting for transfers between devices  517 us (48%)
  matrix products  195 us (18%)
  local copies, waits for them, and re-layouts  183 us (17%)
  other arithmetic  93.2 us (9%)
  blocking collectives  63.1 us (6%)
  between operations  14.1 us (1%)
    ppermute x94, waiting for transfers between devices, passed_along(): return lax.ppermute(value, axis, pairs)  183 us
    reduce_scatter x1, waiting for transfers between devices, shards(): lax.psum_scatter(down_grad, ('rows', 'seq'), scatter_dimension=0, tiled=T...  142 us
    reduce_scatter x1, waiting for transfers between devices, shards(): lax.psum_scatter(up_grad, ('rows', 'seq'), scatter_dimension=0, tiled=True)  141 us
    while x329, local copies, waits for them, and re-layouts  124 us
    unnamed x5, waiting for transfers between devices  51 us
    dot_general x32, matrix products, block_scores(): jnp.einsum('qhe,khe->hqk', query_part, key_part, preferred_element_type=j...  44.9 us
    unnamed x1, blocking collectives  39.4 us
    dot_general x16, matrix products, grad_block(): jnp.einsum('hqk,khe->qhe', score_grad, key_part, preferred_element_type=j...  36.9 us
  transfers between devices with their start and end apart: 98, of which 50 were waited for; matrix products, arithmetic and copies ran while one was open for 34% of the time, Pallas kernels for 0%

commit v1 on v0

--- a/solution.py
+++ b/solution.py
@@ -1,8 +1,11 @@
+import functools
 import math
 
 import jax
 import jax.numpy as jnp
 from jax import lax
+from jax.experimental import pallas as pl
+from jax.experimental.pallas import tpu as pltpu
 from jax.sharding import PartitionSpec as P
 
 HEADS = 12
@@ -359,7 +362,954 @@
     )
 
 
+HALF = HEAD_DIM
+PAIRS = HEADS // 2
+CONTRACT_LAST = (((1,), (1,)), ((), ()))
+CONTRACT_INNER = (((1,), (0,)), ((), ()))
+CONTRACT_FIRST = (((0,), (0,)), ((), ()))
+IN_VMEM = pl.BlockSpec(memory_space=pltpu.VMEM)
+IN_PLACE = pl.BlockSpec(memory_space=pl.ANY)
+MESH_ID = pl.DeviceIdType.MESH
+VMEM_BYTES = 58 << 20
+BLOCKS = 16
+PLANES = 4
+
+
+def product(left, right, dims):
+    return lax.dot_general(left, right, dims, preferred_element_type=jnp.float32)
+
+
+def where_am_i():
+    row = lax.axis_index("rows")
+    place = lax.axis_index("seq")
+    return row, place // 4, place // 2 % 2, place % 2
+
+
+def meet(partners, count):
+    barrier = pltpu.get_barrier_semaphore()
+    for present, target in partners:
+
+        def signal(target=target):
+            pl.semaphore_signal(barrier, inc=1, device_id=target, device_id_type=MESH_ID)
+
+        if present is None:
+            signal()
+        else:
+            pl.when(present)(signal)
+    pl.semaphore_wait(barrier, count)
+
+
+class RowGather:
+    UP, DOWN, ACROSS, BESIDE = range(4)
+
+    def __init__(self, parts, send_sem, recv_sem):
+        self.parts = parts
+        self.send_sem = send_sem
+        self.recv_sem = recv_sem
+        self.row, self.z, self.x, self.c = where_am_i()
+        self.sent = []
+
+    def device(self, z, x, c):
+        return (self.row, z * 4 + x * 2 + c)
+
+    def targets(self):
+        return (
+            self.device(self.z + 1, self.x, self.c),
+            self.device(self.z - 1, self.x, self.c),
+            self.device(self.z, 1 - self.x, self.c),
+            self.device(self.z, self.x, 1 - self.c),
+        )
+
+    def meet(self):
+        up, down, across, beside = self.targets()
+        has_up = self.z < PLANES - 1
+        has_down = self.z > 0
+        meet(
+            [(has_up, up), (has_down, down), (None, across), (None, beside)],
+            2 + has_up.astype(jnp.int32) + has_down.astype(jnp.int32),
+        )
+
+    def copy(self, part, block, way):
+        ref, first, rows = self.parts[part]
+        piece = ref.at[block, pl.ds(first, rows)]
+        return pltpu.make_async_remote_copy(
+            src_ref=piece,
+            dst_ref=piece,
+            send_sem=self.send_sem.at[part, way, block],
+            recv_sem=self.recv_sem.at[part, block],
+            device_id=self.targets()[way],
+            device_id_type=MESH_ID,
+        )
+
+    def send(self, part, block, way, present=None):
+        self.sent.append((part, block, way, present))
+        if present is None:
+            self.copy(part, block, way).start()
+        else:
+            pl.when(present)(lambda: self.copy(part, block, way).start())
+
+    def arrived(self, part, block):
+        self.copy(part, block, self.BESIDE).wait_recv()
+
+    def finish(self):
+        for part, block, way, present in self.sent:
+            if present is None:
+                self.copy(part, block, way).wait_send()
+            else:
+                pl.when(present)(
+                    lambda part=part, block=block, way=way: self.copy(part, block, way).wait_send()
+                )
+
+    def relay(self, part, z, x, ways, present):
+        block = z * 4 + x * 2 + self.c
+
+        def wait():
+            self.arrived(part, block)
+
+        if present is None:
+            wait()
+        else:
+            pl.when(present)(wait)
+        for way, also in ways:
+            both = present if also is None else (also if present is None else present & also)
+            self.send(part, block, way, both)
+
+    def own(self, across_first, line_parts):
+        z, x, c = self.z, self.x, self.c
+        mine = z * 4 + x * 2 + c
+        has_up, has_down = z < PLANES - 1, z > 0
+        for part in across_first:
+            self.send(part, mine, self.ACROSS)
+        for part in list(line_parts) + list(across_first):
+            self.send(part, mine, self.UP, has_up)
+            self.send(part, mine, self.DOWN, has_down)
+        for part in line_parts:
+            self.send(part, mine, self.ACROSS)
+        for part in list(across_first) + list(line_parts):
+            self.send(part, mine, self.BESIDE)
+
+    def first_round(self, across_first, line_parts):
+        z, x = self.z, self.x
+        has_up, has_down = z < PLANES - 1, z > 0
+        up, down, across, beside = (
+            (self.UP, has_up),
+            (self.DOWN, has_down),
+            (self.ACROSS, None),
+            (self.BESIDE, None),
+        )
+        for part in across_first:
+            self.relay(part, z, 1 - x, [up, down, beside], None)
+        for part in line_parts:
+            self.relay(part, z - 1, x, [up, across, beside], has_down)
+            self.relay(part, z + 1, x, [down, across, beside], has_up)
+        for part in across_first:
+            self.relay(part, z - 1, x, [up, beside], has_down)
+            self.relay(part, z + 1, x, [down, beside], has_up)
+        for part in line_parts:
+            self.relay(part, z, 1 - x, [beside], None)
+
+    def plane_done(self, z, parts, present=None):
+        def wait():
+            for x in range(2):
+                for part in parts:
+                    self.arrived(part, z * 4 + x * 2 + 1 - self.c)
+
+        if present is None:
+            wait()
+        else:
+            pl.when(present)(wait)
+
+    def second_round(self, across_first, line_parts):
+        z, x = self.z, self.x
+        has_up, has_down = z < PLANES - 1, z > 0
+        up, down, beside = (self.UP, has_up), (self.DOWN, has_down), (self.BESIDE, None)
+        for part in across_first:
+            self.relay(part, z - 1, 1 - x, [up, beside], has_down)
+            self.relay(part, z + 1, 1 - x, [down, beside], has_up)
+        for part in line_parts:
+            self.relay(part, z - 1, 1 - x, [beside], has_down)
+            self.relay(part, z + 1, 1 - x, [beside], has_up)
+
+    def far_plane(self):
+        return (self.z + 2) % PLANES
+
+    def third_round(self, across_first, line_parts):
+        far, x = self.far_plane(), self.x
+        across, beside = (self.ACROSS, None), (self.BESIDE, None)
+        for part in line_parts:
+            self.relay(part, far, x, [across, beside], None)
+        for part in across_first:
+            self.relay(part, far, x, [beside], None)
+            self.relay(part, far, 1 - x, [beside], None)
+        for part in line_parts:
+            self.relay(part, far, 1 - x, [beside], None)
+
+
+def attend_kernel(
+    frames_ref,
+    ids_row_ref,
+    ids_column_ref,
+    weight_ref,
+    query_bias_ref,
+    value_bias_ref,
+    attended_ref,
+    log_ref,
+    every_ids_ref,
+    projected_hbm,
+    block_ref,
+    projected_ref,
+    bias_ref,
+    send_sem,
+    recv_sem,
+    store_sem,
+):
+    frame_count, width = frames_ref.shape
+    padded = block_ref.shape[1]
+    first_rows = 80
+    link = RowGather(
+        [(block_ref, 0, first_rows), (block_ref, first_rows, padded - first_rows)],
+        send_sem,
+        recv_sem,
+    )
+    z, x, c = link.z, link.x, link.c
+    mine = z * 4 + x * 2 + c
+    has_up, has_down = z < PLANES - 1, z > 0
+    line, crossing = (0,), (1,)
+    link.meet()
+    block_ref[mine, pl.ds(0, frame_count), :] = frames_ref[...]
+    block_ref[mine, pl.ds(frame_count, padded - frame_count), pl.ds(0, frame_count)] = (
+        jnp.broadcast_to(ids_row_ref[...], (padded - frame_count, frame_count))
+        .astype(jnp.float32)
+        .astype(jnp.bfloat16)
+    )
+    link.own(crossing, line)
+
+    def store(plane):
+        return pltpu.make_async_copy(
+            projected_ref.at[pl.ds(plane * 4, 4)],
+            projected_hbm.at[pl.ds(plane * 4, 4)],
+            store_sem.at[plane],
+        )
+
+    def project(plane):
+        rows = jnp.concatenate(
+            [block_ref[plane * 4 + i, pl.ds(0, frame_count), :] for i in range(4)], axis=0
+        )
+        for third in range(3):
+            columns = pl.ds(third * width, width)
+            part = product(rows, weight_ref[:, columns], CONTRACT_INNER)
+            if third == 0:
+                part = (part + query_bias_ref[...]).astype(jnp.bfloat16) * HEAD_DIM**-0.5
+            elif third == 2:
+                part = part + value_bias_ref[...]
+            part = part.astype(jnp.bfloat16)
+            for i in range(4):
+                projected_ref[plane * 4 + i, :, columns] = part[
+                    i * frame_count : (i + 1) * frame_count
+                ]
+        store(plane).start()
+
+    link.first_round(crossing, line)
+    link.plane_done(z, (0, 1))
+    project(z)
+    link.second_round(crossing, line)
+
+    @pl.when(has_down)
+    def _():
+        link.plane_done(z - 1, (0, 1))
+        project(z - 1)
+
+    link.third_round(crossing, line)
+
+    @pl.when(has_up)
+    def _():
+        link.plane_done(z + 1, (0, 1))
+        project(z + 1)
+
+    link.plane_done(link.far_plane(), (0, 1))
+    project(link.far_plane())
+
+    @pl.when(jnp.logical_not(has_up & has_down))
+    def _():
+        lost = PLANES - 1 - z
+        for i in range(4):
+            projected_ref[lost * 4 + i] = jnp.zeros_like(projected_ref[0])
+            block_ref[lost * 4 + i, pl.ds(frame_count, padded - frame_count), :] = jnp.full(
+                (padded - frame_count, width), -1.0, jnp.bfloat16
+            )
+        store(lost).start()
+
+    every = jnp.concatenate(
+        [
+            block_ref[b, pl.ds(frame_count, 8), pl.ds(0, frame_count)].astype(jnp.float32)
+            for b in range(BLOCKS)
+        ],
+        axis=1,
+    )
+    every_ids_ref[...] = every
+    bias_ref[...] = jnp.where(
+        every[:1] == ids_column_ref[...].astype(jnp.float32), 0.0, mask_fill
+    )
+    lane = lax.broadcasted_iota(jnp.int32, (frame_count, 2 * HALF), 1)
+    total = BLOCKS * frame_count
+
+    def pair(j, logs):
+        query = projected_ref[mine, :, pl.ds(pl.multiple_of(j * 128, 128), 128)]
+        keys = projected_ref[:, :, pl.ds(pl.multiple_of(width + j * 128, 128), 128)].reshape(
+            total, 128
+        )
+        values = projected_ref[
+            :, :, pl.ds(pl.multiple_of(2 * width + j * 128, 128), 128)
+        ].reshape(total, 128)
+        outs = []
+        for h in range(2):
+            chosen = (lane < HALF) == (h == 0)
+            scores = (
+                product(jnp.where(chosen, query, jnp.zeros_like(query)), keys, CONTRACT_LAST)
+                + bias_ref[...]
+            )
+            peak = jnp.max(scores, axis=1, keepdims=True)
+            weights = jnp.exp(scores - peak)
+            whole = jnp.sum(weights, axis=1, keepdims=True)
+            outs.append(
+                product(weights.astype(jnp.bfloat16), values, CONTRACT_INNER) / whole
+            )
+            logs = jnp.where(lane == 2 * j + h, peak + jnp.log(whole), logs)
+        attended_ref[:, pl.ds(pl.multiple_of(j * 128, 128), 128)] = jnp.where(
+            lane < HALF, outs[0], outs[1]
+        )
+        return logs
+
+    log_ref[...] = lax.fori_loop(
+        0, PAIRS, pair, jnp.zeros((frame_count, 2 * HALF), jnp.float32)
+    )
+    for plane in range(PLANES):
+        store(plane).wait()
+    link.finish()
+
+
+def attend_back_kernel(
+    context_grad_ref,
+    attended_ref,
+    log_ref,
+    every_ids_ref,
+    ids_column_ref,
+    projected_ref,
+    grad_ref,
+    block_ref,
+    stats_ref,
+    bias_ref,
+    delta_ref,
+    send_sem,
+    recv_sem,
+):
+    frame_count, width = context_grad_ref.shape
+    first_rows = 80
+    link = RowGather(
+        [
+            (block_ref, 0, first_rows),
+            (block_ref, first_rows, frame_count - first_rows),
+            (stats_ref, 0, 32),
+        ],
+        send_sem,
+        recv_sem,
+    )
+    z, x, c = link.z, link.x, link.c
+    mine = z * 4 + x * 2 + c
+    has_up, has_down = z < PLANES - 1, z > 0
+    line, crossing = (2, 0), (1,)
+    lane = lax.broadcasted_iota(jnp.int32, (frame_count, 2 * HALF), 1)
+    total = BLOCKS * frame_count
+    link.meet()
+    block_ref[mine] = context_grad_ref[...]
+    delta = jnp.zeros((frame_count, 2 * HALF), jnp.float32)
+    for j in range(PAIRS):
+        columns = pl.ds(j * 128, 128)
+        both = context_grad_ref[:, columns].astype(jnp.float32) * attended_ref[:, columns]
+        for h in range(2):
+            one = jnp.sum(
+                jnp.where((lane < HALF) == (h == 0), both, 0.0), axis=1, keepdims=True
+            )
+            delta = jnp.where(lane == 2 * j + h, one, delta)
+    delta_ref[...] = delta
+    stats_ref[mine, pl.ds(0, 16), :] = log_ref[...].T[:16]
+    stats_ref[mine, pl.ds(16, 16), :] = delta.T[:16]
+    link.own(crossing, line)
+
+    bias_ref[...] = jnp.where(
+        every_ids_ref[:1] == ids_column_ref[...].astype(jnp.float32), 0.0, mask_fill
+    )
+
+    def columns_of(third, j):
+        return pl.ds(pl.multiple_of(third * width + j * 128, 128), 128)
+
+    def query_pair(j):
+        query = projected_ref[mine, :, columns_of(0, j)]
+        upstream = context_grad_ref[:, columns_of(0, j)]
+        keys = projected_ref[:, :, columns_of(1, j)].reshape(total, 128)
+        values = projected_ref[:, :, columns_of(2, j)].reshape(total, 128)
+        outs = []
+        for h in range(2):
+            chosen = (lane < HALF) == (h == 0)
+            nothing = jnp.zeros_like(query)
+            logs = jnp.sum(
+                jnp.where(lane == 2 * j + h, log_ref[...], 0.0), axis=1, keepdims=True
+            )
+            shift = jnp.sum(
+                jnp.where(lane == 2 * j + h, delta_ref[...], 0.0), axis=1, keepdims=True
+            )
+            scores = product(jnp.where(chosen, query, nothing), keys, CONTRACT_LAST)
+            probs = jnp.exp(scores + bias_ref[...] - logs)
+            prob_grad = product(jnp.where(chosen, upstream, nothing), values, CONTRACT_LAST)
+            score_grad = (probs * (prob_grad - shift)).astype(jnp.bfloat16)
+            outs.append(product(score_grad, keys, CONTRACT_INNER))
+        grad_ref[:, columns_of(0, j)] = (
+            jnp.where(lane < HALF, outs[0], outs[1]) * HEAD_DIM**-0.5
+        ).astype(jnp.bfloat16)
+
+    def query_pairs(first, last):
+        def one(j, carry):
+            query_pair(j)
+            return carry
+
+        lax.fori_loop(first, last, one, 0)
+
+    query_pairs(0, 2)
+    link.first_round(crossing, line)
+    query_pairs(2, 4)
+    link.second_round(crossing, line)
+    query_pairs(4, 5)
+    link.third_round(crossing, line)
+    query_pairs(5, 6)
+    link.plane_done(z, (0, 1, 2))
+    link.plane_done(z - 1, (0, 1, 2), has_down)
+    link.plane_done(z + 1, (0, 1, 2), has_up)
+    link.plane_done(link.far_plane(), (0, 1, 2))
+
+    @pl.when(jnp.logical_not(has_up & has_down))
+    def _():
+        lost = PLANES - 1 - z
+        for i in range(4):
+            block_ref[lost * 4 + i] = jnp.zeros_like(block_ref[0])
+            stats_ref[lost * 4 + i] = jnp.zeros_like(stats_ref[0])
+
+    def key_pair(j, carry):
+        key = projected_ref[mine, :, columns_of(1, j)]
+        value = projected_ref[mine, :, columns_of(2, j)]
+        queries = projected_ref[:, :, columns_of(0, j)].reshape(total, 128)
+        upstream = block_ref[:, :, columns_of(0, j)].reshape(total, 128)
+        key_outs = []
+        value_outs = []
+        for h in range(2):
+            chosen = (lane < HALF) == (h == 0)
+            nothing = jnp.zeros_like(key)
+            logs = jnp.concatenate(
+                [stats_ref[b, pl.ds(2 * j + h, 1), :] for b in range(BLOCKS)], axis=1
+            )
+            shift = jnp.concatenate(
+                [stats_ref[b, pl.ds(16 + 2 * j + h, 1), :] for b in range(BLOCKS)], axis=1
+            )
+            scores = product(jnp.where(chosen, key, nothing), queries, CONTRACT_LAST)
+            probs = jnp.exp(scores + bias_ref[...] - logs)
+            prob_grad = product(jnp.where(chosen, value, nothing), upstream, CONTRACT_LAST)
+            score_grad = (probs * (prob_grad - shift)).astype(jnp.bfloat16)
+            key_outs.append(product(score_grad, queries, CONTRACT_INNER))
+            value_outs.append(product(probs.astype(jnp.bfloat16), upstream, CONTRACT_INNER))
+        grad_ref[:, columns_of(1, j)] = jnp.where(
+            lane < HALF, key_outs[0], key_outs[1]
+        ).astype(jnp.bfloat16)
+        grad_ref[:, columns_of(2, j)] = jnp.where(
+            lane < HALF, value_outs[0], value_outs[1]
+        ).astype(jnp.bfloat16)
+        return carry
+
+    lax.fori_loop(0, PAIRS, key_pair, 0)
+    link.finish()
+
+
+class QuadSum:
+    def __init__(self, left, right, buffers, sems):
+        self.left, self.right = left, right
+        self.lefts, self.rights, self.whole, self.x_in, self.halved, self.z_in, self.last, self.side = (
+            buffers
+        )
+        self.send, self.recv_left, self.recv_right, self.x_sems, self.z_send, self.z_recv, self.side_sems = (
+            sems
+        )
+        self.y, self.z, self.x, self.c = where_am_i()
+        self.quad = self.y * 2 + self.c
+        self.left_half = self.lefts.shape[2]
+        self.right_half = self.rights.shape[2]
+        self.flying = []
+
+    def device(self, y, z, x, c):
+        return (y, z * 4 + x * 2 + c)
+
+    def fly(self, source, target, send_sem, recv_sem, device):
+        copy = pltpu.make_async_remote_copy(
+            src_ref=source,
+            dst_ref=target,
+            send_sem=send_sem,
+            recv_sem=recv_sem,
+            device_id=device,
+            device_id_type=MESH_ID,
+        )
+        copy.start()
+        self.flying.append(copy)
+
+    def left_of(self, y):
+        return self.left.at[:, pl.ds(pl.multiple_of(y * self.left_half, 128), self.left_half)]
+
+    def right_of(self, c):
+        return self.right.at[:, pl.ds(pl.multiple_of(c * self.right_half, 128), self.right_half)]
+
+    def share_left(self):
+        y, z, x, c, quad = self.y, self.z, self.x, self.c, self.quad
+        self.fly(
+            self.left_of(1 - y), self.lefts.at[quad], self.send.at[0], self.recv_left.at[quad],
+            self.device(1 - y, z, x, c),
+        )
+        self.fly(
+            self.left_of(y), self.lefts.at[quad], self.send.at[1], self.recv_left.at[quad],
+            self.device(y, z, x, 1 - c),
+        )
+
+    def share_right(self):
+        y, z, x, c, quad = self.y, self.z, self.x, self.c, self.quad
+        self.fly(
+            self.right_of(c), self.rights.at[quad], self.send.at[2], self.recv_right.at[quad],
+            self.device(1 - y, z, x, c),
+        )
+        self.fly(
+            self.right_of(1 - c), self.rights.at[quad], self.send.at[3], self.recv_right.at[quad],
+            self.device(1 - y, z, x, 1 - c),
+        )
+        self.fly(
+            self.right_of(1 - c), self.rights.at[quad], self.send.at[4], self.recv_right.at[quad],
+            self.device(y, z, x, 1 - c),
+        )
+
+    def landed(self, ref, sem):
+        pltpu.make_async_remote_copy(
+            src_ref=ref,
+            dst_ref=ref,
+            send_sem=self.send.at[0],
+            recv_sem=sem,
+            device_id=self.device(self.y, self.z, self.x, 1 - self.c),
+            device_id_type=MESH_ID,
+        ).wait_recv()
+
+    def relay_left(self):
+        peer = (1 - self.y) * 2 + self.c
+        self.landed(self.lefts.at[peer], self.recv_left.at[peer])
+        self.fly(
+            self.lefts.at[peer], self.lefts.at[peer], self.send.at[5], self.recv_left.at[peer],
+            self.device(self.y, self.z, self.x, 1 - self.c),
+        )
+
+    def multiply(self):
+        y, c = self.y, self.c
+        self.lefts[self.quad] = self.left_of(y)[...]
+        self.rights[self.quad] = self.right_of(c)[...]
+        for other in (y * 2 + 1 - c, (1 - y) * 2 + 1 - c):
+            self.landed(self.lefts.at[other], self.recv_left.at[other])
+        for other in (y * 2 + 1 - c, (1 - y) * 2 + c, (1 - y) * 2 + 1 - c):
+            self.landed(self.rights.at[other], self.recv_right.at[other])
+        tokens = self.lefts.shape[0] * self.lefts.shape[1]
+        planes, _, rows, _ = self.whole.shape
+        step = 384
+        if self.left_half > step:
+            right = self.rights[...].reshape(tokens, self.right_half)
+
+            def one(i, carry):
+                left = self.lefts[:, :, pl.ds(pl.multiple_of(i * step, 128), step)]
+                part = product(left.reshape(tokens, step), right, CONTRACT_FIRST)
+                self.whole[i] = part.astype(jnp.bfloat16).reshape(2, rows, self.right_half)
+                return carry
+
+            lax.fori_loop(0, self.left_half // step, one, 0)
+        else:
+            left = self.lefts[...].reshape(tokens, self.left_half)
+
+            def one(i, carry):
+                columns = pl.ds(pl.multiple_of(i * step, 128), step)
+                part = product(
+                    left, self.rights[:, :, columns].reshape(tokens, step), CONTRACT_FIRST
+                )
+                self.whole[:, :, :, columns] = part.astype(jnp.bfloat16).reshape(
+                    planes, 2, rows, step
+                )
+                return carry
+
+            lax.fori_loop(0, self.right_half // step, one, 0)
+
+    def halve(self):
+        self.fly(
+            self.whole.at[:, 1 - self.x], self.x_in, self.x_sems.at[0], self.x_sems.at[1],
+            self.device(self.y, self.z, 1 - self.x, self.c),
+        )
+
+    def spread(self):
+        self.landed(self.x_in, self.x_sems.at[1])
+        self.halved[...] = (
+            self.whole[:, self.x].astype(jnp.float32) + self.x_in[...].astype(jnp.float32)
+        ).astype(jnp.bfloat16)
+        for step in range(1, PLANES):
+            target = (self.z + step) % PLANES
+            self.fly(
+                self.halved.at[target], self.z_in.at[self.z], self.z_send.at[step],
+                self.z_recv.at[self.z], self.device(self.y, target, self.x, self.c),
+            )
+
+    def collect(self):
+        total = self.halved[self.z].astype(jnp.float32)
+        for step in range(1, PLANES):
+            source = (self.z + step) % PLANES
+            self.landed(self.z_in.at[source], self.z_recv.at[source])
+            total = total + self.z_in[source].astype(jnp.float32)
+        self.last[...] = total
+        rows = self.last.shape[0] // 2
+        self.fly(
+            self.last.at[pl.ds(pl.multiple_of((1 - self.c) * rows, 8), rows)], self.side,
+            self.side_sems.at[0], self.side_sems.at[1],
+            self.device(self.y, self.z, self.x, 1 - self.c),
+        )
+
+    def deliver(self, out_ref):
+        rows = self.last.shape[0] // 2
+        width = self.right_half
+        out_ref[:, pl.ds(pl.multiple_of(self.c * width, 128), width)] = self.last[
+            pl.ds(pl.multiple_of(self.c * rows, 8), rows), :
+        ]
+        self.landed(self.side, self.side_sems.at[1])
+        out_ref[:, pl.ds(pl.multiple_of((1 - self.c) * width, 128), width)] = self.side[...]
+
+    def finish(self):
+        for copy in self.flying:
+            copy.wait_send()
+
+
+QUAD_REFS = 15
+
+
+def quad_scratch(frame_count, left_width, right_width):
+    left_half, right_half = left_width // 2, right_width // 2
+    rows = left_half // (2 * PLANES)
+    low, wide = jnp.bfloat16, jnp.float32
+    return [
+        pltpu.VMEM((4, frame_count, left_half), low),
+        pltpu.VMEM((4, frame_count, right_half), low),
+        pltpu.VMEM((PLANES, 2, rows, right_half), low),
+        pltpu.VMEM((PLANES, rows, right_half), low),
+        pltpu.VMEM((PLANES, rows, right_half), low),
+        pltpu.VMEM((PLANES, rows, right_half), low),
+        pltpu.VMEM((rows, right_half), wide),
+        pltpu.VMEM((rows // 2, right_half), wide),
+        pltpu.SemaphoreType.DMA((6,)),
+        pltpu.SemaphoreType.DMA((4,)),
+        pltpu.SemaphoreType.DMA((4,)),
+        pltpu.SemaphoreType.DMA((2,)),
+        pltpu.SemaphoreType.DMA((PLANES,)),
+        pltpu.SemaphoreType.DMA((PLANES,)),
+        pltpu.SemaphoreType.DMA((2,)),
+    ]
+
+
+class VectorSum:
+    def __init__(self, ref, partial, arrived, send_sem, recv_sem):
+        self.ref, self.partial, self.arrived = ref, partial, arrived
+        self.send_sem, self.recv_sem = send_sem, recv_sem
+        self.y, self.z, self.x, self.c = where_am_i()
+        self.flying = []
+
+    def device(self, y, z, x, c):
+        return (y, z * 4 + x * 2 + c)
+
+    def copy(self, source, slot, device):
+        return pltpu.make_async_remote_copy(
+            src_ref=source,
+            dst_ref=self.arrived.at[slot],
+            send_sem=self.send_sem.at[slot],
+            recv_sem=self.recv_sem.at[slot],
+            device_id=device,
+            device_id_type=MESH_ID,
+        )
+
+    def start(self, stage):
+        y, z, x, c = self.y, self.z, self.x, self.c
+        source = self.ref if stage == 0 else self.partial.at[stage - 1]
+        if stage < 3:
+            device = (
+                self.device(y, z, x, 1 - c),
+                self.device(1 - y, z, x, c),
+                self.device(y, z, 1 - x, c),
+            )[stage]
+            copy = self.copy(source, stage, device)
+            copy.start()
+            self.flying.append(copy)
+        else:
+            for step in range(1, PLANES):
+                copy = self.copy(
+                    source, 2 + step, self.device(y, (z + step) % PLANES, x, c)
+                )
+                copy.start()
+                self.flying.append(copy)
+
+    def take(self, stage):
+        y, z, x, c = self.y, self.z, self.x, self.c
+        total = self.ref[...] if stage == 0 else self.partial[stage - 1]
+        for slot in (stage,) if stage < 3 else (3, 4, 5):
+            self.copy(self.ref, slot, self.device(y, z, x, 1 - c)).wait_recv()
+            total = total + self.arrived[slot]
+        self.partial[stage] = total
+
+    def finish(self):
+        for copy in self.flying:
+            copy.wait_send()
+
+    def own_share(self, rows, share):
+        width = self.ref.shape[1]
+        place = self.y * 16 + self.z * 4 + self.x * 2 + self.c
+        per_row = width // share
+        offset = place % per_row * share
+        row_index = lax.broadcasted_iota(jnp.int32, (width, 128), 0)
+        column_index = lax.broadcasted_iota(jnp.int32, (width, 128), 1)
+        picked = jnp.where(
+            (row_index == column_index + offset) & (column_index < share), 1.0, 0.0
+        ).astype(jnp.bfloat16)
+        rest = rows
+        total = jnp.zeros((rows.shape[0], 128), jnp.float32)
+        for _ in range(3):
+            piece = rest.astype(jnp.bfloat16)
+            total = total + product(piece, picked, CONTRACT_INNER)
+            rest = rest - piece.astype(jnp.float32)
+        return total, place // per_row
+
+
+def gradient_kernel(count, *refs):
+    operands = refs[: 2 * count]
+    vector_ref = refs[2 * count]
+    out_refs = refs[2 * count + 1 : 3 * count + 1]
+    share_ref, up_share_ref = refs[3 * count + 1 : 3 * count + 3]
+    scratch = refs[3 * count + 3 :]
+    sums = []
+    for w in range(count):
+        held = scratch[w * QUAD_REFS : (w + 1) * QUAD_REFS]
+        sums.append(QuadSum(operands[2 * w], operands[2 * w + 1], held[:8], held[8:]))
+    vector = VectorSum(vector_ref, *scratch[count * QUAD_REFS :])
+    one = sums[0]
+    y, z, x, c = one.y, one.z, one.x, one.c
+    partners = [
+        (None, one.device(y, z, x, 1 - c)),
+        (None, one.device(1 - y, z, x, c)),
+        (None, one.device(1 - y, z, x, 1 - c)),
+        (None, one.device(y, z, 1 - x, c)),
+    ]
+    partners += [(None, one.device(y, (z + step) % PLANES, x, c)) for step in range(1, PLANES)]
+    meet(partners, len(partners))
+    vector.start(0)
+    for each in sums:
+        each.share_left()
+        each.share_right()
+    stage = 0
+    for each in sums:
+        each.relay_left()
+        each.multiply()
+        each.halve()
+        vector.take(stage)
+        stage += 1
+        if stage < 4:
+            vector.start(stage)
+    for each in sums:
+        each.spread()
+    for each in sums:
+        each.collect()
+    for each, out_ref in zip(sums, out_refs):
+        each.deliver(out_ref)
+    total = vector.partial[3]
+    shares, _ = vector.own_share(total[:8], out_refs[0].shape[0] // 4)
+    share_ref[...] = shares
+    up_shares, row = vector.own_share(total[8:16], out_refs[0].shape[0])
+    keep = lax.broadcasted_iota(jnp.int32, up_shares.shape, 0) == row
+    up_share_ref[...] = jnp.sum(jnp.where(keep, up_shares, 0.0), axis=0, keepdims=True)
+    for each in sums:
+        each.finish()
+    vector.finish()
+
+
+def weight_gradients(pairs, vectors):
+    frame_count = pairs[0][0].shape[0]
+    operands, outs, scratch = [], [], []
+    for left, right in pairs:
+        operands += [left, right]
+        outs.append(jax.ShapeDtypeStruct((left.shape[1] // 32, right.shape[1]), jnp.float32))
+        scratch += quad_scratch(frame_count, left.shape[1], right.shape[1])
+    outs += [
+        jax.ShapeDtypeStruct((8, 128), jnp.float32),
+        jax.ShapeDtypeStruct((1, 128), jnp.float32),
+    ]
+    scratch += [
+        pltpu.VMEM((4,) + vectors.shape, jnp.float32),
+        pltpu.VMEM((6,) + vectors.shape, jnp.float32),
+        pltpu.SemaphoreType.DMA((6,)),
+        pltpu.SemaphoreType.DMA((6,)),
+    ]
+    return pl.pallas_call(
+        functools.partial(gradient_kernel, len(pairs)),
+        out_shape=tuple(outs),
+        in_specs=[IN_VMEM] * (len(operands) + 1),
+        out_specs=(IN_VMEM,) * len(outs),
+        scratch_shapes=scratch,
+        compiler_params=pltpu.CompilerParams(
+            collective_id=2, has_side_effects=True, vmem_limit_bytes=VMEM_BYTES
+        ),
+    )(*operands, vectors)
+
+
+def layer_step(
+    frames,
+    segment_ids,
+    qkv_weight,
+    query_bias,
+    value_bias,
+    out_weight,
+    out_bias,
+    norm1_gain,
+    norm1_shift,
+    up_weight,
+    up_bias,
+    down_weight,
+    down_bias,
+    norm2_gain,
+    norm2_shift,
+    cotangent,
+):
+    inputs = frames[0]
+    frame_count, width = inputs.shape
+    low, wide = jnp.bfloat16, jnp.float32
+    ids_column = segment_ids.reshape(frame_count, 1)
+    attended, log_total, every_ids, projected = pl.pallas_call(
+        attend_kernel,
+        out_shape=(
+            jax.ShapeDtypeStruct((frame_count, width), wide),
+            jax.ShapeDtypeStruct((frame_count, 2 * HALF), wide),
+            jax.ShapeDtypeStruct((8, BLOCKS * frame_count), wide),
+            jax.ShapeDtypeStruct((BLOCKS, frame_count, 3 * width), low),
+        ),
+        in_specs=[IN_VMEM] * 6,
+        out_specs=(IN_VMEM, IN_VMEM, IN_VMEM, IN_PLACE),
+        scratch_shapes=[
+            pltpu.VMEM((BLOCKS, frame_count + 16, width), low),
+            pltpu.VMEM((BLOCKS, frame_count, 3 * width), low),
+            pltpu.VMEM((frame_count, BLOCKS * frame_count), wide),
+            pltpu.SemaphoreType.DMA((2, 4, BLOCKS)),
+            pltpu.SemaphoreType.DMA((2, BLOCKS)),
+            pltpu.SemaphoreType.DMA((PLANES,)),
+        ],
+        compiler_params=pltpu.CompilerParams(
+            collective_id=0, has_side_effects=True, vmem_limit_bytes=VMEM_BYTES
+        ),
+    )(inputs, segment_ids, ids_column, qkv_weight, query_bias[None], value_bias[None])
+    context = attended.astype(low)
+    resid_one = (
+        inputs.astype(wide) + jnp.dot(context, out_weight, preferred_element_type=wide) + out_bias
+    )
+    hidden, normed_one, inverse_one = layer_norm(resid_one, norm1_gain, norm1_shift)
+    hidden_low = hidden.astype(low)
+    pre_act = jnp.dot(hidden_low, up_weight, preferred_element_type=wide) + up_bias
+    act_low = jax.nn.gelu(pre_act, approximate=False).astype(low)
+    resid_two = hidden + jnp.dot(act_low, down_weight, preferred_element_type=wide) + down_bias
+    output, normed_two, inverse_two = layer_norm(resid_two, norm2_gain, norm2_shift)
+    upstream = cotangent[0].astype(wide)
+    second_grad, gain_two_grad, shift_two_grad = norm_back(
+        upstream, normed_two, inverse_two, norm2_gain
+    )
+    second_low = second_grad.astype(low)
+    pre_grad = jnp.einsum(
+        "td,fd->tf", second_low, down_weight, preferred_element_type=wide
+    ) * gelu_slope(pre_act)
+    pre_low = pre_grad.astype(low)
+    hidden_grad = second_grad + jnp.einsum(
+        "tf,df->td", pre_low, up_weight, preferred_element_type=wide
+    )
+    first_grad, gain_one_grad, shift_one_grad = norm_back(
+        hidden_grad, normed_one, inverse_one, norm1_gain
+    )
+    first_low = first_grad.astype(low)
+    context_grad = jnp.einsum("te,de->td", first_low, out_weight, preferred_element_type=wide).astype(
+        low
+    )
+    proj_grad = pl.pallas_call(
+        attend_back_kernel,
+        out_shape=jax.ShapeDtypeStruct((frame_count, 3 * width), low),
+        in_specs=[IN_VMEM] * 6,
+        out_specs=IN_VMEM,
+        scratch_shapes=[
+            pltpu.VMEM((BLOCKS, frame_count, width), low),
+            pltpu.VMEM((BLOCKS, 32, frame_count), wide),
+            pltpu.VMEM((frame_count, BLOCKS * frame_count), wide),
+            pltpu.VMEM((frame_count, 2 * HALF), wide),
+            pltpu.SemaphoreType.DMA((3, 4, BLOCKS)),
+            pltpu.SemaphoreType.DMA((3, BLOCKS)),
+        ],
+        compiler_params=pltpu.CompilerParams(
+            collective_id=1, has_side_effects=True, vmem_limit_bytes=VMEM_BYTES
+        ),
+    )(context_grad, attended, log_total, every_ids, ids_column, projected)
+    input_grad = (
+        jnp.einsum("te,de->td", proj_grad, qkv_weight, preferred_element_type=wide) + first_grad
+    )
+    proj_sums = jnp.sum(proj_grad.astype(wide), axis=0)
+    vectors = jnp.concatenate(
+        [
+            jnp.stack(
+                [
+                    proj_sums[:width],
+                    proj_sums[2 * width :],
+                    jnp.sum(first_grad, axis=0),
+                    gain_one_grad,
+                    shift_one_grad,
+                    jnp.sum(second_grad, axis=0),
+                    gain_two_grad,
+                    shift_two_grad,
+                ]
+            ),
+            jnp.sum(pre_grad, axis=0).reshape(4, width),
+            jnp.zeros((4, width), wide),
+        ],
+        axis=0,
+    )
+    down_grad, up_grad, out_grad, qkv_grad, shares, up_share = weight_gradients(
+        [
+            (act_low, second_low),
+            (hidden_low, pre_low),
+            (context, first_low),
+            (inputs, proj_grad),
+        ],
+        vectors,
+    )
+    share = down_grad.shape[0] // 4
+    return (
+        output.astype(low)[None],
+        input_grad[None],
+        qkv_grad,
+        shares[0, :share],
+        shares[1, :share],
+        out_grad,
+        shares[2, :share],
+        shares[3, :share],
+        shares[4, :share],
+        up_grad,
+        up_share[0, : 4 * share],
+        down_grad,
+        shares[5, :share],
+        shares[6, :share],
+        shares[7, :share],
+    )
+
+
 def solution(mesh):
+    chosen = layer_step if dict(mesh.shape) == {"rows": 2, "seq": 16} else shards
     in_specs = (
         P("rows", "seq", None),
         P("rows", "seq"),
@@ -395,4 +1345,4 @@
         P(("rows", "seq")),
         P(("rows", "seq")),
     )
-    return jax.shard_map(shards, mesh=mesh, in_specs=in_specs, out_specs=out_specs, check_vma=False)
+    return jax.shard_map(chosen, mesh=mesh, in_specs=in_specs, out_specs=out_specs, check_vma=False)

time: 1070 us -> 213 us (0.20)
  waiting for transfers between devices: 517 us -> 0 us
  Pallas kernels: 0 us -> 181 us
  matrix products: 195 us -> 14.6 us
  local copies, waits for them, and re-layouts: 183 us -> 10.9 us
  other arithmetic: 93.2 us -> 4.13 us
  blocking collectives: 63.1 us -> 0 us
  between operations: 14.1 us -> 1.17 us
    reduce_scatter x3 -> x0, waiting for transfers between devices: 283 us -> none  [the longest x1 142 us: shards(): lax.psum_scatter(down_grad, ('rows', 'seq'), scatter_dimension=0, tiled=T...]
    ppermute x94 -> x0, waiting for transfers between devices: 183 us -> none  [passed_along(): return lax.ppermute(value, axis, pairs)]
    pallas_call x0 -> x3, Pallas kernels: none -> 181 us  [the longest x1 108 us: weight_gradients(): pl.pallas_call(functools.partial(gradient_kernel, len(pairs)), out_shape=...]
    dot_general x124 -> x7, matrix products: 195 us -> 14.6 us  [the longest x1 4.36 us: layer_step(): jnp.dot(hidden_low, up_weight, preferred_element_type=wide) + up_bias]
    while x329 -> x0, local copies, waits for them, and re-layouts: 124 us -> none
    convert_element_type x35 -> x4, other arithmetic: 57.5 us -> 1.21 us  [the longest x1 1.03 us: layer_step(): context = attended.astype(low)]
    unnamed x5 -> x0, waiting for transfers between devices: 51 us -> none
    unnamed x1 -> x0, blocking collectives: 39.4 us -> none
  transfers between devices with their start and end apart: 98 -> 0, of which waited for: 50 -> 0; matrix products, arithmetic and copies ran while one was open for 34% -> 0% of each run, Pallas kernels for 0% -> 0%
where the time goes in v1:
time: 213 us; the launch traced here: 212 us
  Pallas kernels  181 us (85%)
  matrix products  14.6 us (7%)
  local copies, waits for them, and re-layouts  10.9 us (5%)
  other arithmetic  4.13 us (2%)
    pallas_call x1, Pallas kernels, weight_gradients(): pl.pallas_call(functools.partial(gradient_kernel, len(pairs)), out_shape=...  108 us
    pallas_call x1, Pallas kernels, layer_step(): pl.pallas_call(attend_kernel, out_shape=(jax.ShapeDtypeStruct((frame_coun...  36.7 us
    pallas_call x1, Pallas kernels, layer_step(): pl.pallas_call(attend_back_kernel, out_shape=jax.ShapeDtypeStruct((frame_...  36.3 us
    dot_general x1, matrix products, layer_step(): jnp.dot(hidden_low, up_weight, preferred_element_type=wide) + up_bias  4.36 us

profile of v1, /device:TPU:0, one launch (start us, length us, event | category | flops | bytes accessed | tf_op | source)
XLA Modules:
  0.0 212.0 jit_solution(8894238706469355594)
XLA Ops:
  0.6 0.0 copy-start
  0.7 0.0 copy-start.5
  0.7 0.0 copy-start.18
  0.7 1.5 copy.31.ids_column_ref
  2.2 1.3 broadcast_in_dim.10.query_bias_ref
  3.4 1.3 broadcast_in_dim.11.value_bias_ref
  4.7 36.7 %shard_map.271 = (f32[128,768]{1,0:T(8,128)}, f32[128,128]{1,0:T(8,128)}, f32[8,2048]{1,0:T(8,128)}, bf16[16,128,2304]{2,1,0:T(8,128)(2,1)}) custom-call(bf16[128,768]{1,0:T(8,128)(2,1)} %bitcast.62, s32[1,128]{1,0:T(1,128)} %ids_row_ref.1, s32[128,1]{1,0:T(8,128)} %copy.31.ids_column_ref, bf16[768,2304]{1,0:T(8,128)(2,1)} %weight_ref.1, ...), custom_call_target="tpu_custom_call" | custom-call | tf_op jit(solution)/shard_map/pallas_call | solution.py:1191
  41.4 0.0 copy-start.15
  41.5 0.0 copy-start.16
  41.5 1.0 convert_element_type.37.refs_4_
  42.5 0.0 copy-done
  42.5 0.0 copy-done.5
  42.5 0.0 copy-done.18
  42.5 0.0 copy-start.7
  42.5 0.0 copy-start.21
  42.5 0.4 fusion.33
  43.0 0.2 multiply_reduce_fusion.3
  43.2 0.0 copy-done.7
  43.2 0.0 copy-done.15
  43.2 0.0 copy-done.16
  43.2 0.0 slice-start
  43.2 0.1 fusion.26.refs_2_
  43.4 0.0 copy-done.2
  43.4 0.0 copy-done.21
  43.4 0.0 copy-start.9
  43.4 0.0 slice-start.1
  43.4 0.0 copy-start.19
  43.4 4.4 %fusion.2 = (bf16[128,3072]{1,0:T(8,128)(2,1)S(1)}, f32[128,3072]{1,0:T(8,128)S(1)}) fusion(f32[3072]{0:T(1024)S(1)} %copy-done.21, bf16[128,768]{1,0:T(8,128)(2,1)S(1)} %fusion.26.refs_2_, bf16[768,3072]{1,0:T(8,128)(2,1)S(1)} %copy-done.2), kind=kOutput, calls=%fused_computation.6 | convolution fusion | flops 629932032 | bytes 7286784 | tf_op jit(solution)/shard_map/dot_general | solution.py:1219
  47.8 0.0 copy-done.9
  47.8 0.0 copy-start.3
  47.8 0.0 slice-done
  47.8 0.0 slice-done.1
  47.8 0.0 copy-done.19
  47.9 0.0 copy-start.6
  47.9 0.0 copy-start.17
  47.9 0.0 copy-start.20
  47.9 0.9 fusion.34
  48.8 0.0 copy-done.3
  48.8 0.2 multiply_reduce_fusion.2
  49.0 0.0 copy-done.6
  49.0 0.0 copy-done.17
  49.0 0.3 fusion.25
  49.3 0.0 copy-done.20
  49.3 0.9 fusion.28
  50.2 0.0 copy-start.10
  50.2 1.7 fusion.31
  52.0 1.8 multiply_reduce_fusion
  53.9 0.2 fusion.30
  54.1 0.0 copy-start.8
  54.1 1.2 convolution_convert_fusion.context_grad_ref
  55.3 36.3 %shard_map.272.refs_7_ = bf16[128,2304]{1,0:T(8,128)(2,1)} custom-call(bf16[128,768]{1,0:T(8,128)(2,1)} %convolution_convert_fusion.context_grad_ref, f32[128,768]{1,0:T(8,128)} %get-tuple-element.25.attended_ref, f32[128,128]{1,0:T(8,128)} %get-tuple-element.26.log_ref, f32[8,2048]{1,0:T(8,128)} %get-tuple-element.27.every_ids_ref, ...), custom_call_target="tpu_custom_call" | custom-call | tf_op jit(solution)/shard_map/pallas_call | solution.py:1242
  91.6 0.0 copy-done.8
  91.6 1.2 convert_reduce_fusion
  92.9 1.3 concatenate.3.refs_8_
  94.2 108.2 %shard_map.273 = (f32[96,768]{1,0:T(8,128)}, f32[24,3072]{1,0:T(8,128)}, f32[24,768]{1,0:T(8,128)}, f32[24,2304]{1,0:T(8,128)}, f32[8,128]{1,0:T(8,128)}, /*index=5*/f32[1,128]{1,0:T(1,128)}) custom-call(bf16[128,3072]{1,0:T(8,128)(2,1)} %copy-done.3, bf16[128,768]{1,0:T(8,128)(2,1)} %copy-done.10, bf16[128,768]{1,0:T(8,128)(2,1)} %copy-done.9, ...), custom_call_target="tpu_custom_call" | custom-call | tf_op jit(solution)/shard_map/pallas_call | solution.py:1157
  202.4 1.5 slice_bitcast_fusion
  204.0 1.1 slice_bitcast_fusion.3
  205.1 0.0 copy-done.1
  205.1 4.1 %fusion.15 = f32[1,128,768]{2,1,0:T(8,128)} fusion(f32[128,768]{1,0:T(8,128)S(1)} %get-tuple-element.45, bf16[128,2304]{1,0:T(8,128)(2,1)S(1)} %copy-done.1, bf16[768,2304]{1,0:T(8,128)(2,1)} %weight_ref.1), kind=kOutput, calls=%fused_computation.29 | convolution fusion | flops 453083136 | bytes 4915200 | tf_op jit(solution)/shard_map/te,de->td/dot_general | solution.py:1260
  209.2 0.7 copy.37
  209.9 0.6 copy.38
  210.5 0.7 copy.39
  211.2 0.0 copy-done.11
  211.2 0.7 copy.40
  (34 shorter events, 0.2 us)
Async XLA Ops:
  0.6 41.8 %copy-start = (bf16[768,768]{1,0:T(8,128)(2,1)S(1)}, bf16[768,768]{1,0:T(8,128)(2,1)}, u32[]{:S(2)}) copy-start(bf16[768,768]{1,0:T(8,128)(2,1)} %param.21) | copy-start | bytes 3538948
  0.7 41.8 %copy-start.5 = (bf16[1,128,768]{2,1,0:T(8,128)(2,1)S(1)}, bf16[1,128,768]{2,1,0:T(8,128)(2,1)}, u32[]{:S(2)}) copy-start(bf16[1,128,768]{2,1,0:T(8,128)(2,1)} %param.16) | copy-start | bytes 589828
  0.7 41.8 %copy-start.18 = (f32[768]{0:T(1024)S(1)}, f32[768]{0:T(1024)}, u32[]{:S(2)}) copy-start(f32[768]{0:T(1024)} %param.22) | copy-start | bytes 9220
  4.7 38.7 %copy-start.2 = (bf16[768,3072]{1,0:T(8,128)(2,1)S(1)}, bf16[768,3072]{1,0:T(8,128)(2,1)}, u32[]{:S(2)}) copy-start(bf16[768,3072]{1,0:T(8,128)(2,1)} %param.25) | copy-start | bytes 14155780
  41.4 1.8 copy-start.15
  41.5 1.8 copy-start.16
  42.5 0.7 copy-start.7
  42.5 0.9 copy-start.21
  43.2 4.6 %slice-start = ((s8[4718592]{0:T(1024)(128)(4,1)}), s8[4194304]{0:T(1024)(128)(4,1)S(1)}, s32[]{:S(2)}) async-start(s8[4718592]{0:T(1024)(128)(4,1)} %bitcast.60), calls=%async_computation | async-start | bytes 8388608
  43.4 4.4 %copy-start.9 = (bf16[128,768]{1,0:T(8,128)(2,1)}, bf16[128,768]{1,0:T(8,128)(2,1)S(1)}, u32[]{:S(2)}) copy-start(bf16[128,768]{1,0:T(8,128)(2,1)S(1)} %fusion.26.refs_2_) | copy-start | bytes 589828
  43.4 4.4 %slice-start.1 = ((s8[4718592]{0:T(1024)(128)(4,1)}), s8[524288]{0:T(1024)(128)(4,1)S(1)}, s32[]{:S(2)}) async-start(s8[4718592]{0:T(1024)(128)(4,1)} %bitcast.60), calls=%async_computation.1 | async-start | bytes 1048576
  43.4 4.4 %copy-start.19 = (f32[768]{0:T(1024)S(1)}, f32[768]{0:T(1024)}, u32[]{:S(2)}) copy-start(f32[768]{0:T(1024)} %param.28) | copy-start | bytes 9220
  47.8 1.0 copy-start.3
  47.9 1.2 copy-start.6
  47.9 1.2 copy-start.17
  47.9 1.4 copy-start.20
  50.2 1.8 copy-start.10
  52.0 1.8 copy-start.4
  54.1 37.5 %copy-start.8 = (bf16[128,768]{1,0:T(8,128)(2,1)}, bf16[128,768]{1,0:T(8,128)(2,1)S(1)}, u32[]{:S(2)}) copy-start(bf16[128,768]{1,0:T(8,128)(2,1)S(1)} %convert_element_type.45.refs_5_) | copy-start | bytes 589828
  94.2 110.9 %copy-start.1 = (bf16[128,2304]{1,0:T(8,128)(2,1)S(1)}, bf16[128,2304]{1,0:T(8,128)(2,1)}, u32[]{:S(2)}) copy-start(bf16[128,2304]{1,0:T(8,128)(2,1)} %shard_map.272.refs_7_) | copy-start | bytes 1769476
  205.1 4.1 %copy-start.13 = (f32[24,2304]{1,0:T(8,128)S(1)}, f32[24,2304]{1,0:T(8,128)}, u32[]{:S(2)}) copy-start(f32[24,2304]{1,0:T(8,128)} %get-tuple-element.86) | copy-start | bytes 663556
  205.1 4.8 %copy-start.14 = (f32[24,768]{1,0:T(8,128)S(1)}, f32[24,768]{1,0:T(8,128)}, u32[]{:S(2)}) copy-start(f32[24,768]{1,0:T(8,128)} %get-tuple-element.89) | copy-start | bytes 221188
  205.1 5.4 %copy-start.12 = (f32[24,3072]{1,0:T(8,128)S(1)}, f32[24,3072]{1,0:T(8,128)}, u32[]{:S(2)}) copy-start(f32[24,3072]{1,0:T(8,128)} %get-tuple-element.93) | copy-start | bytes 884740
  205.1 6.2 %copy-start.11 = (f32[96,768]{1,0:T(8,128)S(1)}, f32[96,768]{1,0:T(8,128)}, u32[]{:S(2)}) copy-start(f32[96,768]{1,0:T(8,128)} %get-tuple-element.95) | copy-start | bytes 884740

commit v2 on v0

--- a/solution.py
+++ b/solution.py
@@ -1,8 +1,12 @@
+import functools
 import math
+import typing
 
 import jax
 import jax.numpy as jnp
 from jax import lax
+from jax.experimental import pallas as pl
+from jax.experimental.pallas import tpu as pltpu
 from jax.sharding import PartitionSpec as P
 
 HEADS = 12
@@ -359,7 +363,1042 @@
     )
 
 
+HALF = HEAD_DIM
+PAIRS = HEADS // 2
+CONTRACT_LAST = (((1,), (1,)), ((), ()))
+CONTRACT_INNER = (((1,), (0,)), ((), ()))
+CONTRACT_FIRST = (((0,), (0,)), ((), ()))
+IN_VMEM = pl.BlockSpec(memory_space=pltpu.VMEM)
+IN_PLACE = pl.BlockSpec(memory_space=pl.ANY)
+MESH_ID = pl.DeviceIdType.MESH
+VMEM_BYTES = 60 << 20
+BLOCKS = 16
+PLANES = 4
+
+
+def product(left, right, dims):
+    return lax.dot_general(left, right, dims, preferred_element_type=jnp.float32)
+
+
+def where_am_i():
+    row = lax.axis_index("rows")
+    place = lax.axis_index("seq")
+    return row, place // 4, place // 2 % 2, place % 2
+
+
+def meet(partners, count):
+    barrier = pltpu.get_barrier_semaphore()
+    for present, target in partners:
+
+        def signal(target=target):
+            pl.semaphore_signal(barrier, inc=1, device_id=target, device_id_type=MESH_ID)
+
+        if present is None:
+            signal()
+        else:
+            pl.when(present)(signal)
+    pl.semaphore_wait(barrier, count)
+
+
+class RowGather:
+    UP, DOWN, ACROSS, BESIDE = range(4)
+
+    def __init__(self, parts, send_sem, recv_sem):
+        self.parts = parts
+        self.send_sem = send_sem
+        self.recv_sem = recv_sem
+        self.row, self.z, self.x, self.c = where_am_i()
+        self.sent = []
+
+    def device(self, z, x, c):
+        return (self.row, z * 4 + x * 2 + c)
+
+    def targets(self):
+        return (
+            self.device(self.z + 1, self.x, self.c),
+            self.device(self.z - 1, self.x, self.c),
+            self.device(self.z, 1 - self.x, self.c),
+            self.device(self.z, self.x, 1 - self.c),
+        )
+
+    def meet(self):
+        up, down, across, beside = self.targets()
+        has_up = self.z < PLANES - 1
+        has_down = self.z > 0
+        meet(
+            [(has_up, up), (has_down, down), (None, across), (None, beside)],
+            2 + has_up.astype(jnp.int32) + has_down.astype(jnp.int32),
+        )
+
+    def copy(self, part, block, way):
+        ref, first, rows = self.parts[part]
+        piece = ref.at[block, pl.ds(first, rows)]
+        return pltpu.make_async_remote_copy(
+            src_ref=piece,
+            dst_ref=piece,
+            send_sem=self.send_sem.at[part, way, block],
+            recv_sem=self.recv_sem.at[part, block],
+            device_id=self.targets()[way],
+            device_id_type=MESH_ID,
+        )
+
+    def send(self, part, block, way, present=None):
+        self.sent.append((part, block, way, present))
+        if present is None:
+            self.copy(part, block, way).start()
+        else:
+            pl.when(present)(lambda: self.copy(part, block, way).start())
+
+    def arrived(self, part, block):
+        self.copy(part, block, self.BESIDE).wait_recv()
+
+    def finish(self):
+        for part, block, way, present in self.sent:
+            if present is None:
+                self.copy(part, block, way).wait_send()
+            else:
+                pl.when(present)(
+                    lambda part=part, block=block, way=way: self.copy(part, block, way).wait_send()
+                )
+
+    def relay(self, part, z, x, ways, present):
+        block = z * 4 + x * 2 + self.c
+
+        def wait():
+            self.arrived(part, block)
+
+        if present is None:
+            wait()
+        else:
+            pl.when(present)(wait)
+        for way, also in ways:
+            both = present if also is None else (also if present is None else present & also)
+            self.send(part, block, way, both)
+
+    def own(self, across_first, line_parts):
+        z, x, c = self.z, self.x, self.c
+        mine = z * 4 + x * 2 + c
+        has_up, has_down = z < PLANES - 1, z > 0
+        for part in across_first:
+            self.send(part, mine, self.ACROSS)
+        for part in list(line_parts) + list(across_first):
+            self.send(part, mine, self.UP, has_up)
+            self.send(part, mine, self.DOWN, has_down)
+        for part in line_parts:
+            self.send(part, mine, self.ACROSS)
+        for part in list(across_first) + list(line_parts):
+            self.send(part, mine, self.BESIDE)
+
+    def first_round(self, across_first, line_parts):
+        z, x = self.z, self.x
+        has_up, has_down = z < PLANES - 1, z > 0
+        up, down, across, beside = (
+            (self.UP, has_up),
+            (self.DOWN, has_down),
+            (self.ACROSS, None),
+            (self.BESIDE, None),
+        )
+        for part in across_first:
+            self.relay(part, z, 1 - x, [up, down, beside], None)
+        for part in line_parts:
+            self.relay(part, z - 1, x, [up, across, beside], has_down)
+            self.relay(part, z + 1, x, [down, across, beside], has_up)
+        for part in across_first:
+            self.relay(part, z - 1, x, [up, beside], has_down)
+            self.relay(part, z + 1, x, [down, beside], has_up)
+        for part in line_parts:
+            self.relay(part, z, 1 - x, [beside], None)
+
+    def plane_done(self, z, parts, present=None):
+        def wait():
+            for x in range(2):
+                for part in parts:
+                    self.arrived(part, z * 4 + x * 2 + 1 - self.c)
+
+        if present is None:
+            wait()
+        else:
+            pl.when(present)(wait)
+
+    def second_round(self, across_first, line_parts):
+        z, x = self.z, self.x
+        has_up, has_down = z < PLANES - 1, z > 0
+        up, down, beside = (self.UP, has_up), (self.DOWN, has_down), (self.BESIDE, None)
+        for part in across_first:
+            self.relay(part, z - 1, 1 - x, [up, beside], has_down)
+            self.relay(part, z + 1, 1 - x, [down, beside], has_up)
+        for part in line_parts:
+            self.relay(part, z - 1, 1 - x, [beside], has_down)
+            self.relay(part, z + 1, 1 - x, [beside], has_up)
+
+    def far_plane(self):
+        return (self.z + 2) % PLANES
+
+    def third_round(self, across_first, line_parts):
+        far, x = self.far_plane(), self.x
+        across, beside = (self.ACROSS, None), (self.BESIDE, None)
+        for part in line_parts:
+            self.relay(part, far, x, [across, beside], None)
+        for part in across_first:
+            self.relay(part, far, x, [beside], None)
+            self.relay(part, far, 1 - x, [beside], None)
+        for part in line_parts:
+            self.relay(part, far, 1 - x, [beside], None)
+
+
+class VectorSum:
+    def __init__(self, ref, partial, arrived, send_sem, recv_sem):
+        self.ref, self.partial, self.arrived = ref, partial, arrived
+        self.send_sem, self.recv_sem = send_sem, recv_sem
+        self.y, self.z, self.x, self.c = where_am_i()
+        self.flying = []
+
+    def device(self, y, z, x, c):
+        return (y, z * 4 + x * 2 + c)
+
+    def copy(self, source, slot, device):
+        return pltpu.make_async_remote_copy(
+            src_ref=source,
+            dst_ref=self.arrived.at[slot],
+            send_sem=self.send_sem.at[slot],
+            recv_sem=self.recv_sem.at[slot],
+            device_id=device,
+            device_id_type=MESH_ID,
+        )
+
+    def start(self, stage):
+        y, z, x, c = self.y, self.z, self.x, self.c
+        source = self.ref if stage == 0 else self.partial.at[stage - 1]
+        if stage < 3:
+            device = (
+                self.device(y, z, x, 1 - c),
+                self.device(1 - y, z, x, c),
+                self.device(y, z, 1 - x, c),
+            )[stage]
+            copy = self.copy(source, stage, device)
+            copy.start()
+            self.flying.append(copy)
+        else:
+            for step in range(1, PLANES):
+                copy = self.copy(
+                    source, 2 + step, self.device(y, (z + step) % PLANES, x, c)
+                )
+                copy.start()
+                self.flying.append(copy)
+
+    def take(self, stage):
+        y, z, x, c = self.y, self.z, self.x, self.c
+        total = self.ref[...] if stage == 0 else self.partial[stage - 1]
+        for slot in (stage,) if stage < 3 else (3, 4, 5):
+            self.copy(self.ref, slot, self.device(y, z, x, 1 - c)).wait_recv()
+            total = total + self.arrived[slot]
+        self.partial[stage] = total
+
+    def finish(self):
+        for copy in self.flying:
+            copy.wait_send()
+
+    def own_share(self, rows, share):
+        width = self.ref.shape[1]
+        place = self.y * 16 + self.z * 4 + self.x * 2 + self.c
+        per_row = width // share
+        offset = place % per_row * share
+        row_index = lax.broadcasted_iota(jnp.int32, (width, 128), 0)
+        column_index = lax.broadcasted_iota(jnp.int32, (width, 128), 1)
+        picked = jnp.where(
+            (row_index == column_index + offset) & (column_index < share), 1.0, 0.0
+        ).astype(jnp.bfloat16)
+        rest = rows
+        total = jnp.zeros((rows.shape[0], 128), jnp.float32)
+        for _ in range(3):
+            piece = rest.astype(jnp.bfloat16)
+            total = total + product(piece, picked, CONTRACT_INNER)
+            rest = rest - piece.astype(jnp.float32)
+        return total, place // per_row
+
+
+STEP = 384
+
+
+class Shared:
+    def __init__(self, left, held, send_sem, recv_sem):
+        self.left, self.held = left, held
+        self.send_sem, self.recv_sem = send_sem, recv_sem
+        self.y, self.z, self.x, self.c = where_am_i()
+        self.quad = self.y * 2 + self.c
+        self.peer = (1 - self.y) * 2 + self.c
+        self.half = held.shape[2]
+        self.flying = []
+
+    def part(self, y):
+        return self.left.at[:, pl.ds(pl.multiple_of(y * self.half, 128), self.half)]
+
+    def fly(self, source, slot, which, device):
+        copy = pltpu.make_async_remote_copy(
+            src_ref=source,
+            dst_ref=self.held.at[slot],
+            send_sem=self.send_sem.at[which],
+            recv_sem=self.recv_sem.at[slot],
+            device_id=device,
+            device_id_type=MESH_ID,
+        )
+        copy.start()
+        self.flying.append(copy)
+
+    def beside(self):
+        return (self.y, self.z * 4 + self.x * 2 + 1 - self.c)
+
+    def share(self):
+        y, z, x, c = self.y, self.z, self.x, self.c
+        self.fly(self.part(1 - y), self.quad, 0, (1 - y, z * 4 + x * 2 + c))
+        self.fly(self.part(y), self.quad, 1, self.beside())
+        self.held[self.quad] = self.part(y)[...]
+
+    def landed(self, slot):
+        pltpu.make_async_remote_copy(
+            src_ref=self.held.at[slot],
+            dst_ref=self.held.at[slot],
+            send_sem=self.send_sem.at[0],
+            recv_sem=self.recv_sem.at[slot],
+            device_id=self.beside(),
+            device_id_type=MESH_ID,
+        ).wait_recv()
+
+    def relay(self):
+        self.landed(self.peer)
+        self.fly(self.held.at[self.peer], self.peer, 2, self.beside())
+
+    def complete(self):
+        self.landed(self.y * 2 + 1 - self.c)
+        self.landed((1 - self.y) * 2 + 1 - self.c)
+
+
+class Piece:
+    def __init__(self, shared, right, base, stride, out, buffers):
+        self.shared, self.right, self.base, self.stride, self.out = shared, right, base, stride, out
+        (
+            self.rights, self.whole, self.x_in, self.z_in, self.last,
+            self.send_sem, self.recv_sem, self.x_sem, self.z_send, self.z_recv, self.side_sem,
+        ) = buffers
+        self.y, self.z, self.x, self.c = where_am_i()
+        self.quad = self.y * 2 + self.c
+        self.flying = []
+
+    def device(self, y, z, x, c):
+        return (y, z * 4 + x * 2 + c)
+
+    def columns(self, c):
+        return pl.ds(pl.multiple_of(self.base + c * self.stride, 128), STEP)
+
+    def fly(self, source, target, send_sem, recv_sem, device):
+        copy = pltpu.make_async_remote_copy(
+            src_ref=source,
+            dst_ref=target,
+            send_sem=send_sem,
+            recv_sem=recv_sem,
+            device_id=device,
+            device_id_type=MESH_ID,
+        )
+        copy.start()
+        self.flying.append(copy)
+
+    def landed(self, ref, sem):
+        pltpu.make_async_remote_copy(
+            src_ref=ref,
+            dst_ref=ref,
+            send_sem=self.send_sem.at[0],
+            recv_sem=sem,
+            device_id=self.device(self.y, self.z, self.x, 1 - self.c),
+            device_id_type=MESH_ID,
+        ).wait_recv()
+
+    def share(self):
+        y, z, x, c, quad = self.y, self.z, self.x, self.c, self.quad
+        mine, other = self.right.at[:, self.columns(c)], self.right.at[:, self.columns(1 - c)]
+        target, arrival = self.rights.at[quad], self.recv_sem.at[quad]
+        self.fly(mine, target, self.send_sem.at[0], arrival, self.device(1 - y, z, x, c))
+        self.fly(other, target, self.send_sem.at[1], arrival, self.device(1 - y, z, x, 1 - c))
+        self.fly(other, target, self.send_sem.at[2], arrival, self.device(y, z, x, 1 - c))
+        self.rights[quad] = mine[...]
+
+    def multiply(self):
+        y, c = self.y, self.c
+        for other in (y * 2 + 1 - c, (1 - y) * 2 + c, (1 - y) * 2 + 1 - c):
+            self.landed(self.rights.at[other], self.recv_sem.at[other])
+        held = self.shared.held
+        tokens = held.shape[0] * held.shape[1]
+        planes, _, rows, _ = self.whole.shape
+        right = self.rights[...].reshape(tokens, STEP)
+        if self.shared.half > STEP:
+
+            def one(i, carry):
+                left = held[:, :, pl.ds(pl.multiple_of(i * STEP, 128), STEP)]
+                part = product(left.reshape(tokens, STEP), right, CONTRACT_FIRST)
+                self.whole[i] = part.astype(jnp.bfloat16).reshape(2, rows, STEP)
+                return carry
+
+            lax.fori_loop(0, self.shared.half // STEP, one, 0)
+        else:
+            part = product(held[...].reshape(tokens, STEP), right, CONTRACT_FIRST)
+            self.whole[...] = part.astype(jnp.bfloat16).reshape(planes, 2, rows, STEP)
+        self.fly(
+            self.whole.at[:, 1 - self.x], self.x_in, self.x_sem.at[0], self.x_sem.at[1],
+            self.device(self.y, self.z, 1 - self.x, self.c),
+        )
+
+    def spread(self):
+        self.landed(self.x_in, self.x_sem.at[1])
+        self.whole[:, self.x] = (
+            self.whole[:, self.x].astype(jnp.float32) + self.x_in[...].astype(jnp.float32)
+        ).astype(jnp.bfloat16)
+        for step in range(1, PLANES):
+            target = (self.z + step) % PLANES
+            self.fly(
+                self.whole.at[target, self.x], self.z_in.at[self.z], self.z_send.at[step],
+                self.z_recv.at[self.z], self.device(self.y, target, self.x, self.c),
+            )
+
+    def collect(self):
+        total = self.whole[self.z, self.x].astype(jnp.float32)
+        for step in range(1, PLANES):
+            source = (self.z + step) % PLANES
+            self.landed(self.z_in.at[source], self.z_recv.at[source])
+            total = total + self.z_in[source].astype(jnp.float32)
+        self.last[...] = total
+        rows = self.last.shape[0] // 2
+        self.fly(
+            self.last.at[pl.ds(pl.multiple_of((1 - self.c) * rows, 8), rows)],
+            self.out.at[:, self.columns(self.c)],
+            self.side_sem.at[0], self.side_sem.at[1],
+            self.device(self.y, self.z, self.x, 1 - self.c),
+        )
+        self.out[:, self.columns(self.c)] = self.last[
+            pl.ds(pl.multiple_of(self.c * rows, 8), rows), :
+        ]
+
+    def delivered(self):
+        self.landed(self.out.at[:, self.columns(1 - self.c)], self.side_sem.at[1])
+
+
+def shared_scratch(frame_count, left_width):
+    return [
+        pltpu.VMEM((4, frame_count, left_width // 2), jnp.bfloat16),
+        pltpu.SemaphoreType.DMA((3,)),
+        pltpu.SemaphoreType.DMA((4,)),
+    ]
+
+
+def piece_scratch(frame_count, left_width):
+    rows = left_width // 2 // (2 * PLANES)
+    low = jnp.bfloat16
+    return [
+        pltpu.VMEM((4, frame_count, STEP), low),
+        pltpu.VMEM((PLANES, 2, rows, STEP), low),
+        pltpu.VMEM((PLANES, rows, STEP), low),
+        pltpu.VMEM((PLANES, rows, STEP), low),
+        pltpu.VMEM((rows, STEP), jnp.float32),
+        pltpu.SemaphoreType.DMA((3,)),
+        pltpu.SemaphoreType.DMA((4,)),
+        pltpu.SemaphoreType.DMA((2,)),
+        pltpu.SemaphoreType.DMA((PLANES,)),
+        pltpu.SemaphoreType.DMA((PLANES,)),
+        pltpu.SemaphoreType.DMA((2,)),
+    ]
+
+
+def layer_scratch(frame_count, width, inner):
+    low, wide = jnp.bfloat16, jnp.float32
+    dma = pltpu.SemaphoreType.DMA
+    return dict(
+        qkv_held=pltpu.VMEM((width, 3 * width), low),
+        out_held=pltpu.VMEM((width, width), low),
+        up_held=pltpu.VMEM((width, inner), low),
+        down_held=pltpu.VMEM((inner, width), low),
+        weight_sem=dma((4,)),
+        block=pltpu.VMEM((BLOCKS, frame_count + 16, width), low),
+        block_send=dma((2, 4, BLOCKS)),
+        block_recv=dma((2, BLOCKS)),
+        grad_block=pltpu.VMEM((BLOCKS, frame_count, width), low),
+        stats=pltpu.VMEM((BLOCKS, 32, frame_count), wide),
+        grad_send=dma((3, 4, BLOCKS)),
+        grad_recv=dma((3, BLOCKS)),
+        projected=pltpu.VMEM((BLOCKS, frame_count, 3 * width), low),
+        mask=pltpu.VMEM((frame_count, BLOCKS * frame_count), wide),
+        attended=pltpu.VMEM((frame_count, width), wide),
+        slope=pltpu.VMEM((frame_count, inner), wide),
+        logs=pltpu.VMEM((frame_count, 128), wide),
+        delta=pltpu.VMEM((frame_count, 128), wide),
+        inner_bias=pltpu.VMEM((1, inner), wide),
+        act=pltpu.VMEM((frame_count, inner), low),
+        pre_low=pltpu.VMEM((frame_count, inner), low),
+        context=pltpu.VMEM((frame_count, width), low),
+        hidden_low=pltpu.VMEM((frame_count, width), low),
+        second_low=pltpu.VMEM((frame_count, width), low),
+        first_low=pltpu.VMEM((frame_count, width), low),
+        normed=pltpu.VMEM((frame_count, width), wide),
+        running=pltpu.VMEM((frame_count, width), wide),
+        first_grad=pltpu.VMEM((frame_count, width), wide),
+        proj_grad=pltpu.VMEM((frame_count, 3 * width), low),
+        vector=pltpu.VMEM((16, width), wide),
+        vector_partial=pltpu.VMEM((4, 16, width), wide),
+        vector_arrived=pltpu.VMEM((6, 16, width), wide),
+        vector_send=dma((6,)),
+        vector_recv=dma((6,)),
+        down_left=shared_scratch(frame_count, inner),
+        up_left=shared_scratch(frame_count, width),
+        out_left=shared_scratch(frame_count, width),
+        qkv_left=shared_scratch(frame_count, width),
+        down_piece=piece_scratch(frame_count, inner),
+        up_pieces=[piece_scratch(frame_count, width) for _ in range(4)],
+        out_piece=piece_scratch(frame_count, width),
+        qkv_pieces=[piece_scratch(frame_count, width) for _ in range(3)],
+    )
+
+
+class Inputs(typing.NamedTuple):
+    frames: typing.Any
+    segment_ids: typing.Any
+    qkv_weight: typing.Any
+    query_bias: typing.Any
+    value_bias: typing.Any
+    out_weight: typing.Any
+    out_bias: typing.Any
+    norm1_gain: typing.Any
+    norm1_shift: typing.Any
+    up_weight: typing.Any
+    up_bias: typing.Any
+    down_weight: typing.Any
+    down_bias: typing.Any
+    norm2_gain: typing.Any
+    norm2_shift: typing.Any
+    cotangent: typing.Any
+
+
+class Outputs(typing.NamedTuple):
+    layer_out: typing.Any
+    input_grad: typing.Any
+    qkv_g: typing.Any
+    query_g: typing.Any
+    value_g: typing.Any
+    out_g: typing.Any
+    outbias_g: typing.Any
+    gain1_g: typing.Any
+    shift1_g: typing.Any
+    up_g: typing.Any
+    upbias_g: typing.Any
+    down_g: typing.Any
+    downbias_g: typing.Any
+    gain2_g: typing.Any
+    shift2_g: typing.Any
+
+
+class Refs:
+    def __init__(self, *groups):
+        for group in groups:
+            for name, ref in group.items():
+                setattr(self, name, ref)
+
+
+def layer_kernel(held, *refs):
+    inputs, outputs = len(Inputs._fields), len(Outputs._fields)
+    scratch = jax.tree.unflatten(held, refs[inputs + outputs :])
+    k = Refs(dict(zip(Inputs._fields + Outputs._fields, refs)), scratch)
+    frame_count, width = k.frames.shape
+    inner = k.inner_bias.shape[1]
+    low, wide = jnp.bfloat16, jnp.float32
+    total = BLOCKS * frame_count
+    row, z, x, c = where_am_i()
+    mine = z * 4 + x * 2 + c
+    has_up, has_down = z < PLANES - 1, z > 0
+    edge = jnp.logical_not(has_up & has_down)
+    far = (z + 2) % PLANES
+    lost = PLANES - 1 - z
+    lane = lax.broadcasted_iota(jnp.int32, (frame_count, 128), 1)
+
+    def fetch(i):
+        source, target = (
+            (k.qkv_weight, k.qkv_held),
+            (k.out_weight, k.out_held),
+            (k.up_weight, k.up_held),
+            (k.down_weight, k.down_held),
+        )[i]
+        return pltpu.make_async_copy(source, target, k.weight_sem.at[i])
+
+    for i in range(4):
+        fetch(i).start()
+
+    link = RowGather(
+        [(k.block, 0, 64), (k.block, 64, frame_count - 48)], k.block_send, k.block_recv
+    )
+    back = RowGather(
+        [(k.grad_block, 0, 64), (k.grad_block, 64, frame_count - 64), (k.stats, 0, 32)],
+        k.grad_send,
+        k.grad_recv,
+    )
+    down_left = Shared(k.act, *k.down_left)
+    up_left = Shared(k.hidden_low, *k.up_left)
+    out_left = Shared(k.context, *k.out_left)
+    qkv_left = Shared(k.frames, *k.qkv_left)
+    half_inner, half_width = inner // 2, width // 2
+    down = Piece(down_left, k.second_low, 0, half_width, k.down_g, k.down_piece)
+    ups = [
+        Piece(up_left, k.pre_low, p * STEP, half_inner, k.up_g, k.up_pieces[p])
+        for p in range(4)
+    ]
+    out = Piece(out_left, k.first_low, 0, half_width, k.out_g, k.out_piece)
+    qkvs = [
+        Piece(qkv_left, k.proj_grad, p * width, half_width, k.qkv_g, k.qkv_pieces[p])
+        for p in range(3)
+    ]
+    vector = VectorSum(
+        k.vector, k.vector_partial, k.vector_arrived, k.vector_send, k.vector_recv
+    )
+
+    partners = [
+        (None, down.device(row, z, x, 1 - c)),
+        (None, down.device(1 - row, z, x, c)),
+        (None, down.device(1 - row, z, x, 1 - c)),
+        (None, down.device(row, z, 1 - x, c)),
+    ]
+    partners += [(None, down.device(row, (z + step) % PLANES, x, c)) for step in range(1, PLANES)]
+    meet(partners, len(partners))
+
+    line, crossing = (0,), (1,)
+    k.block[mine, pl.ds(0, frame_count), :] = k.frames[...]
+    own_ids = jnp.broadcast_to(k.segment_ids[...], (frame_count, frame_count)).astype(wide)
+    k.block[mine, pl.ds(frame_count, 16), pl.ds(0, frame_count)] = own_ids[:16].astype(low)
+    link.own(crossing, line)
+    qkv_left.share()
+    ids_column = own_ids.T
+    k.inner_bias[...] = k.up_bias[...].reshape(1, inner)
+    query_bias = k.query_bias[...].reshape(1, width)
+    value_bias = k.value_bias[...].reshape(1, width)
+
+    def plane_rows(plane):
+        return jnp.concatenate(
+            [k.block[plane * 4 + i, pl.ds(0, frame_count), :] for i in range(4)], axis=0
+        )
+
+    def store_rows(plane, third, part):
+        for i in range(4):
+            k.projected[plane * 4 + i, :, pl.ds(third * width, width)] = part[
+                i * frame_count : (i + 1) * frame_count
+            ]
+
+    def as_query(part):
+        return (part + query_bias).astype(low) * HEAD_DIM**-0.5
+
+    def project(plane):
+        rows = plane_rows(plane)
+        keys = product(rows, k.qkv_held[:, pl.ds(width, width)], CONTRACT_INNER)
+        store_rows(plane, 1, keys.astype(low))
+        values = product(rows, k.qkv_held[:, pl.ds(2 * width, width)], CONTRACT_INNER)
+        store_rows(plane, 2, (values + value_bias).astype(low))
+        for i in range(4):
+            ids = k.block[plane * 4 + i, pl.ds(frame_count, 8), pl.ds(0, frame_count)]
+            same = jnp.broadcast_to(ids.astype(wide)[:1], own_ids.shape) == ids_column
+            at = pl.multiple_of((plane * 4 + i) * frame_count, 128)
+            k.mask[:, pl.ds(at, frame_count)] = jnp.where(same, 0.0, mask_fill)
+
+    def project_queries(plane):
+        queries = product(plane_rows(plane), k.qkv_held[:, pl.ds(0, width)], CONTRACT_INNER)
+        store_rows(plane, 0, as_query(queries))
+
+    def columns_of(third, j):
+        return pl.ds(pl.multiple_of(third * width + j * 128, 128), 128)
+
+    def head_state(h):
+        return pl.ds(pl.multiple_of(h * 128, 128), 128)
+
+    def attend(plane, first):
+        at = pl.multiple_of(plane * 4 * frame_count, 128)
+
+        def pair(j, carry):
+            query = k.projected[mine, :, columns_of(0, j)]
+            keys = k.projected[pl.ds(plane * 4, 4), :, columns_of(1, j)].reshape(-1, 128)
+            values = k.projected[pl.ds(plane * 4, 4), :, columns_of(2, j)].reshape(-1, 128)
+            outs, factors = [], []
+            for h in range(2):
+                chosen = (lane < HALF) == (h == 0)
+                scores = product(
+                    jnp.where(chosen, query, jnp.zeros_like(query)), keys, CONTRACT_LAST
+                )
+                scores = scores + k.mask[:, pl.ds(at, 4 * frame_count)]
+                peak = jnp.broadcast_to(jnp.max(scores, axis=1, keepdims=True), lane.shape)
+                if not first:
+                    old = k.slope[:, head_state(2 * j + h)]
+                    peak = jnp.maximum(peak, old)
+                    factors.append(jnp.exp(old - peak))
+                weights = jnp.exp(scores - jnp.concatenate([peak] * 4, axis=1))
+                whole = jnp.broadcast_to(jnp.sum(weights, axis=1, keepdims=True), lane.shape)
+                if not first:
+                    whole = whole + k.slope[:, head_state(HEADS + 2 * j + h)] * factors[h]
+                k.slope[:, head_state(2 * j + h)] = peak
+                k.slope[:, head_state(HEADS + 2 * j + h)] = whole
+                outs.append(product(weights.astype(low), values, CONTRACT_INNER))
+            both = jnp.where(lane < HALF, outs[0], outs[1])
+            if not first:
+                both = both + k.attended[:, columns_of(0, j)] * jnp.where(
+                    lane < HALF, factors[0], factors[1]
+                )
+            k.attended[:, columns_of(0, j)] = both
+            return carry
+
+        lax.fori_loop(0, PAIRS, pair, 0)
+
+    fetch(0).wait()
+    own_query = product(k.frames[...], k.qkv_held[:, pl.ds(0, width)], CONTRACT_INNER)
+    k.projected[mine, :, pl.ds(0, width)] = as_query(own_query)
+    link.first_round(crossing, line)
+    link.plane_done(z, (0, 1))
+    project(z)
+    link.second_round(crossing, line)
+    attend(z, True)
+
+    @pl.when(has_down)
+    def _():
+        link.plane_done(z - 1, (0, 1))
+        project(z - 1)
+
+    link.third_round(crossing, line)
+
+    @pl.when(has_down)
+    def _():
+        attend(z - 1, False)
+
+    @pl.when(has_up)
+    def _():
+        link.plane_done(z + 1, (0, 1))
+        project(z + 1)
+        attend(z + 1, False)
+
+    link.plane_done(far, (0, 1))
+    project(far)
+    attend(far, False)
+    logs = jnp.zeros(lane.shape, wide)
+    for j in range(PAIRS):
+        parts = []
+        for h in range(2):
+            whole = k.slope[:, head_state(HEADS + 2 * j + h)]
+            logs = jnp.where(
+                lane == 2 * j + h, k.slope[:, head_state(2 * j + h)] + jnp.log(whole), logs
+            )
+            parts.append(whole)
+        done = k.attended[:, columns_of(0, j)] / jnp.where(lane < HALF, parts[0], parts[1])
+        k.attended[:, columns_of(0, j)] = done
+        k.context[:, columns_of(0, j)] = done.astype(low)
+    k.logs[...] = logs
+    out_left.share()
+
+    def normalize(resid):
+        centred = resid - jnp.mean(resid, axis=-1, keepdims=True)
+        inverse = lax.rsqrt(jnp.mean(centred * centred, axis=-1, keepdims=True) + norm_eps)
+        return centred * inverse, inverse
+
+    def normalize_back(upstream, normed, inverse, gain):
+        scaled = upstream * gain
+        first_mean = jnp.mean(scaled, axis=-1, keepdims=True)
+        second_mean = jnp.mean(scaled * normed, axis=-1, keepdims=True)
+        return inverse * (scaled - first_mean - normed * second_mean)
+
+    def note(index, values):
+        k.vector[pl.ds(index, 1), :] = jnp.sum(values, axis=0, keepdims=True)
+
+    def flat(ref):
+        return ref[...].reshape(1, width)
+
+    k.vector[pl.ds(8, 8), :] = jnp.zeros((8, width), wide)
+    fetch(1).wait()
+    resid_one = (
+        k.frames[...].astype(wide)
+        + product(k.context[...], k.out_held[...], CONTRACT_INNER)
+        + flat(k.out_bias)
+    )
+    normed_one, inverse_one = normalize(resid_one)
+    k.normed[...] = normed_one
+    hidden = normed_one * flat(k.norm1_gain) + flat(k.norm1_shift)
+    k.hidden_low[...] = hidden.astype(low)
+    up_left.share()
+    k.running[...] = hidden + flat(k.down_bias)
+    fetch(2).wait()
+    fetch(3).wait()
+
+    def forward(f, carry):
+        columns = pl.ds(pl.multiple_of(f * width, 128), width)
+        pre_act = (
+            product(k.hidden_low[...], k.up_held[:, columns], CONTRACT_INNER)
+            + k.inner_bias[:, columns]
+        )
+        normal_cdf = 0.5 * (1.0 + lax.erf(pre_act * 0.5**0.5))
+        normal_pdf = jnp.exp(-0.5 * pre_act * pre_act) * (2.0 * math.pi) ** (-0.5)
+        act = (pre_act * normal_cdf).astype(low)
+        k.act[:, columns] = act
+        k.slope[:, columns] = normal_cdf + pre_act * normal_pdf
+        k.running[...] += product(
+            act, k.down_held[pl.ds(pl.multiple_of(f * width, 128), width), :], CONTRACT_INNER
+        )
+        return carry
+
+    lax.fori_loop(0, inner // width, forward, 0)
+    down_left.share()
+    normed_two, inverse_two = normalize(k.running[...])
+    k.layer_out[...] = (normed_two * flat(k.norm2_gain) + flat(k.norm2_shift)).astype(low)
+    upstream = k.cotangent[...].astype(wide)
+    second_grad = normalize_back(upstream, normed_two, inverse_two, flat(k.norm2_gain))
+    k.second_low[...] = second_grad.astype(low)
+    down.share()
+    note(5, second_grad)
+    note(6, upstream * normed_two)
+    note(7, upstream)
+    k.running[...] = second_grad
+    for p in range(4):
+        for side in range(2):
+            first = side * half_inner + p * STEP
+            columns = pl.ds(first, STEP)
+            pre_grad = (
+                product(k.second_low[...], k.down_held[columns, :], CONTRACT_LAST)
+                * k.slope[:, columns]
+            )
+            k.vector[pl.ds(8 + first // width, 1), pl.ds(first % width, STEP)] = jnp.sum(
+                pre_grad, axis=0, keepdims=True
+            )
+            k.pre_low[:, columns] = pre_grad.astype(low)
+            k.running[...] += product(
+                k.pre_low[:, columns], k.up_held[:, columns], CONTRACT_LAST
+            )
+        ups[p].share()
+        if p == 1:
+            out_left.relay()
+            up_left.relay()
+            qkv_left.relay()
+    hidden_grad = k.running[...]
+    normed_one = k.normed[...]
+    first_grad = normalize_back(hidden_grad, normed_one, inverse_one, flat(k.norm1_gain))
+    k.first_grad[...] = first_grad
+    k.first_low[...] = first_grad.astype(low)
+    out.share()
+    context_grad = product(k.first_low[...], k.out_held[...], CONTRACT_LAST).astype(low)
+    k.grad_block[mine] = context_grad
+    delta = jnp.zeros(lane.shape, wide)
+    for j in range(PAIRS):
+        columns = slice(j * 128, (j + 1) * 128)
+        both = context_grad[:, columns].astype(wide) * k.attended[:, columns]
+        for h in range(2):
+            one = jnp.sum(
+                jnp.where((lane < HALF) == (h == 0), both, 0.0), axis=1, keepdims=True
+            )
+            delta = jnp.where(lane == 2 * j + h, one, delta)
+    k.delta[...] = delta
+    k.stats[mine, pl.ds(0, 16), :] = k.logs[...].T[:16]
+    k.stats[mine, pl.ds(16, 16), :] = delta.T[:16]
+    back_line, back_crossing = (2, 0), (1,)
+    back.own(back_crossing, back_line)
+    note(2, first_grad)
+    note(3, hidden_grad * normed_one)
+    note(4, hidden_grad)
+
+    @pl.when(edge)
+    def _():
+        for i in range(4):
+            k.projected[lost * 4 + i] = jnp.zeros((frame_count, 3 * width), low)
+            k.grad_block[lost * 4 + i] = jnp.zeros((frame_count, width), low)
+            k.stats[lost * 4 + i] = jnp.zeros((32, frame_count), wide)
+            at = pl.multiple_of((lost * 4 + i) * frame_count, 128)
+            k.mask[:, pl.ds(at, frame_count)] = jnp.full(lane.shape, mask_fill, wide)
+
+    def query_pair(j):
+        query = k.projected[mine, :, columns_of(0, j)]
+        upstream = k.grad_block[mine, :, columns_of(0, j)]
+        keys = k.projected[:, :, columns_of(1, j)].reshape(total, 128)
+        values = k.projected[:, :, columns_of(2, j)].reshape(total, 128)
+        outs = []
+        for h in range(2):
+            chosen = (lane < HALF) == (h == 0)
+            nothing = jnp.zeros_like(query)
+            logs = jnp.sum(
+                jnp.where(lane == 2 * j + h, k.logs[...], 0.0), axis=1, keepdims=True
+            )
+            shift = jnp.sum(
+                jnp.where(lane == 2 * j + h, k.delta[...], 0.0), axis=1, keepdims=True
+            )
+            scores = product(jnp.where(chosen, query, nothing), keys, CONTRACT_LAST)
+            probs = jnp.exp(scores + k.mask[...] - logs)
+            prob_grad = product(jnp.where(chosen, upstream, nothing), values, CONTRACT_LAST)
+            score_grad = (probs * (prob_grad - shift)).astype(low)
+            outs.append(product(score_grad, keys, CONTRACT_INNER))
+        k.proj_grad[:, columns_of(0, j)] = (
+            jnp.where(lane < HALF, outs[0], outs[1]) * HEAD_DIM**-0.5
+        ).astype(low)
+
+    def key_pair(j):
+        key = k.projected[mine, :, columns_of(1, j)]
+        value = k.projected[mine, :, columns_of(2, j)]
+        queries = k.projected[:, :, columns_of(0, j)].reshape(total, 128)
+        upstream = k.grad_block[:, :, columns_of(0, j)].reshape(total, 128)
+        key_outs, value_outs = [], []
+        for h in range(2):
+            chosen = (lane < HALF) == (h == 0)
+            nothing = jnp.zeros_like(key)
+            logs = jnp.concatenate(
+                [k.stats[b, pl.ds(2 * j + h, 1), :] for b in range(BLOCKS)], axis=1
+            )
+            shift = jnp.concatenate(
+                [k.stats[b, pl.ds(16 + 2 * j + h, 1), :] for b in range(BLOCKS)], axis=1
+            )
+            scores = product(jnp.where(chosen, key, nothing), queries, CONTRACT_LAST)
+            probs = jnp.exp(scores + k.mask[...] - logs)
+            prob_grad = product(jnp.where(chosen, value, nothing), upstream, CONTRACT_LAST)
+            score_grad = (probs * (prob_grad - shift)).astype(low)
+            key_outs.append(product(score_grad, queries, CONTRACT_INNER))
+            value_outs.append(product(probs.astype(low), upstream, CONTRACT_INNER))
+        k.proj_grad[:, columns_of(1, j)] = jnp.where(
+            lane < HALF, key_outs[0], key_outs[1]
+        ).astype(low)
+        k.proj_grad[:, columns_of(2, j)] = jnp.where(
+            lane < HALF, value_outs[0], value_outs[1]
+        ).astype(low)
+
+    def pairs(one, first, last):
+        def body(j, carry):
+            one(j)
+            return carry
+
+        lax.fori_loop(first, last, body, 0)
+
+    pairs(query_pair, 0, 2)
+    back.first_round(back_crossing, back_line)
+    down_left.relay()
+    pairs(query_pair, 2, 4)
+    back.second_round(back_crossing, back_line)
+    pairs(query_pair, 4, 6)
+    back.third_round(back_crossing, back_line)
+    qkvs[0].share()
+    down_left.complete()
+    down.multiply()
+    up_left.complete()
+    project_queries(z)
+    project_queries(far)
+    ups[0].multiply()
+
+    @pl.when(has_down)
+    def _():
+        project_queries(z - 1)
+
+    @pl.when(has_up)
+    def _():
+        project_queries(z + 1)
+
+    back.plane_done(z, (0, 1, 2))
+    back.plane_done(z - 1, (0, 1, 2), has_down)
+    back.plane_done(z + 1, (0, 1, 2), has_up)
+    back.plane_done(far, (0, 1, 2))
+    pairs(key_pair, 0, 2)
+    ups[1].multiply()
+    down.spread()
+    pairs(key_pair, 2, 4)
+    ups[2].multiply()
+    ups[0].spread()
+    pairs(key_pair, 4, 6)
+    qkvs[1].share()
+    qkvs[2].share()
+    note(0, k.proj_grad[:, pl.ds(0, width)].astype(wide))
+    note(1, k.proj_grad[:, pl.ds(2 * width, width)].astype(wide))
+    vector.start(0)
+    ups[3].multiply()
+    down.collect()
+    ups[1].spread()
+    k.input_grad[...] = k.first_grad[...] + product(
+        k.proj_grad[...], k.qkv_held[...], CONTRACT_LAST
+    )
+    vector.take(0)
+    vector.start(1)
+    out_left.complete()
+    out.multiply()
+    ups[2].spread()
+    qkv_left.complete()
+    qkvs[0].multiply()
+    ups[0].collect()
+    ups[3].spread()
+    vector.take(1)
+    vector.start(2)
+    qkvs[1].multiply()
+    ups[1].collect()
+    out.spread()
+    qkvs[2].multiply()
+    ups[2].collect()
+    qkvs[0].spread()
+    vector.take(2)
+    vector.start(3)
+    ups[3].collect()
+    qkvs[1].spread()
+    out.collect()
+    qkvs[2].spread()
+    vector.take(3)
+    summed = k.vector_partial[3]
+    share = k.query_g.shape[0]
+    shares, _ = vector.own_share(summed[:8], share)
+    for i, ref in enumerate(
+        (k.query_g, k.value_g, k.outbias_g, k.gain1_g, k.shift1_g, k.downbias_g, k.gain2_g, k.shift2_g)
+    ):
+        ref[...] = shares[i, :share]
+    up_shares, at = vector.own_share(summed[8:], 4 * share)
+    keep = lax.broadcasted_iota(jnp.int32, up_shares.shape, 0) == at
+    picked = jnp.sum(jnp.where(keep, up_shares, 0.0), axis=0, keepdims=True)
+    k.upbias_g[...] = picked[0, : 4 * share]
+    qkvs[0].collect()
+    qkvs[1].collect()
+    qkvs[2].collect()
+    pieces = [down] + ups + [out] + qkvs
+    for each in pieces:
+        each.delivered()
+    link.finish()
+    back.finish()
+    for each in [down_left, up_left, out_left, qkv_left] + pieces:
+        for copy in each.flying:
+            copy.wait_send()
+    vector.finish()
+
+
+def layer_step(*args):
+    frames = args[0]
+    frame_count, width = frames.shape[1:]
+    inner = args[9].shape[1]
+    low, wide = jnp.bfloat16, jnp.float32
+    scratch, held = jax.tree.flatten(layer_scratch(frame_count, width, inner))
+    operands = [frames[0]] + list(args[1:-1]) + [args[-1][0]]
+    share = width // 32
+    shapes = [
+        ((frame_count, width), low),
+        ((frame_count, width), wide),
+        ((share, 3 * width), wide),
+        ((share,), wide),
+        ((share,), wide),
+        ((share, width), wide),
+        ((share,), wide),
+        ((share,), wide),
+        ((share,), wide),
+        ((share, inner), wide),
+        ((4 * share,), wide),
+        ((4 * share, width), wide),
+        ((share,), wide),
+        ((share,), wide),
+        ((share,), wide),
+    ]
+    results = pl.pallas_call(
+        functools.partial(layer_kernel, held),
+        out_shape=tuple(jax.ShapeDtypeStruct(shape, kind) for shape, kind in shapes),
+        in_specs=[IN_PLACE if each.ndim == 2 and each.shape[0] >= width else IN_VMEM for each in operands],
+        out_specs=(IN_VMEM,) * len(shapes),
+        scratch_shapes=scratch,
+        compiler_params=pltpu.CompilerParams(
+            collective_id=0, has_side_effects=True, vmem_limit_bytes=VMEM_BYTES
+        ),
+    )(*operands)
+    return (results[0][None], results[1][None]) + tuple(results[2:])
+
+
 def solution(mesh):
+    chosen = layer_step if dict(mesh.shape) == {"rows": 2, "seq": 16} else shards
     in_specs = (
         P("rows", "seq", None),
         P("rows", "seq"),
@@ -395,4 +1434,4 @@
         P(("rows", "seq")),
         P(("rows", "seq")),
     )
-    return jax.shard_map(shards, mesh=mesh, in_specs=in_specs, out_specs=out_specs, check_vma=False)
+    return jax.shard_map(chosen, mesh=mesh, in_specs=in_specs, out_specs=out_specs, check_vma=False)

time: 1070 us -> 152 us (0.14)
  waiting for transfers between devices: 517 us -> 0 us
  matrix products: 195 us -> 0 us
  local copies, waits for them, and re-layouts: 183 us -> 20.2 us
  Pallas kernels: 0 us -> 131 us
  other arithmetic: 93.2 us -> 0 us
  blocking collectives: 63.1 us -> 0 us
  between operations: 14.1 us -> 0.67 us
    reduce_scatter x3 -> x0, waiting for transfers between devices: 283 us -> none  [the longest x1 142 us: shards(): lax.psum_scatter(down_grad, ('rows', 'seq'), scatter_dimension=0, tiled=T...]
    dot_general x124 -> x0, matrix products: 195 us -> none  [the longest x32 44.9 us: block_scores(): jnp.einsum('qhe,khe->hqk', query_part, key_part, preferred_element_type=j...]
    ppermute x94 -> x0, waiting for transfers between devices: 183 us -> none  [passed_along(): return lax.ppermute(value, axis, pairs)]
    pallas_call x0 -> x1, Pallas kernels: none -> 131 us  [layer_step(): pl.pallas_call(functools.partial(layer_kernel, held), out_shape=tuple((ja...]
    while x329 -> x0, local copies, waits for them, and re-layouts: 124 us -> none
    convert_element_type x35 -> x0, other arithmetic: 57.5 us -> none  [the longest x16 27.3 us: pass_grads(): passed_along(blocks[0].astype(jnp.bfloat16), 'seq', 1).astype(jnp.float32)]
    unnamed x5 -> x0, waiting for transfers between devices: 51 us -> none
    unnamed x1 -> x0, blocking collectives: 39.4 us -> none
  transfers between devices with their start and end apart: 98 -> 0, of which waited for: 50 -> 0; matrix products, arithmetic and copies ran while one was open for 34% -> 0% of each run, Pallas kernels for 0% -> 0%
where the time goes in v2:
time: 152 us
  Pallas kernels  131 us (86%)
  local copies, waits for them, and re-layouts  20.2 us (13%)
    pallas_call x1, Pallas kernels, layer_step(): pl.pallas_call(functools.partial(layer_kernel, held), out_shape=tuple((ja...  131 us
    unnamed x15, local copies, waits for them, and re-layouts  20.2 us

profile of v2, /device:TPU:0, one launch (start us, length us, event | category | flops | bytes accessed | tf_op | source)
XLA Modules:
  0.0 151.6 jit_solution(6338571621676523840)
XLA Ops:
  0.7 130.7 %shard_map.271 = (bf16[128,768]{1,0:T(8,128)(2,1)}, f32[128,768]{1,0:T(8,128)}, f32[24,2304]{1,0:T(8,128)}, f32[24]{0:T(128)}, f32[24]{0:T(128)}, /*index=5*/f32...) custom-call(bf16[128,768]{1,0:T(8,128)(2,1)} %bitcast.5, ...), custom_call_target="tpu_custom_call" | custom-call | tf_op jit(solution)/shard_map/pallas_call | solution.py:1387
  131.4 1.6 %copy.46 = bf16[1,128,768]{2,1,0:T(8,128)(2,1)} copy(bf16[1,128,768]{2,1,0:T(8,128)(2,1)} %bitcast.7) | data formatting | bytes 393216
  133.0 1.8 %copy.47 = f32[1,128,768]{2,1,0:T(8,128)} copy(f32[1,128,768]{2,1,0:T(8,128)} %bitcast.4) | data formatting | bytes 786432
  134.8 1.6 %copy.48 = f32[24,2304]{1,0:T(8,128)} copy(f32[24,2304]{1,0:T(8,128)} %get-tuple-element.62) | data formatting | bytes 442368
  136.4 1.2 copy.49
  137.6 1.1 copy.50
  138.7 1.5 %copy.51 = f32[24,768]{1,0:T(8,128)} copy(f32[24,768]{1,0:T(8,128)} %get-tuple-element.65) | data formatting | bytes 147456
  140.2 1.1 copy.52
  141.4 1.1 copy.53
  142.5 1.1 copy.54
  143.6 1.7 %copy.55 = f32[24,3072]{1,0:T(8,128)} copy(f32[24,3072]{1,0:T(8,128)} %get-tuple-element.69) | data formatting | bytes 589824
  145.3 1.2 copy.56
  146.5 1.7 %copy.57 = f32[96,768]{1,0:T(8,128)} copy(f32[96,768]{1,0:T(8,128)} %get-tuple-element.71) | data formatting | bytes 589824
  148.2 1.1 copy.58
  149.3 1.2 copy.59
  150.5 1.1 copy.60

commit v3 on v2

--- a/solution.py
+++ b/solution.py
@@ -403,147 +403,160 @@
 class RowGather:
     UP, DOWN, ACROSS, BESIDE = range(4)
 
-    def __init__(self, parts, send_sem, recv_sem):
-        self.parts = parts
-        self.send_sem = send_sem
-        self.recv_sem = recv_sem
+    def __init__(self, parts, line, crossing, sems):
+        self.parts, self.line, self.crossing = parts, line, crossing
+        self.recv_sem, self.beside_sem, self.line_sem, self.out_sem = sems
         self.row, self.z, self.x, self.c = where_am_i()
-        self.sent = []
+        self.has_up, self.has_down = self.z < PLANES - 1, self.z > 0
+        self.far = (self.z + 2) % PLANES
+        self.buffers = []
+        for ref, _, _ in parts:
+            if not any(ref is known for known in self.buffers):
+                self.buffers.append(ref)
+
+    def group(self, part):
+        return [self.parts[part][0] is ref for ref in self.buffers].index(True)
 
     def device(self, z, x, c):
         return (self.row, z * 4 + x * 2 + c)
 
-    def targets(self):
+    def target(self, way):
         return (
             self.device(self.z + 1, self.x, self.c),
             self.device(self.z - 1, self.x, self.c),
             self.device(self.z, 1 - self.x, self.c),
             self.device(self.z, self.x, 1 - self.c),
-        )
-
-    def meet(self):
-        up, down, across, beside = self.targets()
-        has_up = self.z < PLANES - 1
-        has_down = self.z > 0
-        meet(
-            [(has_up, up), (has_down, down), (None, across), (None, beside)],
-            2 + has_up.astype(jnp.int32) + has_down.astype(jnp.int32),
-        )
-
-    def copy(self, part, block, way):
+        )[way]
+
+    def copy(self, part, z, x, way):
         ref, first, rows = self.parts[part]
-        piece = ref.at[block, pl.ds(first, rows)]
+        piece = ref.at[z * 4 + x * 2 + self.c, pl.ds(first, rows)]
+        beside = way == self.BESIDE
         return pltpu.make_async_remote_copy(
             src_ref=piece,
             dst_ref=piece,
-            send_sem=self.send_sem.at[part, way, block],
-            recv_sem=self.recv_sem.at[part, block],
-            device_id=self.targets()[way],
+            send_sem=self.out_sem.at[self.group(part)] if beside else self.line_sem.at[part, way],
+            recv_sem=(
+                self.beside_sem.at[self.group(part), z]
+                if beside
+                else self.recv_sem.at[part, z * 2 + x]
+            ),
+            device_id=self.target(way),
             device_id_type=MESH_ID,
         )
 
-    def send(self, part, block, way, present=None):
-        self.sent.append((part, block, way, present))
+    def send(self, part, z, x, way):
+        present = {self.UP: self.has_up, self.DOWN: self.has_down}.get(way)
         if present is None:
-            self.copy(part, block, way).start()
+            self.copy(part, z, x, way).start()
         else:
-            pl.when(present)(lambda: self.copy(part, block, way).start())
-
-    def arrived(self, part, block):
-        self.copy(part, block, self.BESIDE).wait_recv()
-
-    def finish(self):
-        for part, block, way, present in self.sent:
-            if present is None:
-                self.copy(part, block, way).wait_send()
-            else:
-                pl.when(present)(
-                    lambda part=part, block=block, way=way: self.copy(part, block, way).wait_send()
-                )
-
-    def relay(self, part, z, x, ways, present):
-        block = z * 4 + x * 2 + self.c
-
+            pl.when(present)(lambda: self.copy(part, z, x, way).start())
+
+    def relay(self, part, z, x, ways, present=None):
+        def both():
+            self.copy(part, z, x, self.ACROSS).wait_recv()
+            for way in ways:
+                self.send(part, z, x, way)
+
+        if present is None:
+            both()
+        else:
+            pl.when(present)(both)
+
+    def own(self):
+        z, x = self.z, self.x
+        for part in self.crossing:
+            self.send(part, z, x, self.ACROSS)
+        for part in self.line + self.crossing:
+            self.send(part, z, x, self.UP)
+            self.send(part, z, x, self.DOWN)
+        for part in self.line:
+            self.send(part, z, x, self.ACROSS)
+        for part in self.crossing + self.line:
+            self.send(part, z, x, self.BESIDE)
+
+    def near_first(self):
+        z, x = self.z, self.x
+        for part in self.line:
+            self.relay(part, z - 1, x, (self.UP, self.ACROSS, self.BESIDE), self.has_down)
+            self.relay(part, z + 1, x, (self.DOWN, self.ACROSS, self.BESIDE), self.has_up)
+        for part in self.crossing:
+            self.relay(part, z, 1 - x, (self.UP, self.DOWN, self.BESIDE))
+        for part in self.crossing:
+            self.relay(part, z - 1, x, (self.UP, self.BESIDE), self.has_down)
+            self.relay(part, z + 1, x, (self.DOWN, self.BESIDE), self.has_up)
+        for part in self.line:
+            self.relay(part, z, 1 - x, (self.BESIDE,))
+
+    def near_second(self):
+        z, x = self.z, self.x
+        for part in self.crossing:
+            self.relay(part, z - 1, 1 - x, (self.UP, self.BESIDE), self.has_down)
+            self.relay(part, z + 1, 1 - x, (self.DOWN, self.BESIDE), self.has_up)
+        for part in self.line:
+            self.relay(part, z - 1, 1 - x, (self.BESIDE,), self.has_down)
+            self.relay(part, z + 1, 1 - x, (self.BESIDE,), self.has_up)
+
+    def far_line(self):
+        for part in self.line:
+            self.relay(part, self.far, self.x, (self.ACROSS, self.BESIDE))
+
+    def far_rest(self):
+        for part in self.crossing:
+            self.relay(part, self.far, self.x, (self.BESIDE,))
+        for part in self.line:
+            self.relay(part, self.far, 1 - self.x, (self.BESIDE,))
+        for part in self.crossing:
+            self.relay(part, self.far, 1 - self.x, (self.BESIDE,))
+
+    def plane_done(self, z, present=None):
         def wait():
-            self.arrived(part, block)
+            for i, ref in enumerate(self.buffers):
+                both = ref.at[pl.ds(0, 2)]
+                pltpu.make_async_remote_copy(
+                    src_ref=both,
+                    dst_ref=both,
+                    send_sem=self.out_sem.at[i],
+                    recv_sem=self.beside_sem.at[i, z],
+                    device_id=self.target(self.BESIDE),
+                    device_id_type=MESH_ID,
+                ).wait_recv()
 
         if present is None:
             wait()
         else:
             pl.when(present)(wait)
-        for way, also in ways:
-            both = present if also is None else (also if present is None else present & also)
-            self.send(part, block, way, both)
-
-    def own(self, across_first, line_parts):
-        z, x, c = self.z, self.x, self.c
-        mine = z * 4 + x * 2 + c
-        has_up, has_down = z < PLANES - 1, z > 0
-        for part in across_first:
-            self.send(part, mine, self.ACROSS)
-        for part in list(line_parts) + list(across_first):
-            self.send(part, mine, self.UP, has_up)
-            self.send(part, mine, self.DOWN, has_down)
-        for part in line_parts:
-            self.send(part, mine, self.ACROSS)
-        for part in list(across_first) + list(line_parts):
-            self.send(part, mine, self.BESIDE)
-
-    def first_round(self, across_first, line_parts):
-        z, x = self.z, self.x
-        has_up, has_down = z < PLANES - 1, z > 0
-        up, down, across, beside = (
-            (self.UP, has_up),
-            (self.DOWN, has_down),
-            (self.ACROSS, None),
-            (self.BESIDE, None),
-        )
-        for part in across_first:
-            self.relay(part, z, 1 - x, [up, down, beside], None)
-        for part in line_parts:
-            self.relay(part, z - 1, x, [up, across, beside], has_down)
-            self.relay(part, z + 1, x, [down, across, beside], has_up)
-        for part in across_first:
-            self.relay(part, z - 1, x, [up, beside], has_down)
-            self.relay(part, z + 1, x, [down, beside], has_up)
-        for part in line_parts:
-            self.relay(part, z, 1 - x, [beside], None)
-
-    def plane_done(self, z, parts, present=None):
-        def wait():
-            for x in range(2):
-                for part in parts:
-                    self.arrived(part, z * 4 + x * 2 + 1 - self.c)
-
-        if present is None:
-            wait()
-        else:
-            pl.when(present)(wait)
-
-    def second_round(self, across_first, line_parts):
-        z, x = self.z, self.x
-        has_up, has_down = z < PLANES - 1, z > 0
-        up, down, beside = (self.UP, has_up), (self.DOWN, has_down), (self.BESIDE, None)
-        for part in across_first:
-            self.relay(part, z - 1, 1 - x, [up, beside], has_down)
-            self.relay(part, z + 1, 1 - x, [down, beside], has_up)
-        for part in line_parts:
-            self.relay(part, z - 1, 1 - x, [beside], has_down)
-            self.relay(part, z + 1, 1 - x, [beside], has_up)
-
-    def far_plane(self):
-        return (self.z + 2) % PLANES
-
-    def third_round(self, across_first, line_parts):
-        far, x = self.far_plane(), self.x
-        across, beside = (self.ACROSS, None), (self.BESIDE, None)
-        for part in line_parts:
-            self.relay(part, far, x, [across, beside], None)
-        for part in across_first:
-            self.relay(part, far, x, [beside], None)
-            self.relay(part, far, 1 - x, [beside], None)
-        for part in line_parts:
-            self.relay(part, far, 1 - x, [beside], None)
+
+    def left(self, sem, ref, count, first, rows):
+        sent = ref.at[pl.ds(0, count), pl.ds(first, rows)]
+        pltpu.make_async_remote_copy(
+            src_ref=sent,
+            dst_ref=sent,
+            send_sem=sem,
+            recv_sem=self.beside_sem.at[0, 0],
+            device_id=self.target(self.BESIDE),
+            device_id_type=MESH_ID,
+        ).wait_send()
+
+    def finish(self):
+        def settle(ways, hops, planes):
+            for part, (ref, first, rows) in enumerate(self.parts):
+                wide = 1 if part in self.line else 2
+                for way in ways:
+                    self.left(self.line_sem.at[part, way], ref, wide * hops, first, rows)
+                across = planes if part in self.line else 1
+                self.left(self.line_sem.at[part, self.ACROSS], ref, across, first, rows)
+            for i, ref in enumerate(self.buffers):
+                self.left(self.out_sem.at[i], ref, 2 * planes, 0, ref.shape[1])
+
+        pl.when(self.has_up & self.has_down)(lambda: settle((self.UP, self.DOWN), 2, 4))
+        pl.when(jnp.logical_not(self.has_down))(lambda: settle((self.UP,), 1, 3))
+        pl.when(jnp.logical_not(self.has_up))(lambda: settle((self.DOWN,), 1, 3))
+
+
+def gather_sems(parts, groups):
+    dma = pltpu.SemaphoreType.DMA
+    return [dma((parts, 2 * PLANES)), dma((groups, PLANES)), dma((parts, 3)), dma((groups,))]
 
 
 class VectorSum:
@@ -551,17 +564,17 @@
         self.ref, self.partial, self.arrived = ref, partial, arrived
         self.send_sem, self.recv_sem = send_sem, recv_sem
         self.y, self.z, self.x, self.c = where_am_i()
-        self.flying = []
 
     def device(self, y, z, x, c):
         return (y, z * 4 + x * 2 + c)
 
     def copy(self, source, slot, device):
+        stage = min(slot, 3)
         return pltpu.make_async_remote_copy(
             src_ref=source,
             dst_ref=self.arrived.at[slot],
-            send_sem=self.send_sem.at[slot],
-            recv_sem=self.recv_sem.at[slot],
+            send_sem=self.send_sem.at[stage],
+            recv_sem=self.recv_sem.at[stage],
             device_id=device,
             device_id_type=MESH_ID,
         )
@@ -575,28 +588,34 @@
                 self.device(1 - y, z, x, c),
                 self.device(y, z, 1 - x, c),
             )[stage]
-            copy = self.copy(source, stage, device)
-            copy.start()
-            self.flying.append(copy)
+            self.copy(source, stage, device).start()
         else:
             for step in range(1, PLANES):
-                copy = self.copy(
+                self.copy(
                     source, 2 + step, self.device(y, (z + step) % PLANES, x, c)
-                )
-                copy.start()
-                self.flying.append(copy)
+                ).start()
+
+    def counted(self, stage):
+        both = self.arrived.at[pl.ds(0, 1 if stage < 3 else 3)]
+        return pltpu.make_async_remote_copy(
+            src_ref=both,
+            dst_ref=both,
+            send_sem=self.send_sem.at[stage],
+            recv_sem=self.recv_sem.at[stage],
+            device_id=self.device(self.y, self.z, self.x, 1 - self.c),
+            device_id_type=MESH_ID,
+        )
 
     def take(self, stage):
-        y, z, x, c = self.y, self.z, self.x, self.c
         total = self.ref[...] if stage == 0 else self.partial[stage - 1]
+        self.counted(stage).wait_recv()
         for slot in (stage,) if stage < 3 else (3, 4, 5):
-            self.copy(self.ref, slot, self.device(y, z, x, 1 - c)).wait_recv()
             total = total + self.arrived[slot]
         self.partial[stage] = total
 
     def finish(self):
-        for copy in self.flying:
-            copy.wait_send()
+        for stage in range(4):
+            self.counted(stage).wait_send()
 
     def own_share(self, rows, share):
         width = self.ref.shape[1]
@@ -618,80 +637,34 @@
 
 
 STEP = 384
-
-
-class Shared:
-    def __init__(self, left, held, send_sem, recv_sem):
-        self.left, self.held = left, held
-        self.send_sem, self.recv_sem = send_sem, recv_sem
+UNROLL = 6
+
+
+class Quad:
+    def __init__(self, by_x):
+        self.by_x = by_x
         self.y, self.z, self.x, self.c = where_am_i()
-        self.quad = self.y * 2 + self.c
-        self.peer = (1 - self.y) * 2 + self.c
-        self.half = held.shape[2]
-        self.flying = []
-
-    def part(self, y):
-        return self.left.at[:, pl.ds(pl.multiple_of(y * self.half, 128), self.half)]
-
-    def fly(self, source, slot, which, device):
-        copy = pltpu.make_async_remote_copy(
-            src_ref=source,
-            dst_ref=self.held.at[slot],
-            send_sem=self.send_sem.at[which],
-            recv_sem=self.recv_sem.at[slot],
-            device_id=device,
-            device_id_type=MESH_ID,
-        )
-        copy.start()
-        self.flying.append(copy)
-
-    def beside(self):
-        return (self.y, self.z * 4 + self.x * 2 + 1 - self.c)
-
-    def share(self):
-        y, z, x, c = self.y, self.z, self.x, self.c
-        self.fly(self.part(1 - y), self.quad, 0, (1 - y, z * 4 + x * 2 + c))
-        self.fly(self.part(y), self.quad, 1, self.beside())
-        self.held[self.quad] = self.part(y)[...]
-
-    def landed(self, slot):
-        pltpu.make_async_remote_copy(
-            src_ref=self.held.at[slot],
-            dst_ref=self.held.at[slot],
-            send_sem=self.send_sem.at[0],
-            recv_sem=self.recv_sem.at[slot],
-            device_id=self.beside(),
-            device_id_type=MESH_ID,
-        ).wait_recv()
-
-    def relay(self):
-        self.landed(self.peer)
-        self.fly(self.held.at[self.peer], self.peer, 2, self.beside())
-
-    def complete(self):
-        self.landed(self.y * 2 + 1 - self.c)
-        self.landed((1 - self.y) * 2 + 1 - self.c)
-
-
-class Piece:
-    def __init__(self, shared, right, base, stride, out, buffers):
-        self.shared, self.right, self.base, self.stride, self.out = shared, right, base, stride, out
-        (
-            self.rights, self.whole, self.x_in, self.z_in, self.last,
-            self.send_sem, self.recv_sem, self.x_sem, self.z_send, self.z_recv, self.side_sem,
-        ) = buffers
-        self.y, self.z, self.x, self.c = where_am_i()
-        self.quad = self.y * 2 + self.c
-        self.flying = []
-
-    def device(self, y, z, x, c):
+        self.a, self.b = (self.x, self.y) if by_x else (self.y, self.x)
+        self.mine = self.a * 2 + self.c
+        self.peer = (1 - self.a) * 2 + self.c
+        self.beside = self.a * 2 + 1 - self.c
+        self.corner = (1 - self.a) * 2 + 1 - self.c
+
+    def device(self, a, b, z, c):
+        y, x = (b, a) if self.by_x else (a, b)
         return (y, z * 4 + x * 2 + c)
 
-    def columns(self, c):
-        return pl.ds(pl.multiple_of(self.base + c * self.stride, 128), STEP)
-
-    def fly(self, source, target, send_sem, recv_sem, device):
-        copy = pltpu.make_async_remote_copy(
+    def at_peer(self):
+        return self.device(1 - self.a, self.b, self.z, self.c)
+
+    def at_beside(self):
+        return self.device(self.a, self.b, self.z, 1 - self.c)
+
+    def at_corner(self):
+        return self.device(1 - self.a, self.b, self.z, 1 - self.c)
+
+    def link(self, source, target, send_sem, recv_sem, device):
+        return pltpu.make_async_remote_copy(
             src_ref=source,
             dst_ref=target,
             send_sem=send_sem,
@@ -699,110 +672,192 @@
             device_id=device,
             device_id_type=MESH_ID,
         )
-        copy.start()
-        self.flying.append(copy)
-
-    def landed(self, ref, sem):
-        pltpu.make_async_remote_copy(
-            src_ref=ref,
-            dst_ref=ref,
-            send_sem=self.send_sem.at[0],
-            recv_sem=sem,
-            device_id=self.device(self.y, self.z, self.x, 1 - self.c),
-            device_id_type=MESH_ID,
-        ).wait_recv()
+
+    def count(self, ref, send_sem, recv_sem):
+        return self.link(ref, ref, send_sem, recv_sem, self.at_beside())
+
+
+class Shared:
+    def __init__(self, left, by_x, buffers):
+        self.left = left
+        self.held, self.send_sem, self.recv_sem = buffers
+        self.quad = Quad(by_x)
+        self.width = self.held.shape[2]
+
+    def part(self, a):
+        if self.quad.by_x:
+            return self.left
+        return self.left.at[:, pl.ds(pl.multiple_of(a * self.width, 128), self.width)]
 
     def share(self):
-        y, z, x, c, quad = self.y, self.z, self.x, self.c, self.quad
-        mine, other = self.right.at[:, self.columns(c)], self.right.at[:, self.columns(1 - c)]
-        target, arrival = self.rights.at[quad], self.recv_sem.at[quad]
-        self.fly(mine, target, self.send_sem.at[0], arrival, self.device(1 - y, z, x, c))
-        self.fly(other, target, self.send_sem.at[1], arrival, self.device(1 - y, z, x, 1 - c))
-        self.fly(other, target, self.send_sem.at[2], arrival, self.device(y, z, x, 1 - c))
-        self.rights[quad] = mine[...]
+        q = self.quad
+        slot = self.held.at[q.mine]
+        send = self.send_sem.at[0]
+        q.link(self.part(1 - q.a), slot, send, self.recv_sem.at[0], q.at_peer()).start()
+        q.link(self.part(q.a), slot, send, self.recv_sem.at[1], q.at_beside()).start()
+        self.held[q.mine] = self.part(q.a)[...]
+
+    def relay(self):
+        q = self.quad
+        slot = self.held.at[q.peer]
+        q.count(slot, self.send_sem.at[0], self.recv_sem.at[0]).wait_recv()
+        q.link(slot, slot, self.send_sem.at[0], self.recv_sem.at[1], q.at_beside()).start()
+
+    def complete(self):
+        two = self.held.at[pl.ds(0, 2)]
+        self.quad.count(two, self.send_sem.at[0], self.recv_sem.at[1]).wait_recv()
+
+    def finish(self):
+        three = self.held.at[pl.ds(0, 3)]
+        self.quad.count(three, self.send_sem.at[0], self.recv_sem.at[1]).wait_send()
+
+
+class Piece:
+    def __init__(self, shared, right, base, stride, out, buffers):
+        self.shared, self.right, self.base, self.stride, self.out = shared, right, base, stride, out
+        self.rights, self.whole, self.b_in, self.z_in, self.last, self.send_sem, self.recv_sem = buffers
+        self.quad = shared.quad
+        self.share_rows = out.shape[0]
+
+    def columns(self, member):
+        place = member if self.quad.by_x else member % 2
+        return pl.ds(pl.multiple_of(self.base + place * self.stride, 128), STEP)
+
+    def give(self, member, device):
+        self.quad.link(
+            self.right.at[:, self.columns(member)], self.rights.at[self.quad.mine],
+            self.send_sem.at[0], self.recv_sem.at[0], device,
+        ).start()
+
+    def share(self):
+        q = self.quad
+        self.give(q.peer, q.at_peer())
+        self.give(q.corner, q.at_corner())
+        self.give(q.beside, q.at_beside())
+        self.rights[q.mine] = self.right[:, self.columns(q.mine)]
+
+    def share_early(self):
+        q = self.quad
+
+        @pl.when(q.c == 0)
+        def _():
+            self.give(q.peer, q.at_peer())
+
+        @pl.when(q.c == 1)
+        def _():
+            self.give(q.corner, q.at_corner())
+            self.give(q.beside, q.at_beside())
+
+    def share_late(self):
+        q = self.quad
+
+        @pl.when(q.c == 1)
+        def _():
+            self.give(q.peer, q.at_peer())
+
+        @pl.when(q.c == 0)
+        def _():
+            self.give(q.corner, q.at_corner())
+            self.give(q.beside, q.at_beside())
+
+        self.rights[q.mine] = self.right[:, self.columns(q.mine)]
+
+    def slab(self, b):
+        return self.whole.at[b] if self.quad.by_x else self.whole.at[:, b]
+
+    def cell(self, z):
+        b = self.quad.b
+        return self.whole.at[b, z] if self.quad.by_x else self.whole.at[z, b]
 
     def multiply(self):
-        y, c = self.y, self.c
-        for other in (y * 2 + 1 - c, (1 - y) * 2 + c, (1 - y) * 2 + 1 - c):
-            self.landed(self.rights.at[other], self.recv_sem.at[other])
+        q = self.quad
+        three = self.rights.at[pl.ds(0, 3)]
+        q.count(three, self.send_sem.at[0], self.recv_sem.at[0]).wait_recv()
         held = self.shared.held
         tokens = held.shape[0] * held.shape[1]
-        planes, _, rows, _ = self.whole.shape
         right = self.rights[...].reshape(tokens, STEP)
-        if self.shared.half > STEP:
+        if self.shared.width > STEP:
 
             def one(i, carry):
                 left = held[:, :, pl.ds(pl.multiple_of(i * STEP, 128), STEP)]
                 part = product(left.reshape(tokens, STEP), right, CONTRACT_FIRST)
-                self.whole[i] = part.astype(jnp.bfloat16).reshape(2, rows, STEP)
+                self.whole[i] = part.astype(jnp.bfloat16).reshape(self.whole.shape[1:])
                 return carry
 
-            lax.fori_loop(0, self.shared.half // STEP, one, 0)
+            lax.fori_loop(0, self.shared.width // STEP, one, 0)
         else:
             part = product(held[...].reshape(tokens, STEP), right, CONTRACT_FIRST)
-            self.whole[...] = part.astype(jnp.bfloat16).reshape(planes, 2, rows, STEP)
-        self.fly(
-            self.whole.at[:, 1 - self.x], self.x_in, self.x_sem.at[0], self.x_sem.at[1],
-            self.device(self.y, self.z, 1 - self.x, self.c),
+            self.whole[...] = part.astype(jnp.bfloat16).reshape(self.whole.shape)
+        q.link(
+            self.slab(1 - q.b), self.b_in, self.send_sem.at[1], self.recv_sem.at[1],
+            q.device(q.a, 1 - q.b, q.z, q.c),
+        ).start()
+
+    def spread(self):
+        q = self.quad
+        q.count(self.b_in, self.send_sem.at[1], self.recv_sem.at[1]).wait_recv()
+        slab = self.slab(q.b)
+        slab[...] = (slab[...].astype(jnp.float32) + self.b_in[...].astype(jnp.float32)).astype(
+            jnp.bfloat16
         )
-
-    def spread(self):
-        self.landed(self.x_in, self.x_sem.at[1])
-        self.whole[:, self.x] = (
-            self.whole[:, self.x].astype(jnp.float32) + self.x_in[...].astype(jnp.float32)
-        ).astype(jnp.bfloat16)
+        q.count(self.rights.at[pl.ds(0, 3)], self.send_sem.at[0], self.recv_sem.at[0]).wait_send()
         for step in range(1, PLANES):
-            target = (self.z + step) % PLANES
-            self.fly(
-                self.whole.at[target, self.x], self.z_in.at[self.z], self.z_send.at[step],
-                self.z_recv.at[self.z], self.device(self.y, target, self.x, self.c),
-            )
+            target = (q.z + step) % PLANES
+            q.link(
+                self.cell(target), self.z_in.at[q.z], self.send_sem.at[0], self.recv_sem.at[2],
+                q.device(q.a, q.b, target, q.c),
+            ).start()
+
+    def rows_of(self, member):
+        place = member if self.quad.by_x else member % 2
+        return self.last.at[pl.ds(pl.multiple_of(place * self.share_rows, 8), self.share_rows)]
 
     def collect(self):
-        total = self.whole[self.z, self.x].astype(jnp.float32)
+        q = self.quad
+        three = self.z_in.at[pl.ds(0, 3)]
+        q.count(three, self.send_sem.at[0], self.recv_sem.at[2]).wait_recv()
+        total = self.cell(q.z)[...].astype(jnp.float32)
         for step in range(1, PLANES):
-            source = (self.z + step) % PLANES
-            self.landed(self.z_in.at[source], self.z_recv.at[source])
-            total = total + self.z_in[source].astype(jnp.float32)
+            total = total + self.z_in[(q.z + step) % PLANES].astype(jnp.float32)
         self.last[...] = total
-        rows = self.last.shape[0] // 2
-        self.fly(
-            self.last.at[pl.ds(pl.multiple_of((1 - self.c) * rows, 8), rows)],
-            self.out.at[:, self.columns(self.c)],
-            self.side_sem.at[0], self.side_sem.at[1],
-            self.device(self.y, self.z, self.x, 1 - self.c),
-        )
-        self.out[:, self.columns(self.c)] = self.last[
-            pl.ds(pl.multiple_of(self.c * rows, 8), rows), :
-        ]
-
-    def delivered(self):
-        self.landed(self.out.at[:, self.columns(1 - self.c)], self.side_sem.at[1])
-
-
-def shared_scratch(frame_count, left_width):
+        q.count(self.b_in, self.send_sem.at[1], self.recv_sem.at[1]).wait_send()
+        columns = self.out.at[:, self.columns(q.mine)]
+        partners = [(q.beside, q.at_beside())]
+        if q.by_x:
+            partners = [(q.peer, q.at_peer()), (q.corner, q.at_corner())] + partners
+        for member, device in partners:
+            q.link(
+                self.rows_of(member), columns, self.send_sem.at[1], self.recv_sem.at[3], device
+            ).start()
+        columns[...] = self.rows_of(q.mine)[...]
+
+    def finish(self):
+        q = self.quad
+        others = self.last.at[pl.ds(0, (3 if q.by_x else 1) * self.share_rows)]
+        q.count(others, self.send_sem.at[1], self.recv_sem.at[3]).wait()
+        three = self.z_in.at[pl.ds(0, 3)]
+        q.count(three, self.send_sem.at[0], self.recv_sem.at[2]).wait_send()
+
+
+def shared_scratch(frame_count, left_width, by_x):
     return [
-        pltpu.VMEM((4, frame_count, left_width // 2), jnp.bfloat16),
-        pltpu.SemaphoreType.DMA((3,)),
-        pltpu.SemaphoreType.DMA((4,)),
+        pltpu.VMEM((4, frame_count, left_width if by_x else left_width // 2), jnp.bfloat16),
+        pltpu.SemaphoreType.DMA((1,)),
+        pltpu.SemaphoreType.DMA((2,)),
     ]
 
 
-def piece_scratch(frame_count, left_width):
-    rows = left_width // 2 // (2 * PLANES)
+def piece_scratch(frame_count, left_width, by_x):
+    rows = left_width // (2 * PLANES) if by_x else left_width // (4 * PLANES)
     low = jnp.bfloat16
     return [
         pltpu.VMEM((4, frame_count, STEP), low),
-        pltpu.VMEM((PLANES, 2, rows, STEP), low),
+        pltpu.VMEM((2, PLANES, rows, STEP) if by_x else (PLANES, 2, rows, STEP), low),
         pltpu.VMEM((PLANES, rows, STEP), low),
         pltpu.VMEM((PLANES, rows, STEP), low),
         pltpu.VMEM((rows, STEP), jnp.float32),
-        pltpu.SemaphoreType.DMA((3,)),
+        pltpu.SemaphoreType.DMA((2,)),
         pltpu.SemaphoreType.DMA((4,)),
-        pltpu.SemaphoreType.DMA((2,)),
-        pltpu.SemaphoreType.DMA((PLANES,)),
-        pltpu.SemaphoreType.DMA((PLANES,)),
-        pltpu.SemaphoreType.DMA((2,)),
     ]
 
 
@@ -816,12 +871,10 @@
         down_held=pltpu.VMEM((inner, width), low),
         weight_sem=dma((4,)),
         block=pltpu.VMEM((BLOCKS, frame_count + 16, width), low),
-        block_send=dma((2, 4, BLOCKS)),
-        block_recv=dma((2, BLOCKS)),
+        block_sems=gather_sems(2, 1),
         grad_block=pltpu.VMEM((BLOCKS, frame_count, width), low),
         stats=pltpu.VMEM((BLOCKS, 32, frame_count), wide),
-        grad_send=dma((3, 4, BLOCKS)),
-        grad_recv=dma((3, BLOCKS)),
+        grad_sems=gather_sems(3, 2),
         projected=pltpu.VMEM((BLOCKS, frame_count, 3 * width), low),
         mask=pltpu.VMEM((frame_count, BLOCKS * frame_count), wide),
         attended=pltpu.VMEM((frame_count, width), wide),
@@ -842,16 +895,16 @@
         vector=pltpu.VMEM((16, width), wide),
         vector_partial=pltpu.VMEM((4, 16, width), wide),
         vector_arrived=pltpu.VMEM((6, 16, width), wide),
-        vector_send=dma((6,)),
-        vector_recv=dma((6,)),
-        down_left=shared_scratch(frame_count, inner),
-        up_left=shared_scratch(frame_count, width),
-        out_left=shared_scratch(frame_count, width),
-        qkv_left=shared_scratch(frame_count, width),
-        down_piece=piece_scratch(frame_count, inner),
-        up_pieces=[piece_scratch(frame_count, width) for _ in range(4)],
-        out_piece=piece_scratch(frame_count, width),
-        qkv_pieces=[piece_scratch(frame_count, width) for _ in range(3)],
+        vector_send=dma((4,)),
+        vector_recv=dma((4,)),
+        down_left=shared_scratch(frame_count, inner, False),
+        up_left=shared_scratch(frame_count, width, True),
+        out_left=shared_scratch(frame_count, width, False),
+        qkv_left=shared_scratch(frame_count, width, False),
+        down_piece=piece_scratch(frame_count, inner, False),
+        up_pieces=[piece_scratch(frame_count, width, True) for _ in range(2)],
+        out_piece=piece_scratch(frame_count, width, False),
+        qkv_pieces=[piece_scratch(frame_count, width, False) for _ in range(3)],
     )
 
 
@@ -927,23 +980,34 @@
     for i in range(4):
         fetch(i).start()
 
+    line_rows = frame_count // 2
     link = RowGather(
-        [(k.block, 0, 64), (k.block, 64, frame_count - 48)], k.block_send, k.block_recv
+        [
+            (k.block, 0, line_rows),
+            (k.block, line_rows, k.block.shape[1] - line_rows),
+        ],
+        (0,),
+        (1,),
+        k.block_sems,
     )
     back = RowGather(
-        [(k.grad_block, 0, 64), (k.grad_block, 64, frame_count - 64), (k.stats, 0, 32)],
-        k.grad_send,
-        k.grad_recv,
-    )
-    down_left = Shared(k.act, *k.down_left)
-    up_left = Shared(k.hidden_low, *k.up_left)
-    out_left = Shared(k.context, *k.out_left)
-    qkv_left = Shared(k.frames, *k.qkv_left)
-    half_inner, half_width = inner // 2, width // 2
+        [
+            (k.grad_block, 0, line_rows),
+            (k.grad_block, line_rows, frame_count - line_rows),
+            (k.stats, 0, 32),
+        ],
+        (2, 0),
+        (1,),
+        k.grad_sems,
+    )
+    down_left = Shared(k.act, False, k.down_left)
+    up_left = Shared(k.hidden_low, True, k.up_left)
+    out_left = Shared(k.context, False, k.out_left)
+    qkv_left = Shared(k.frames, False, k.qkv_left)
+    half_width = width // 2
     down = Piece(down_left, k.second_low, 0, half_width, k.down_g, k.down_piece)
     ups = [
-        Piece(up_left, k.pre_low, p * STEP, half_inner, k.up_g, k.up_pieces[p])
-        for p in range(4)
+        Piece(up_left, k.pre_low, p * STEP, width, k.up_g, k.up_pieces[p]) for p in range(2)
     ]
     out = Piece(out_left, k.first_low, 0, half_width, k.out_g, k.out_piece)
     qkvs = [
@@ -954,20 +1018,16 @@
         k.vector, k.vector_partial, k.vector_arrived, k.vector_send, k.vector_recv
     )
 
-    partners = [
-        (None, down.device(row, z, x, 1 - c)),
-        (None, down.device(1 - row, z, x, c)),
-        (None, down.device(1 - row, z, x, 1 - c)),
-        (None, down.device(row, z, 1 - x, c)),
-    ]
-    partners += [(None, down.device(row, (z + step) % PLANES, x, c)) for step in range(1, PLANES)]
+    places = [(row, z, x, 1 - c), (1 - row, z, x, c), (1 - row, z, x, 1 - c)]
+    places += [(row, z, 1 - x, c), (row, z, 1 - x, 1 - c)]
+    places += [(row, (z + step) % PLANES, x, c) for step in range(1, PLANES)]
+    partners = [(None, (y, at * 4 + across * 2 + core)) for y, at, across, core in places]
     meet(partners, len(partners))
 
-    line, crossing = (0,), (1,)
     k.block[mine, pl.ds(0, frame_count), :] = k.frames[...]
     own_ids = jnp.broadcast_to(k.segment_ids[...], (frame_count, frame_count)).astype(wide)
     k.block[mine, pl.ds(frame_count, 16), pl.ds(0, frame_count)] = own_ids[:16].astype(low)
-    link.own(crossing, line)
+    link.own()
     qkv_left.share()
     ids_column = own_ids.T
     k.inner_bias[...] = k.up_bias[...].reshape(1, inner)
@@ -1010,69 +1070,85 @@
     def head_state(h):
         return pl.ds(pl.multiple_of(h * 128, 128), 128)
 
+    def both_heads(values):
+        nothing = jnp.zeros_like(values)
+        return jnp.concatenate(
+            [jnp.where(lane < HALF, values, nothing), jnp.where(lane < HALF, nothing, values)],
+            axis=0,
+        )
+
+    def own_halves(values):
+        return jnp.where(lane < HALF, values[:frame_count], values[frame_count:])
+
     def attend(plane, first):
         at = pl.multiple_of(plane * 4 * frame_count, 128)
 
+        def state(kind, j):
+            return k.slope.at[:, pl.ds(pl.multiple_of((kind * HEADS + 2 * j) * 128, 128), 256)]
+
+        def read(kind, j):
+            pair_state = state(kind, j)[...]
+            return jnp.concatenate([pair_state[:, :128], pair_state[:, 128:]], axis=0)
+
+        def write(kind, j, values):
+            state(kind, j)[...] = jnp.concatenate(
+                [values[:frame_count], values[frame_count:]], axis=1
+            )
+
         def pair(j, carry):
-            query = k.projected[mine, :, columns_of(0, j)]
+            query = both_heads(k.projected[mine, :, columns_of(0, j)])
             keys = k.projected[pl.ds(plane * 4, 4), :, columns_of(1, j)].reshape(-1, 128)
             values = k.projected[pl.ds(plane * 4, 4), :, columns_of(2, j)].reshape(-1, 128)
-            outs, factors = [], []
-            for h in range(2):
-                chosen = (lane < HALF) == (h == 0)
-                scores = product(
-                    jnp.where(chosen, query, jnp.zeros_like(query)), keys, CONTRACT_LAST
-                )
-                scores = scores + k.mask[:, pl.ds(at, 4 * frame_count)]
-                peak = jnp.broadcast_to(jnp.max(scores, axis=1, keepdims=True), lane.shape)
-                if not first:
-                    old = k.slope[:, head_state(2 * j + h)]
-                    peak = jnp.maximum(peak, old)
-                    factors.append(jnp.exp(old - peak))
-                weights = jnp.exp(scores - jnp.concatenate([peak] * 4, axis=1))
-                whole = jnp.broadcast_to(jnp.sum(weights, axis=1, keepdims=True), lane.shape)
-                if not first:
-                    whole = whole + k.slope[:, head_state(HEADS + 2 * j + h)] * factors[h]
-                k.slope[:, head_state(2 * j + h)] = peak
-                k.slope[:, head_state(HEADS + 2 * j + h)] = whole
-                outs.append(product(weights.astype(low), values, CONTRACT_INNER))
-            both = jnp.where(lane < HALF, outs[0], outs[1])
+            mask = k.mask[:, pl.ds(at, 4 * frame_count)]
+            scores = product(query, keys, CONTRACT_LAST) + jnp.concatenate([mask, mask], axis=0)
+            tile = (2 * frame_count, 128)
+            peak = jnp.broadcast_to(jnp.max(scores, axis=1, keepdims=True), tile)
             if not first:
-                both = both + k.attended[:, columns_of(0, j)] * jnp.where(
-                    lane < HALF, factors[0], factors[1]
-                )
+                old = read(0, j)
+                peak = jnp.maximum(peak, old)
+                factor = jnp.exp(old - peak)
+            weights = jnp.exp(scores - jnp.concatenate([peak] * 4, axis=1))
+            whole = jnp.broadcast_to(jnp.sum(weights, axis=1, keepdims=True), tile)
+            if not first:
+                whole = whole + read(1, j) * factor
+            write(0, j, peak)
+            write(1, j, whole)
+            both = own_halves(product(weights.astype(low), values, CONTRACT_INNER))
+            if not first:
+                both = both + k.attended[:, columns_of(0, j)] * own_halves(factor)
             k.attended[:, columns_of(0, j)] = both
             return carry
 
-        lax.fori_loop(0, PAIRS, pair, 0)
+        lax.fori_loop(0, PAIRS, pair, 0, unroll=UNROLL)
 
     fetch(0).wait()
     own_query = product(k.frames[...], k.qkv_held[:, pl.ds(0, width)], CONTRACT_INNER)
     k.projected[mine, :, pl.ds(0, width)] = as_query(own_query)
-    link.first_round(crossing, line)
-    link.plane_done(z, (0, 1))
+    link.near_first()
+    link.plane_done(z)
     project(z)
-    link.second_round(crossing, line)
+    link.near_second()
     attend(z, True)
+    link.far_line()
 
     @pl.when(has_down)
     def _():
-        link.plane_done(z - 1, (0, 1))
+        link.plane_done(z - 1)
         project(z - 1)
-
-    link.third_round(crossing, line)
-
-    @pl.when(has_down)
-    def _():
         attend(z - 1, False)
 
     @pl.when(has_up)
     def _():
-        link.plane_done(z + 1, (0, 1))
+        link.plane_done(z + 1)
         project(z + 1)
+
+    link.far_rest()
+
+    @pl.when(has_up)
+    def _():
         attend(z + 1, False)
 
-    link.plane_done(far, (0, 1))
+    link.plane_done(far)
     project(far)
     attend(far, False)
     logs = jnp.zeros(lane.shape, wide)
@@ -1151,9 +1227,9 @@
     note(6, upstream * normed_two)
     note(7, upstream)
     k.running[...] = second_grad
-    for p in range(4):
-        for side in range(2):
-            first = side * half_inner + p * STEP
+    for p in range(2):
+        for member in range(4):
+            first = member * width + p * STEP
             columns = pl.ds(first, STEP)
             pre_grad = (
                 product(k.second_low[...], k.down_held[columns, :], CONTRACT_LAST)
@@ -1167,10 +1243,8 @@
                 k.pre_low[:, columns], k.up_held[:, columns], CONTRACT_LAST
             )
         ups[p].share()
-        if p == 1:
-            out_left.relay()
+        if p == 0:
             up_left.relay()
-            qkv_left.relay()
     hidden_grad = k.running[...]
     normed_one = k.normed[...]
     first_grad = normalize_back(hidden_grad, normed_one, inverse_one, flat(k.norm1_gain))
@@ -1191,8 +1265,7 @@
     k.delta[...] = delta
     k.stats[mine, pl.ds(0, 16), :] = k.logs[...].T[:16]
     k.stats[mine, pl.ds(16, 16), :] = delta.T[:16]
-    back_line, back_crossing = (2, 0), (1,)
-    back.own(back_crossing, back_line)
+    back.own()
     note(2, first_grad)
     note(3, hidden_grad * normed_one)
     note(4, hidden_grad)
@@ -1265,20 +1338,24 @@
 
         lax.fori_loop(first, last, body, 0)
 
+    qkv_left.relay()
     pairs(query_pair, 0, 2)
-    back.first_round(back_crossing, back_line)
+    back.near_first()
+    up_left.complete()
+    pairs(query_pair, 2, 3)
+    ups[0].multiply()
+    back.near_second()
+    pairs(query_pair, 3, 5)
+    back.far_line()
     down_left.relay()
-    pairs(query_pair, 2, 4)
-    back.second_round(back_crossing, back_line)
-    pairs(query_pair, 4, 6)
-    back.third_round(back_crossing, back_line)
+    ups[1].multiply()
+    pairs(query_pair, 5, 6)
     qkvs[0].share()
+    back.far_rest()
+    project_queries(z)
+    project_queries(far)
     down_left.complete()
     down.multiply()
-    up_left.complete()
-    project_queries(z)
-    project_queries(far)
-    ups[0].multiply()
 
     @pl.when(has_down)
     def _():
@@ -1288,50 +1365,49 @@
     def _():
         project_queries(z + 1)
 
-    back.plane_done(z, (0, 1, 2))
-    back.plane_done(z - 1, (0, 1, 2), has_down)
-    back.plane_done(z + 1, (0, 1, 2), has_up)
-    back.plane_done(far, (0, 1, 2))
+    out_left.relay()
+    ups[0].spread()
+    back.plane_done(z)
+    back.plane_done(z - 1, has_down)
+    back.plane_done(z + 1, has_up)
+    back.plane_done(far)
     pairs(key_pair, 0, 2)
-    ups[1].multiply()
+    ups[1].spread()
+    out_left.complete()
+    out.multiply()
+    pairs(key_pair, 2, 3)
+    qkvs[1].share_early()
+    qkvs[2].share_early()
+    qkv_left.complete()
+    qkvs[0].multiply()
+    pairs(key_pair, 3, 4)
     down.spread()
-    pairs(key_pair, 2, 4)
-    ups[2].multiply()
-    ups[0].spread()
-    pairs(key_pair, 4, 6)
-    qkvs[1].share()
-    qkvs[2].share()
+    ups[0].collect()
+    pairs(key_pair, 4, 5)
+    out.spread()
+    ups[1].collect()
+    pairs(key_pair, 5, 6)
+    qkvs[1].share_late()
+    qkvs[2].share_late()
     note(0, k.proj_grad[:, pl.ds(0, width)].astype(wide))
     note(1, k.proj_grad[:, pl.ds(2 * width, width)].astype(wide))
     vector.start(0)
-    ups[3].multiply()
-    down.collect()
-    ups[1].spread()
+    qkvs[0].spread()
     k.input_grad[...] = k.first_grad[...] + product(
         k.proj_grad[...], k.qkv_held[...], CONTRACT_LAST
     )
     vector.take(0)
     vector.start(1)
-    out_left.complete()
-    out.multiply()
-    ups[2].spread()
-    qkv_left.complete()
-    qkvs[0].multiply()
-    ups[0].collect()
-    ups[3].spread()
+    down.collect()
+    out.collect()
+    qkvs[1].multiply()
     vector.take(1)
     vector.start(2)
-    qkvs[1].multiply()
-    ups[1].collect()
-    out.spread()
     qkvs[2].multiply()
-    ups[2].collect()
-    qkvs[0].spread()
+    qkvs[0].collect()
+    qkvs[1].spread()
     vector.take(2)
     vector.start(3)
-    ups[3].collect()
-    qkvs[1].spread()
-    out.collect()
     qkvs[2].spread()
     vector.take(3)
     summed = k.vector_partial[3]
@@ -1345,18 +1421,28 @@
     keep = lax.broadcasted_iota(jnp.int32, up_shares.shape, 0) == at
     picked = jnp.sum(jnp.where(keep, up_shares, 0.0), axis=0, keepdims=True)
     k.upbias_g[...] = picked[0, : 4 * share]
-    qkvs[0].collect()
     qkvs[1].collect()
     qkvs[2].collect()
-    pieces = [down] + ups + [out] + qkvs
-    for each in pieces:
-        each.delivered()
+    for each in [down_left, up_left, out_left, qkv_left, down, out] + ups + qkvs:
+        each.finish()
+    back.finish()
     link.finish()
-    back.finish()
-    for each in [down_left, up_left, out_left, qkv_left] + pieces:
-        for copy in each.flying:
-            copy.wait_send()
     vector.finish()
+
+
+def copy_kernel(*refs):
+    count = len(refs) // 2
+    for source, target in zip(refs[:count], refs[count:]):
+        target[...] = source[...]
+
+
+def hand_over(results):
+    return pl.pallas_call(
+        copy_kernel,
+        out_shape=tuple(jax.ShapeDtypeStruct(each.shape, each.dtype) for each in results),
+        in_specs=[IN_VMEM] * len(results),
+        out_specs=(IN_VMEM,) * len(results),
+    )(*results)
 
 
 def layer_step(*args):
@@ -1394,6 +1480,7 @@
             collective_id=0, has_side_effects=True, vmem_limit_bytes=VMEM_BYTES
         ),
     )(*operands)
+    results = hand_over(results)
     return (results[0][None], results[1][None]) + tuple(results[2:])
 
 

time: 152 us -> 117 us (0.77)
  local copies, waits for them, and re-layouts: 20.2 us -> 0 us
  Pallas kernels: 131 us -> 115 us
    unnamed x15 -> x0, local copies, waits for them, and re-layouts: 20.2 us -> none
    pallas_call x1, Pallas kernels: 131 us -> 113 us  [layer_step(): pl.pallas_call(functools.partial(layer_kernel, held), out_shape=tuple((ja...]
    pallas_call x0 -> x1, Pallas kernels: none -> 2.55 us  [hand_over(): pl.pallas_call(copy_kernel, out_shape=tuple((jax.ShapeDtypeStruct(each.sh...]
where the time goes in v3:
time: 117 us; the launch traced here: 116 us
  Pallas kernels  115 us (98%)
    pallas_call x1, Pallas kernels, layer_step(): pl.pallas_call(functools.partial(layer_kernel, held), out_shape=tuple((ja...  113 us
    pallas_call x1, Pallas kernels, hand_over(): pl.pallas_call(copy_kernel, out_shape=tuple((jax.ShapeDtypeStruct(each.sh...  2.55 us

profile of v3, /device:TPU:0, one launch (start us, length us, event | category | flops | bytes accessed | tf_op | source)
XLA Modules:
  0.0 116.3 jit_solution(16033428484054091730)
XLA Ops:
  0.7 112.9 %shard_map.271 = (bf16[128,768]{1,0:T(8,128)(2,1)}, f32[128,768]{1,0:T(8,128)}, f32[24,2304]{1,0:T(8,128)}, f32[24]{0:T(128)}, f32[24]{0:T(128)}, /*index=5*/f32...) custom-call(bf16[128,768]{1,0:T(8,128)(2,1)} %bitcast.4, ...), custom_call_target="tpu_custom_call" | custom-call | tf_op jit(solution)/shard_map/pallas_call | solution.py:1473
  113.6 2.5 %shard_map.272 = (bf16[128,768]{1,0:T(8,128)(2,1)}, f32[128,768]{1,0:T(8,128)}, f32[24,2304]{1,0:T(8,128)}, f32[24]{0:T(128)}, f32[24]{0:T(128)}, /*index=5*/f32...) custom-call(bf16[128,768]{1,0:T(8,128)(2,1)} %get-tuple-element.45.r, ...), custom_call_target="tpu_custom_call" | custom-call | tf_op jit(solution)/shard_map/pallas_call | solution.py:1440
